TPU v7x, 32 devices: a whole 2x2x4 slice. The times are simulated.
32 devices in a mesh: fsdp: 2 (over x), heads: 4 (over y, core), tensor: 4 (over z).
Axes of the slice: x: 2, y: 2, z: 4, core: 2. Of those that a mesh axis runs over, the one named last changes fastest.
Arguments:
- block_input: bfloat16 [4096, 2048], P(('fsdp', 'tensor')), may hold values from -6 to 6
- cotangent: bfloat16 [4096, 2048], P(('fsdp', 'tensor')), may hold values from -6 to 6
- norm1_gain: float32 [2048], replicated, may hold values from 0.25 to 1.75
- latent_gain: float32 [512], replicated, may hold values from 0.25 to 1.75
- norm2_gain: float32 [2048], replicated, may hold values from 0.25 to 1.75
- w_query: bfloat16 [2048, 3072], P(('fsdp', 'tensor'), 'heads'), may hold values from -0.125 to 0.125
- w_latent: bfloat16 [2048, 576], P(('fsdp', 'tensor')), may hold values from -0.125 to 0.125
- w_kv: bfloat16 [512, 4096], P(('fsdp', 'tensor'), 'heads'), may hold values from -0.25 to 0.25
- w_out: bfloat16 [2048, 2048], P('heads', ('fsdp', 'tensor')), may hold values from -0.5 to 0.5
- expert_gate: bfloat16 [16, 2048, 1408], P(('fsdp', 'heads'), None, 'tensor'), may hold values from -0.125 to 0.125
- expert_up: bfloat16 [16, 2048, 1408], P(('fsdp', 'heads'), None, 'tensor'), may hold values from -0.125 to 0.125
- expert_down: bfloat16 [16, 1408, 2048], P(('fsdp', 'heads'), 'tensor'), may hold values from -0.15625 to 0.15625
- shared_gate: bfloat16 [2048, 2816], P(('fsdp', 'heads'), 'tensor'), may hold values from -0.125 to 0.125
- shared_up: bfloat16 [2048, 2816], P(('fsdp', 'heads'), 'tensor'), may hold values from -0.125 to 0.125
- shared_down: bfloat16 [2816, 2048], P('tensor', ('fsdp', 'heads')), may hold values from -0.109375 to 0.109375
- routed_expert_index: int32 [4096, 6], P(('fsdp', 'tensor')), may hold values from 0 to 15, as said below
- slots: int32 [4096, 6], P(('fsdp', 'tensor')), may hold values from 0 to 240, as said below
- gate_weights: bfloat16 [4096, 6], P(('fsdp', 'tensor')), may hold values from 0.049804688 to 0.5
Outputs:
- output: bfloat16 [4096, 2048], P(('fsdp', 'tensor'))
- input_grad: float32 [4096, 2048], P(('fsdp', 'tensor'))
- norm1_gain_grad: float32 [2048], P(('fsdp', 'tensor'))
- latent_gain_grad: float32 [512], P(('fsdp', 'tensor'))
- norm2_gain_grad: float32 [2048], P(('fsdp', 'tensor'))
- w_query_grad: float32 [2048, 3072], P(('fsdp', 'tensor'), 'heads')
- w_latent_grad: float32 [2048, 576], P(('fsdp', 'tensor'))
- w_kv_grad: float32 [512, 4096], P(('fsdp', 'tensor'), 'heads')
- w_out_grad: float32 [2048, 2048], P('heads', ('fsdp', 'tensor'))
- expert_gate_grad: float32 [16, 2048, 1408], P(('fsdp', 'heads'), None, 'tensor')
- expert_up_grad: float32 [16, 2048, 1408], P(('fsdp', 'heads'), None, 'tensor')
- expert_down_grad: float32 [16, 1408, 2048], P(('fsdp', 'heads'), 'tensor')
- shared_gate_grad: float32 [2048, 2816], P(('fsdp', 'heads'), 'tensor')
- shared_up_grad: float32 [2048, 2816], P(('fsdp', 'heads'), 'tensor')
- shared_down_grad: float32 [2816, 2048], P('tensor', ('fsdp', 'heads'))
Inputs may be any that keep to these rules, and one draw needn't show every extreme that they name: `routed_expert_index`: each row names 6 different experts. In every routing block (f, h), the rows f * 2048 + t * 512 + h * 128 + i, one expert is named by every row. `slots`: A route's slot is the number of earlier routes of its routing block to the same expert, in the order of place t * 128 + i and then of the route's position, with 240 for every route beyond the first 240; 240 marks a dropped route, so each used (expert, slot) pair of a block appears once.
All inputs are finite; a program needn't handle non-finite values.
Results may differ from a plain program's by a relative error of at most 0.024.
Values may be sent and summed in bfloat16 or wider, within the bound.
No kernel may reach another device: no remote copies, remote signals or barrier semaphores. Data moves between devices by JAX's collectives and lax.ppermute only.
A program may use at most 384 MiB of HBM per device.

v0:
```python
import jax
import jax.numpy as jnp
from jax import lax
from jax.sharding import PartitionSpec as P
from jax.experimental import pallas as pl
from jax.experimental.pallas import tpu as pltpu

FSDP = "fsdp"
HEADS = "heads"
TENSOR = "tensor"
SCORE = "qhd,khd->hqk"
MIX = "hqk,khd->qhd"
BACK = "hqk,qhd->khd"

D = 2048
NOPE = 128
ROPE = 64
VDIM = 128
KVR = 512
TOP = 6
EXP_LOC = 2
LEN = 512
SEQ_DEV = 1


epsilon = 1e-06
theta_base = 10000.0


def rms_parts(vector):
    inverse = lax.rsqrt(jnp.mean(vector * vector, axis=-1, keepdims=True) + epsilon)
    return (vector * inverse, inverse)


def rms_back(grad_norm, normed, inverse, gain_vec):
    scaled = grad_norm * gain_vec
    inner_mean = jnp.mean(scaled * normed, axis=-1, keepdims=True)
    return inverse * (scaled - normed * inner_mean)


def rope_tables(row_count):
    half_width = ROPE // 2
    position = (jnp.arange(row_count) % LEN).astype(jnp.float32)
    exponent = jnp.arange(half_width).astype(jnp.float32) * (2.0 / ROPE)
    frequency = theta_base ** (-exponent)
    angles = position[:, None] * frequency[None, :]
    return (jnp.cos(angles), jnp.sin(angles))


def rotate(vector, cosine, sine_table):
    half_width = vector.shape[-1] // 2
    first_half = vector[..., :half_width]
    second_half = vector[..., half_width:]
    return jnp.concatenate(
        [
            first_half * cosine - second_half * sine_table,
            second_half * cosine + first_half * sine_table,
        ],
        axis=-1,
    )


def unrotate(vector, cosine, sine_table):
    half_width = vector.shape[-1] // 2
    first_half = vector[..., :half_width]
    second_half = vector[..., half_width:]
    return jnp.concatenate(
        [
            first_half * cosine + second_half * sine_table,
            second_half * cosine - first_half * sine_table,
        ],
        axis=-1,
    )


def combine(returned, positions, weighting, block_rows):
    width = returned.shape[-1]
    padded = jnp.concatenate(
        [returned.reshape(-1, width), jnp.zeros((1, width), jnp.float32)], axis=0
    )
    summed = jnp.zeros((block_rows, width), jnp.float32)
    for route_index in range(TOP):
        picked = padded[positions[:, route_index]]
        if weighting is None:
            summed = summed + picked
        else:
            summed = summed + picked * weighting[:, route_index : route_index + 1]
    return summed


def dispatch(outgoing):
    return lax.all_to_all(outgoing, (FSDP, HEADS), split_axis=0, concat_axis=0, tiled=True)


def bring_back(host_term, local_term, positions, weighting):
    block_rows = local_term.shape[0]
    arrived_rows = lax.all_to_all(
        host_term.astype(jnp.bfloat16), (FSDP, HEADS), split_axis=0, concat_axis=0, tiled=True
    ).astype(host_term.dtype)
    merged = combine(arrived_rows, positions, weighting, block_rows) + local_term
    own_rows = lax.psum_scatter(
        merged.astype(jnp.bfloat16), TENSOR, scatter_dimension=0, tiled=True
    ).astype(jnp.float32)
    return (
        own_rows,
        lax.all_gather(own_rows.astype(jnp.bfloat16), HEADS, axis=0, tiled=True).astype(
            own_rows.dtype
        ),
    )


def shards(
    block_input,
    cotangent,
    norm1_gain,
    latent_gain,
    norm2_gain,
    w_query,
    w_latent,
    w_kv,
    w_out,
    expert_gate,
    expert_up,
    expert_down,
    shared_gate,
    shared_up,
    shared_down,
    routed_expert_index,
    slots,
    gate_weights,
):
    row_count = block_input.shape[0]
    head_dim = NOPE + ROPE
    local_heads = w_query.shape[1] // head_dim
    score_scale = head_dim ** (-0.5)
    query_full, latent_full, kv_full, out_full = (
        lax.all_gather(w_query, (FSDP, TENSOR), axis=0, tiled=True),
        lax.all_gather(w_latent, (FSDP, TENSOR), axis=0, tiled=True),
        lax.all_gather(w_kv, (FSDP, TENSOR), axis=0, tiled=True),
        lax.all_gather(w_out, (FSDP, TENSOR), axis=1, tiled=True),
    )
    shared_gate_full, shared_up_full, shared_down_full = (
        lax.all_gather(shared_gate, (FSDP, HEADS), axis=0, tiled=True),
        lax.all_gather(shared_up, (FSDP, HEADS), axis=0, tiled=True),
        lax.all_gather(shared_down, (FSDP, HEADS), axis=1, tiled=True),
    )
    residual = block_input.astype(jnp.float32)
    first_normed, first_inverse = rms_parts(residual)
    first_input = (first_normed * norm1_gain).astype(jnp.bfloat16)
    cosine, sine_table = rope_tables(row_count)
    query_raw = jnp.dot(first_input, query_full, preferred_element_type=jnp.float32).reshape(
        row_count, local_heads, head_dim
    )
    queries = jnp.concatenate(
        [
            query_raw[..., :NOPE],
            rotate(query_raw[..., NOPE:], cosine[:, None, :], sine_table[:, None, :]),
        ],
        axis=-1,
    ).astype(jnp.bfloat16)
    latent_raw = jnp.dot(first_input, latent_full, preferred_element_type=jnp.float32)
    latent_normed, latent_inverse = rms_parts(latent_raw[:, :KVR])
    latent_norm = (latent_normed * latent_gain).astype(jnp.bfloat16)
    key_rope = rotate(latent_raw[:, KVR:], cosine, sine_table).astype(jnp.bfloat16)
    key_value = (
        jnp.dot(latent_norm, kv_full, preferred_element_type=jnp.float32)
        .astype(jnp.bfloat16)
        .reshape(row_count, local_heads, NOPE + VDIM)
    )
    key_all = jnp.concatenate(
        [
            key_value[..., :NOPE],
            jnp.broadcast_to(key_rope[:, None, :], (row_count, local_heads, ROPE)),
        ],
        axis=-1,
    )
    values = key_value[..., NOPE:]
    causal = jnp.arange(LEN)[:, None] >= jnp.arange(LEN)[None, :]

    def score_block(queries_s, keys_s):
        scores = (
            jnp.einsum(SCORE, queries_s, keys_s, preferred_element_type=jnp.float32)
            * score_scale
        )
        return jnp.where(causal[None], scores, -1e30)

    def attend(pieces):
        queries_s, keys_s, values_s = pieces
        scores = score_block(queries_s, keys_s)
        highest_score = jnp.max(scores, axis=-1, keepdims=True)
        log_total = highest_score + jnp.log(
            jnp.sum(jnp.exp(scores - highest_score), axis=-1, keepdims=True)
        )
        probabilities = jnp.exp(scores - log_total).astype(jnp.bfloat16)
        context_s = jnp.einsum(
            MIX, probabilities, values_s, preferred_element_type=jnp.float32
        )
        return (context_s.astype(jnp.bfloat16), log_total)

    seq_queries = queries.reshape(SEQ_DEV, LEN, local_heads, head_dim)
    seq_keys = key_all.reshape(SEQ_DEV, LEN, local_heads, head_dim)
    seq_values = values.reshape(SEQ_DEV, LEN, local_heads, VDIM)
    context, log_totals = lax.map(attend, (seq_queries, seq_keys, seq_values))
    context_flat = context.reshape(row_count, local_heads * VDIM)
    attention_part = jnp.dot(context_flat, out_full, preferred_element_type=jnp.float32)
    after_attention = residual + lax.psum(attention_part.astype(jnp.bfloat16), HEADS).astype(
        jnp.float32
    )
    second_normed, second_inverse = rms_parts(after_attention)
    second_input = (second_normed * norm2_gain).astype(jnp.bfloat16)
    quarter = row_count // lax.axis_size(HEADS)
    row_start = lax.axis_index(HEADS) * quarter

    def own_part(array):
        return lax.dynamic_slice_in_dim(array, row_start, quarter, 0)

    tokens_in, grads_in, ids_in, slots_in, gates_in = (
        lax.all_gather(own_part(second_input), TENSOR, axis=0, tiled=True),
        lax.all_gather(own_part(cotangent), TENSOR, axis=0, tiled=True),
        lax.all_gather(own_part(routed_expert_index), TENSOR, axis=0, tiled=True),
        lax.all_gather(own_part(slots), TENSOR, axis=0, tiled=True),
        lax.all_gather(own_part(gate_weights), TENSOR, axis=0, tiled=True),
    )
    hosts = lax.axis_size(FSDP) * lax.axis_size(HEADS)
    experts = EXP_LOC * hosts
    block_rows = tokens_in.shape[0]
    capacity = block_rows * TOP * 5 // (4 * experts)
    positions = jnp.where(slots_in < capacity, ids_in * capacity + slots_in, experts * capacity)
    flat_positions = positions.reshape(-1)
    row_labels = jnp.repeat(jnp.arange(block_rows, dtype=jnp.int32), TOP)
    owners = (
        jnp.full((experts * capacity + 1,), block_rows, jnp.int32)
        .at[flat_positions]
        .set(row_labels)[: experts * capacity]
    )
    routing_gate_weights = gates_in.astype(jnp.float32)
    slot_gates = (
        jnp.zeros((experts * capacity + 1,), jnp.float32)
        .at[flat_positions]
        .set(routing_gate_weights.reshape(-1))[: experts * capacity]
    )
    buffer_shape = (hosts, EXP_LOC, capacity, D)
    tokens_padded = jnp.concatenate([tokens_in, jnp.zeros((1, D), jnp.bfloat16)], axis=0)
    arrived = dispatch(tokens_padded[owners].reshape(buffer_shape))
    gate_act = jnp.einsum(
        "secd,edf->secf", arrived, expert_gate, preferred_element_type=jnp.float32
    )
    up_act = jnp.einsum("secd,edf->secf", arrived, expert_up, preferred_element_type=jnp.float32)
    gate_sigmoid = jax.nn.sigmoid(gate_act)
    gate_silu = gate_act * gate_sigmoid
    expert_hidden = (gate_silu * up_act).astype(jnp.bfloat16)
    expert_out = jnp.einsum(
        "secf,efd->secd", expert_hidden, expert_down, preferred_element_type=jnp.float32
    )
    shared_act = jnp.dot(tokens_in, shared_gate_full, preferred_element_type=jnp.float32)
    shared_lin = jnp.dot(tokens_in, shared_up_full, preferred_element_type=jnp.float32)
    shared_sigmoid = jax.nn.sigmoid(shared_act)
    shared_silu = shared_act * shared_sigmoid
    shared_hidden = (shared_silu * shared_lin).astype(jnp.bfloat16)
    shared_out = jnp.dot(shared_hidden, shared_down_full, preferred_element_type=jnp.float32)
    _, ffn_full = bring_back(expert_out, shared_out, positions, routing_gate_weights)
    output = (after_attention + ffn_full).astype(jnp.bfloat16)
    grads_padded = jnp.concatenate([grads_in, jnp.zeros((1, D), jnp.bfloat16)], axis=0)
    grad_slots = (
        (grads_padded[owners].astype(jnp.float32) * slot_gates[:, None])
        .astype(jnp.bfloat16)
        .reshape(buffer_shape)
    )
    grad_arrived = dispatch(grad_slots)
    grad_hidden = jnp.einsum(
        "secd,efd->secf", grad_arrived, expert_down, preferred_element_type=jnp.float32
    )
    grad_gate = (
        grad_hidden * up_act * gate_sigmoid * (1.0 + gate_act * (1.0 - gate_sigmoid))
    ).astype(jnp.bfloat16)
    grad_up = (grad_hidden * gate_silu).astype(jnp.bfloat16)
    expert_down_grad = jnp.einsum(
        "secf,secd->efd", expert_hidden, grad_arrived, preferred_element_type=jnp.float32
    )
    expert_gate_grad = jnp.einsum(
        "secd,secf->edf", arrived, grad_gate, preferred_element_type=jnp.float32
    )
    expert_up_grad = jnp.einsum(
        "secd,secf->edf", arrived, grad_up, preferred_element_type=jnp.float32
    )
    host_back = jnp.einsum(
        "secf,edf->secd", grad_gate, expert_gate, preferred_element_type=jnp.float32
    ) + jnp.einsum("secf,edf->secd", grad_up, expert_up, preferred_element_type=jnp.float32)
    grad_shared_hidden = jnp.dot(grads_in, shared_down_full.T, preferred_element_type=jnp.float32)
    shared_gate_back = (
        grad_shared_hidden
        * shared_lin
        * shared_sigmoid
        * (1.0 + shared_act * (1.0 - shared_sigmoid))
    ).astype(jnp.bfloat16)
    shared_up_back = (grad_shared_hidden * shared_silu).astype(jnp.bfloat16)
    shared_down_part = jnp.dot(shared_hidden.T, grads_in, preferred_element_type=jnp.float32)
    shared_gate_part = jnp.dot(tokens_in.T, shared_gate_back, preferred_element_type=jnp.float32)
    shared_up_part = jnp.dot(tokens_in.T, shared_up_back, preferred_element_type=jnp.float32)
    shared_gate_grad, shared_up_grad, shared_down_grad = (
        lax.psum_scatter(
            shared_gate_part.astype(jnp.bfloat16),
            (FSDP, HEADS),
            scatter_dimension=0,
            tiled=True,
        ).astype(jnp.float32),
        lax.psum_scatter(
            shared_up_part.astype(jnp.bfloat16), (FSDP, HEADS), scatter_dimension=0, tiled=True
        ).astype(jnp.float32),
        lax.psum_scatter(
            shared_down_part.astype(jnp.bfloat16),
            (FSDP, HEADS),
            scatter_dimension=1,
            tiled=True,
        ).astype(jnp.float32),
    )
    shared_back = jnp.dot(
        shared_gate_back, shared_gate_full.T, preferred_element_type=jnp.float32
    ) + jnp.dot(shared_up_back, shared_up_full.T, preferred_element_type=jnp.float32)
    _, grad_second = bring_back(host_back, shared_back, positions, None)
    second_gain_part = jnp.sum(grad_second * second_normed, axis=0)
    grad_after = cotangent.astype(jnp.float32) + rms_back(
        grad_second, second_normed, second_inverse, norm2_gain
    )
    grad_attention = grad_after.astype(jnp.bfloat16)
    out_part = jnp.dot(context_flat.T, grad_attention, preferred_element_type=jnp.float32)
    grad_context = (
        jnp.dot(grad_attention, out_full.T, preferred_element_type=jnp.float32)
        .astype(jnp.bfloat16)
        .reshape(SEQ_DEV, LEN, local_heads, VDIM)
    )

    def attend_back(pieces):
        queries_s, keys_s, values_s, log_total, grad_context_s = pieces
        scores = score_block(queries_s, keys_s)
        probabilities = jnp.exp(scores - log_total)
        grad_probs = jnp.einsum(
            SCORE, grad_context_s, values_s, preferred_element_type=jnp.float32
        )
        centred = jnp.sum(probabilities * grad_probs, axis=-1, keepdims=True)
        grad_scores = (probabilities * (grad_probs - centred)).astype(jnp.bfloat16)
        grad_queries_s = (
            jnp.einsum(MIX, grad_scores, keys_s, preferred_element_type=jnp.float32)
            * score_scale
        )
        grad_keys_s = (
            jnp.einsum(BACK, grad_scores, queries_s, preferred_element_type=jnp.float32)
            * score_scale
        )
        grad_values_s = jnp.einsum(
            BACK,
            probabilities.astype(jnp.bfloat16),
            grad_context_s,
            preferred_element_type=jnp.float32,
        )
        return (grad_queries_s, grad_keys_s, grad_values_s)

    grad_queries, grad_keys, grad_values = lax.map(
        attend_back, (seq_queries, seq_keys, seq_values, log_totals, grad_context)
    )
    grad_queries = grad_queries.reshape(row_count, local_heads, head_dim)
    grad_keys = grad_keys.reshape(row_count, local_heads, head_dim)
    grad_values = grad_values.reshape(row_count, local_heads, VDIM)
    grad_query_raw = (
        jnp.concatenate(
            [
                grad_queries[..., :NOPE],
                unrotate(grad_queries[..., NOPE:], cosine[:, None, :], sine_table[:, None, :]),
            ],
            axis=-1,
        )
        .astype(jnp.bfloat16)
        .reshape(row_count, local_heads * head_dim)
    )
    query_part = jnp.dot(first_input.T, grad_query_raw, preferred_element_type=jnp.float32)
    first_from_query = jnp.dot(grad_query_raw, query_full.T, preferred_element_type=jnp.float32)
    grad_key_value = (
        jnp.concatenate([grad_keys[..., :NOPE], grad_values], axis=-1)
        .astype(jnp.bfloat16)
        .reshape(row_count, local_heads * (NOPE + VDIM))
    )
    kv_part = jnp.dot(latent_norm.T, grad_key_value, preferred_element_type=jnp.float32)
    grad_latent_norm = jnp.dot(grad_key_value, kv_full.T, preferred_element_type=jnp.float32)
    latent_gain_part = jnp.sum(grad_latent_norm * latent_normed, axis=0)
    grad_compressed = rms_back(grad_latent_norm, latent_normed, latent_inverse, latent_gain)
    grad_key_rope = unrotate(jnp.sum(grad_keys[..., NOPE:], axis=1), cosine, sine_table)
    latent_term = jnp.concatenate([grad_compressed, grad_key_rope], axis=-1)
    first_summed, latent_summed, latent_gain_summed = (
        lax.psum(first_from_query.astype(jnp.bfloat16), HEADS).astype(jnp.float32),
        lax.psum(latent_term.astype(jnp.bfloat16), HEADS).astype(jnp.float32),
        lax.psum(latent_gain_part.astype(jnp.bfloat16), HEADS).astype(jnp.float32),
    )
    grad_latent = latent_summed.astype(jnp.bfloat16)
    latent_part = jnp.dot(first_input.T, grad_latent, preferred_element_type=jnp.float32)
    grad_first = first_summed + jnp.dot(
        grad_latent, latent_full.T, preferred_element_type=jnp.float32
    )
    first_gain_part = jnp.sum(grad_first * first_normed, axis=0)
    input_grad = grad_after + rms_back(grad_first, first_normed, first_inverse, norm1_gain)
    (
        w_query_grad,
        w_latent_grad,
        w_kv_grad,
        w_out_grad,
        norm1_gain_grad,
        latent_gain_grad,
        norm2_gain_grad,
    ) = (
        lax.psum_scatter(
            query_part.astype(jnp.bfloat16), (FSDP, TENSOR), scatter_dimension=0, tiled=True
        ).astype(jnp.float32),
        lax.psum_scatter(
            latent_part.astype(jnp.bfloat16), (FSDP, TENSOR), scatter_dimension=0, tiled=True
        ).astype(jnp.float32),
        lax.psum_scatter(
            kv_part.astype(jnp.bfloat16), (FSDP, TENSOR), scatter_dimension=0, tiled=True
        ).astype(jnp.float32),
        lax.psum_scatter(
            out_part.astype(jnp.bfloat16), (FSDP, TENSOR), scatter_dimension=1, tiled=True
        ).astype(jnp.float32),
        lax.psum_scatter(
            first_gain_part.astype(jnp.bfloat16),
            (FSDP, TENSOR),
            scatter_dimension=0,
            tiled=True,
        ).astype(jnp.float32),
        lax.psum_scatter(
            latent_gain_summed.astype(jnp.bfloat16),
            (FSDP, TENSOR),
            scatter_dimension=0,
            tiled=True,
        ).astype(jnp.float32),
        lax.psum_scatter(
            second_gain_part.astype(jnp.bfloat16),
            (FSDP, TENSOR),
            scatter_dimension=0,
            tiled=True,
        ).astype(jnp.float32),
    )
    return (
        output,
        input_grad,
        norm1_gain_grad,
        latent_gain_grad,
        norm2_gain_grad,
        w_query_grad,
        w_latent_grad,
        w_kv_grad,
        w_out_grad,
        expert_gate_grad,
        expert_up_grad,
        expert_down_grad,
        shared_gate_grad,
        shared_up_grad,
        shared_down_grad,
    )


PLANE = (FSDP, HEADS)
GROUPS = ((0,), (1, 3), (2,))
LANES = 128
TILE = 512
UNIT = 128
bf16 = jnp.bfloat16
f32 = jnp.float32


def after(array, *others):
    return lax.optimization_barrier((array, *others))[0]


def from_tensor(array, k):
    return lax.ppermute(array, TENSOR, [((i + k) % 4, i) for i in range(4)])


def to_tensor(array, k):
    return lax.ppermute(array, TENSOR, [(i, (i + k) % 4) for i in range(4)])


def swap_fsdp(array):
    return lax.ppermute(array, FSDP, [(0, 1), (1, 0)])


def swap_heads(array, mask):
    return lax.ppermute(array, HEADS, [(i, i ^ mask) for i in range(4)])


def swap_plane(array, first):
    pairs = []
    for f in range(2):
        for h in range(4):
            f_to, h_to = (f ^ 1, h) if h % 2 == first else (f, h ^ 2)
            pairs.append((f * 4 + h, f_to * 4 + h_to))
    return lax.ppermute(array, PLANE, pairs)


def gather_rows(unit):
    along = {0: unit}
    for k in (1, 3, 2):
        along[k] = from_tensor(unit, k)
    groups = []
    for group in GROUPS:
        here = jnp.concatenate([along[k] for k in group], axis=0) if len(group) > 1 else along[group[0]]
        first = swap_plane(here, 0)
        second = swap_plane(here, 1)
        mine = [here, first, second, swap_plane(first, 1)]
        groups.append(mine + [swap_heads(p, 1) for p in mine])
    return groups


def scatter_rows(groups):
    total = None
    for group, (mine, other) in zip(GROUPS, groups):
        other = swap_heads(other, 1)
        half = mine.shape[0] // 2
        sent = (mine[half:].astype(f32) + other[half:].astype(f32)).astype(bf16)
        sent = swap_plane(sent, 1)
        part = half // 2
        near = [a[:part].astype(f32) for a in (mine, other, sent)]
        far = [a[part:half].astype(f32) for a in (mine, other)] + [sent[part:].astype(f32)]
        far = swap_plane((far[0] + far[1] + far[2]).astype(bf16), 0)
        summed = near[0] + near[1] + near[2] + far.astype(f32)
        for k, piece in zip(group, jnp.split(summed, len(group), axis=0)):
            if k:
                piece = to_tensor(piece.astype(bf16), k).astype(f32)
            total = piece if total is None else total + piece
    return total


def gather_weight(shard):
    along = {0: shard}
    for k in (1, 3, 2):
        along[k] = from_tensor(shard, k)
    along = [along[k] for k in range(4)]
    return along, [swap_fsdp(p) for p in along]


def scatter_weight(parts):
    parts = [p.astype(bf16) for p in parts]
    summed = {}
    for k in (1, 3, 2, 0):
        far = swap_fsdp(parts[4 + k])
        summed[k] = parts[k].astype(f32) + far.astype(f32)
    total = summed[0]
    for k in (1, 3, 2):
        total = total + to_tensor(summed[k].astype(bf16), k).astype(f32)
    return total


def pick(array, index, count, axis):
    size = array.shape[axis] // count
    return lax.dynamic_slice_in_dim(array, index * size, size, axis)


def nn(left, right):
    return jnp.dot(left, right, preferred_element_type=f32)


def nt(left, right):
    return lax.dot_general(left, right, (((1,), (1,)), ((), ())), preferred_element_type=f32)


def tn(left, right):
    return lax.dot_general(left, right, (((0,), (0,)), ((), ())), preferred_element_type=f32)


def spans(counts, size):
    steps, place = [[]], 0
    for index, count in enumerate(counts):
        row = 0
        while row < count:
            if place == size:
                steps.append([])
                place = 0
            taken = min(count - row, size - place)
            steps[-1].append((index, row, taken, place))
            row += taken
            place += taken
    return steps


def hidden_kernel(first_ref, *refs):
    pieces = 8
    x_refs, g_refs = refs[:pieces], refs[pieces : 2 * pieces]
    gate_ref, up_ref, shared_ref, down_ref = refs[2 * pieces : 2 * pieces + 4]
    d1_ref, d2_ref, h_ref, bg_ref, bu_ref, bs_ref = refs[2 * pieces + 4 : 2 * pieces + 10]
    x_scr, g_scr, sems = refs[2 * pieces + 10 :]
    step = pl.program_id(0)
    half = pl.num_programs(0) // 2
    plan = spans([r.shape[0] for r in x_refs], TILE)

    def copies(j):
        slot = j % 2
        made = []
        for i, (piece, row, count, place) in enumerate(plan[j]):
            for side, (sources, target) in enumerate(((x_refs, x_scr), (g_refs, g_scr))):
                made.append(
                    pltpu.make_async_copy(
                        sources[piece].at[pl.ds(row, count), :],
                        target.at[slot, pl.ds(place, count), :],
                        sems.at[slot, side, i],
                    )
                )
        return made

    @pl.when(step == 0)
    def _():
        for copy in copies(0):
            copy.start()

    for j in range(len(plan)):

        @pl.when(step == j)
        def _(j=j):
            if j + 1 < len(plan):
                for copy in copies(j + 1):
                    copy.start()
            for copy in copies(j):
                copy.wait()

    slot = step % 2
    rows = x_scr[slot]
    routes = g_scr[slot, :, D:].astype(f32)
    routed = gate_ref.shape[0]
    part = routed // EXP_LOC
    lane = lax.broadcasted_iota(jnp.int32, routes.shape, 1)
    scales = [
        jnp.sum(jnp.where(lane == first_ref[0] + e, routes, 0.0), axis=1, keepdims=True)
        for e in range(EXP_LOC)
    ]
    column = lax.broadcasted_iota(jnp.int32, (1, routed), 1)
    scale = jnp.where(column < part, scales[0], scales[1])
    grad_hidden = nt(g_scr[slot, :, :D], down_ref[...])

    def steps(gate_act, up_act, grad, scale):
        sigmoid = jax.nn.sigmoid(gate_act)
        silu = gate_act * sigmoid
        kept = silu * up_act
        if scale is not None:
            kept, grad = kept * scale, grad * scale
        back_gate = grad * up_act * (sigmoid + silu * (1.0 - sigmoid))
        return kept.astype(bf16), back_gate.astype(bf16), (grad * silu).astype(bf16)

    gate_act = nt(rows, gate_ref[...])
    up_act = nt(rows, up_ref[...])
    kept, back_gate, back_up = steps(gate_act, up_act, grad_hidden[:, :routed], scale)
    shared = nt(rows, shared_ref[...])
    kept_s, back_gate_s, back_up_s = steps(
        shared[:, :LANES], shared[:, LANES:], grad_hidden[:, routed:], None
    )
    h_ref[:, :routed] = kept
    h_ref[:, routed:] = kept_s
    bg_ref[...] = back_gate
    bu_ref[...] = back_up
    bs_ref[:, :LANES] = back_gate_s
    bs_ref[:, LANES:] = back_up_s
    result = nn(back_gate, gate_ref[...]) + nn(back_up, up_ref[...])
    result = (result + nn(bs_ref[...], shared_ref[...])).astype(bf16)

    @pl.when(step < half)
    def _():
        d1_ref[...] = result

    @pl.when(step >= half)
    def _():
        d2_ref[...] = result


def hidden_step(first, rows, grads, gate_all, up_all, shared_all, down_all):
    count = 4 * rows[0].shape[0]
    half = count // TILE
    routed = gate_all.shape[0]
    width = down_all.shape[0]

    def near(i, first):
        return (jnp.minimum(i, half - 1), 0)

    def far(i, first):
        return (jnp.maximum(i - half, 0), 0)

    def whole(i, first):
        return (0, 0)

    def step(i, first):
        return (i, 0)

    once = pl.Buffered(1)
    row_shape = jax.ShapeDtypeStruct((count, D), bf16)
    widths = (width, routed, routed, 2 * LANES)
    weights = (gate_all, up_all, shared_all, down_all)
    return pl.pallas_call(
        hidden_kernel,
        out_shape=(row_shape, row_shape)
        + tuple(jax.ShapeDtypeStruct((2 * count, w), bf16) for w in widths),
        grid_spec=pltpu.PrefetchScalarGridSpec(
            num_scalar_prefetch=1,
            grid=(2 * half,),
            in_specs=[pl.BlockSpec(memory_space=pl.ANY)] * (len(rows) + len(grads))
            + [pl.BlockSpec(w.shape, whole, pipeline_mode=once) for w in weights],
            out_specs=[pl.BlockSpec((TILE, D), near), pl.BlockSpec((TILE, D), far)]
            + [pl.BlockSpec((TILE, w), step) for w in widths],
            scratch_shapes=[
                pltpu.VMEM((2, TILE, D), bf16),
                pltpu.VMEM((2, TILE, D + LANES), bf16),
                pltpu.SemaphoreType.DMA((2, 2, TILE // UNIT)),
            ],
        ),
        compiler_params=pltpu.CompilerParams(vmem_limit_bytes=58 * 1024 * 1024),
        cost_estimate=pl.CostEstimate(
            flops=2 * count * D * (3 * routed + width + 4 * LANES + routed) * 2,
            bytes_accessed=2 * count * (3 * D + 3 * width) * 2 + 3 * D * width * 2,
            transcendentals=2 * count * width,
        ),
    )(first, *rows, *grads, *weights)


def weight_grad(lefts, rights, left_start, left_width, shape, dtype=f32):
    places = shape[0]
    stride = left_width // places
    used = shape[1]
    tile = 512
    left_steps = spans([p.shape[0] for p in lefts], tile)
    right_steps = spans([p.shape[0] for p in rights], tile)
    steps = list(zip(left_steps, right_steps))

    def kernel(*refs):
        left_refs, right_refs = refs[: len(lefts)], refs[len(lefts) : len(lefts) + len(rights)]
        out_ref, sum_ref, left_buf, right_buf, left_sems, right_sems = refs[len(lefts) + len(rights) :]

        def copies(i):
            slot = i % 2
            made = []
            for n, (piece, row, count, place) in enumerate(steps[i][0]):
                made.append(
                    pltpu.make_async_copy(
                        left_refs[piece].at[pl.ds(row, count), pl.ds(left_start, left_width)],
                        left_buf.at[slot, pl.ds(place, count), :],
                        left_sems.at[slot, n],
                    )
                )
            for n, (piece, row, count, place) in enumerate(steps[i][1]):
                made.append(
                    pltpu.make_async_copy(
                        right_refs[piece].at[pl.ds(row, count), pl.ds(0, D)],
                        right_buf.at[slot, pl.ds(place, count), :],
                        right_sems.at[slot, n],
                    )
                )
            return made

        for copy in copies(0):
            copy.start()
        for i in range(len(steps)):
            if i + 1 < len(steps):
                for copy in copies(i + 1):
                    copy.start()
            for copy in copies(i):
                copy.wait()
            product = tn(left_buf[i % 2], right_buf[i % 2])
            if i == 0:
                sum_ref[...] = product
            else:
                sum_ref[...] += product
        for e in range(places):
            out_ref[e] = sum_ref[e * stride : e * stride + used, :].astype(dtype)

    return pl.pallas_call(
        kernel,
        out_shape=jax.ShapeDtypeStruct(shape, dtype),
        in_specs=[pl.BlockSpec(memory_space=pl.ANY)] * (len(lefts) + len(rights)),
        out_specs=pl.BlockSpec(memory_space=pltpu.VMEM),
        scratch_shapes=[
            pltpu.VMEM((left_width, D), f32),
            pltpu.VMEM((2, tile, left_width), bf16),
            pltpu.VMEM((2, tile, D), bf16),
            pltpu.SemaphoreType.DMA((2, tile // UNIT)),
            pltpu.SemaphoreType.DMA((2, tile // UNIT)),
        ],
        compiler_params=pltpu.CompilerParams(vmem_limit_bytes=58 * 1024 * 1024),
        cost_estimate=pl.CostEstimate(
            flops=2 * tile * len(steps) * D * left_width,
            bytes_accessed=2 * tile * len(steps) * (D + left_width) + 4 * D * left_width,
            transcendentals=0,
        ),
    )(*lefts, *rights)


def shared_grad(backs, hiddens, rows, grads, hidden_start, used):
    tile = 512
    sources = (backs, rows, hiddens, grads)
    starts = (0, 0, hidden_start, 0)
    widths = (2 * LANES, D, LANES, D)
    plans = [spans([p.shape[0] for p in arrays], tile) for arrays in sources]
    flat = [a for arrays in sources for a in arrays]
    side = D // 8

    def kernel(*refs):
        groups, place = [], 0
        for arrays in sources:
            groups.append(refs[place : place + len(arrays)])
            place += len(arrays)
        out_ref, sum_ref = refs[place], refs[place + 1]
        bufs, sems = refs[place + 2 : place + 6], refs[place + 6]

        def copies(i):
            slot = i % 2
            made = []
            for n, (group, plan) in enumerate(zip(groups, plans)):
                for m, (piece, row, count, target) in enumerate(plan[i]):
                    made.append(
                        pltpu.make_async_copy(
                            group[piece].at[pl.ds(row, count), pl.ds(starts[n], widths[n])],
                            bufs[n].at[slot, pl.ds(target, count), :],
                            sems.at[slot, n, m],
                        )
                    )
            return made

        for copy in copies(0):
            copy.start()
        for i in range(len(plans[0])):
            if i + 1 < len(plans[0]):
                for copy in copies(i + 1):
                    copy.start()
            for copy in copies(i):
                copy.wait()
            slot = i % 2
            first = tn(bufs[0][slot], bufs[1][slot])
            second = tn(bufs[2][slot], bufs[3][slot])
            if i == 0:
                sum_ref[: 2 * LANES] = first
                sum_ref[2 * LANES :] = second
            else:
                sum_ref[: 2 * LANES] += first
                sum_ref[2 * LANES :] += second
        for d in range(8):
            for n in range(3):
                part = sum_ref[n * LANES : n * LANES + used, d * side : (d + 1) * side]
                out_ref[d, n * used : (n + 1) * used, :] = part.astype(bf16)

    return pl.pallas_call(
        kernel,
        out_shape=jax.ShapeDtypeStruct((8, 3 * used, side), bf16),
        in_specs=[pl.BlockSpec(memory_space=pl.ANY)] * len(flat),
        out_specs=pl.BlockSpec(memory_space=pltpu.VMEM),
        scratch_shapes=[pltpu.VMEM((3 * LANES, D), f32)]
        + [pltpu.VMEM((2, tile, w), bf16) for w in widths]
        + [pltpu.SemaphoreType.DMA((2, 4, tile // UNIT))],
        compiler_params=pltpu.CompilerParams(vmem_limit_bytes=58 * 1024 * 1024),
        cost_estimate=pl.CostEstimate(
            flops=2 * tile * len(plans[0]) * D * 3 * LANES,
            bytes_accessed=2 * tile * len(plans[0]) * (2 * D + 3 * LANES),
            transcendentals=0,
        ),
    )(*flat)


def first_kernel(place_ref, x_ref, *refs):
    pieces, (out_ref, w_ref, kv_ref, sems) = refs[:8], refs[8:]
    rows = w_ref.shape[0] // 8
    kv_rows = kv_ref.shape[0] // 8
    copies = []
    for j, piece in enumerate(pieces):
        copies.append(
            pltpu.make_async_copy(
                piece.at[pl.ds(0, rows), :], w_ref.at[pl.ds(j * rows, rows), :], sems.at[0, j]
            )
        )
        start = pl.multiple_of(place_ref[j] * kv_rows, kv_rows)
        copies.append(
            pltpu.make_async_copy(
                piece.at[pl.ds(rows, kv_rows), :], kv_ref.at[pl.ds(start, kv_rows), :], sems.at[1, j]
            )
        )
    for copy in copies:
        copy.start()
    for copy in copies:
        copy.wait()
    out_ref[...] = nn(x_ref[...], w_ref[...])


def first_step(places, rows, pieces, kv_rows):
    side = pieces[0].shape[0] - kv_rows
    width = pieces[0].shape[1]
    vmem = pl.BlockSpec(memory_space=pltpu.VMEM)
    return pl.pallas_call(
        first_kernel,
        out_shape=(
            jax.ShapeDtypeStruct((rows.shape[0], width), f32),
            jax.ShapeDtypeStruct((8 * side, width), bf16),
            jax.ShapeDtypeStruct((8 * kv_rows, width), bf16),
        ),
        in_specs=[pl.BlockSpec(memory_space=pltpu.SMEM), vmem]
        + [pl.BlockSpec(memory_space=pl.ANY)] * 8,
        out_specs=(vmem, vmem, vmem),
        scratch_shapes=[pltpu.SemaphoreType.DMA((2, 8))],
        compiler_params=pltpu.CompilerParams(vmem_limit_bytes=58 * 1024 * 1024),
    )(places, rows, *pieces)


def out_kernel(x_ref, *refs):
    pieces, (kept_ref, sent_ref, w_ref, sems) = refs[:8], refs[8:]
    rows = w_ref.shape[0] // 8
    copies = [
        pltpu.make_async_copy(piece, w_ref.at[pl.ds(j * rows, rows), :], sems.at[j])
        for j, piece in enumerate(pieces)
    ]
    for copy in copies:
        copy.start()
    for copy in copies:
        copy.wait()
    half = kept_ref.shape[0]
    kept_ref[...] = nt(x_ref[:half], w_ref[...])
    sent_ref[...] = nt(x_ref[half:], w_ref[...]).astype(bf16)


def out_step(rows, pieces):
    half = rows.shape[0] // 2
    vmem = pl.BlockSpec(memory_space=pltpu.VMEM)
    return pl.pallas_call(
        out_kernel,
        out_shape=(
            jax.ShapeDtypeStruct((half, D), f32),
            jax.ShapeDtypeStruct((half, D), bf16),
            jax.ShapeDtypeStruct((D, rows.shape[1]), bf16),
        ),
        in_specs=[vmem] + [pl.BlockSpec(memory_space=pl.ANY)] * 8,
        out_specs=(vmem, vmem, vmem),
        scratch_shapes=[pltpu.SemaphoreType.DMA((8,))],
        compiler_params=pltpu.CompilerParams(vmem_limit_bytes=58 * 1024 * 1024),
    )(rows, *pieces)


def pack_kernel(place_ref, x_ref, query_ref, latent_ref, norm_ref, kv_ref, *refs):
    out_refs, kv_scr = refs[:8], refs[8]
    kv_scr[...] = tn(norm_ref[...], kv_ref[...]).astype(bf16)
    rows = x_ref.shape[1] // 8
    query = query_ref.shape[1]
    kv_rows = norm_ref.shape[1] // 8
    for j, out_ref in enumerate(out_refs):
        part = x_ref[:, j * rows : (j + 1) * rows]
        out_ref[:rows, :query] = tn(part, query_ref[...]).astype(bf16)
        out_ref[:rows, query:] = tn(part, latent_ref[...]).astype(bf16)
        start = pl.multiple_of(place_ref[j] * kv_rows, kv_rows)
        out_ref[rows:, :] = kv_scr[pl.ds(start, kv_rows), :]


def pack_step(places, rows, grad_query, grad_latent, latent_norm, grad_kv):
    vmem = pl.BlockSpec(memory_space=pltpu.VMEM)
    width = grad_kv.shape[1]
    count = (rows.shape[1] + latent_norm.shape[1]) // 8
    grad_latent = jnp.pad(
        grad_latent, ((0, 0), (0, width - grad_query.shape[1] - grad_latent.shape[1]))
    )
    return pl.pallas_call(
        pack_kernel,
        out_shape=(jax.ShapeDtypeStruct((count, width), bf16),) * 8,
        in_specs=[pl.BlockSpec(memory_space=pltpu.SMEM)] + [vmem] * 5,
        out_specs=(vmem,) * 8,
        scratch_shapes=[pltpu.VMEM((latent_norm.shape[1], width), bf16)],
        compiler_params=pltpu.CompilerParams(vmem_limit_bytes=58 * 1024 * 1024),
    )(places, rows, grad_query, grad_latent, latent_norm, grad_kv)


def dense_shards(*arrays):
    return dense_layer(*arrays)


def dense_layer(
    block_input,
    cotangent,
    norm1_gain,
    latent_gain,
    norm2_gain,
    w_query,
    w_latent,
    w_kv,
    w_out,
    expert_gate,
    expert_up,
    expert_down,
    shared_gate,
    shared_up,
    shared_down,
    routed_expert_index,
    slots,
    gate_weights,
):
    f = lax.axis_index(FSDP)
    h = lax.axis_index(HEADS)
    t = lax.axis_index(TENSOR)
    row_count = block_input.shape[0]
    head_dim = NOPE + ROPE
    local_heads = w_query.shape[1] // head_dim
    query_width = local_heads * head_dim
    score_scale = head_dim ** (-0.5)
    hosts = lax.axis_size(FSDP) * lax.axis_size(HEADS)
    experts = EXP_LOC * hosts
    capacity = row_count * TOP * 5 // (4 * experts)

    relative = [(f ^ dx) * 4 + (t + k) % 4 for dx in range(2) for k in range(4)]
    absolute = [(F ^ f) * 4 + (T - t) % 4 for F in range(2) for T in range(4)]
    turns = (0, 2, 1, 3)

    def chunks_to(array, order, axis):
        return jnp.concatenate([pick(array, i, 8, axis) for i in order], axis=axis)

    def quarter(array):
        return pick(array, h, 4, 0)

    def rows_relative(array):
        return jnp.concatenate([pick(array, h ^ j, 4, 0) for j in turns], axis=0)

    def rows_absolute(array):
        places = [h ^ i for i in range(4)]
        return jnp.concatenate([pick(array, (p % 2) * 2 + p // 2, 4, 0) for p in places], axis=0)

    def reduce_heads(kept, sent):
        summed = kept + swap_heads(sent.astype(bf16), 1).astype(f32)
        half = summed.shape[0] // 2
        return summed[:half] + swap_heads(summed[half:].astype(bf16), 2).astype(f32)

    def gather_heads(own):
        near = jnp.concatenate([own, swap_heads(own, 2)], axis=0)
        return jnp.concatenate([near, swap_heads(near, 1)], axis=0)

    query_rows = w_query.shape[0]
    latent_width = w_latent.shape[1] // 4
    latent_stop = query_width + latent_width
    kv_width = w_kv.shape[1]

    def fill(piece, axis, size):
        return jnp.pad(piece, [(0, size - piece.shape[axis] if a == axis else 0) for a in range(2)])

    first_pack = jnp.concatenate([w_query, pick(w_latent, h, 4, 1)], axis=1)
    first_pack = jnp.concatenate([fill(first_pack, 1, kv_width), w_kv], axis=0)
    first_along, first_far = gather_weight(first_pack)
    first_parts = first_along + first_far

    own_ids, own_slots, own_gates = quarter(routed_expert_index), quarter(slots), quarter(gate_weights)
    lanes = jnp.arange(LANES)[None, None, :]
    used_route = (own_ids[:, :, None] == lanes) & (own_slots[:, :, None] < capacity)
    route_weights = jnp.sum(jnp.where(used_route, own_gates[:, :, None].astype(f32), 0.0), axis=1)
    cotangent_own = quarter(cotangent)
    grad_unit = jnp.concatenate([cotangent_own, route_weights.astype(bf16)], axis=1)

    hidden = expert_gate.shape[2]
    part = -(-hidden // LANES) * LANES
    shared_own = lax.all_to_all(
        jnp.stack([shared_gate.T, shared_up.T, shared_down]),
        PLANE,
        split_axis=1,
        concat_axis=2,
        tiled=True,
    )
    shared_hidden = shared_own.shape[1]

    def side_by_side(routed):
        return jnp.pad(routed, ((0, 0), (0, part - hidden), (0, 0))).reshape(-1, D)

    gate_all = side_by_side(jnp.swapaxes(expert_gate, 1, 2))
    up_all = side_by_side(jnp.swapaxes(expert_up, 1, 2))
    shared_own = after(shared_own, first_along[1], first_along[3])
    shared_all = jnp.concatenate([fill(shared_own[i], 0, LANES) for i in range(2)], axis=0)
    down_all = jnp.concatenate([side_by_side(expert_down), fill(shared_own[2], 0, LANES)], axis=0)

    residual = chunks_to(block_input, relative, 1).astype(f32)
    gain1 = chunks_to(norm1_gain, relative, 0)
    first_normed, first_inverse = rms_parts(residual)
    first_input = (first_normed * gain1).astype(bf16)
    cosine, sine_table = rope_tables(row_count)
    first_input = after(first_input, gate_all, up_all, shared_all, down_all)
    places = jnp.stack(relative).astype(jnp.int32)
    first_out, w_first, kv_full = first_step(places, first_input, first_parts, w_kv.shape[0])
    w_queries, w_latents = w_first[:, :query_width], w_first[:, query_width:latent_stop]
    latent_own = first_out[:, query_width:latent_stop].astype(bf16).T
    latent_raw = rows_absolute(gather_heads(latent_own)).T.astype(f32)
    query_raw = first_out[:, :query_width].reshape(row_count, local_heads, head_dim)
    queries = jnp.concatenate(
        [
            query_raw[..., :NOPE],
            rotate(query_raw[..., NOPE:], cosine[:, None, :], sine_table[:, None, :]),
        ],
        axis=-1,
    ).astype(bf16)
    latent_normed, latent_inverse = rms_parts(latent_raw[:, :KVR])
    latent_norm = (latent_normed * latent_gain).astype(bf16)
    key_rope = rotate(latent_raw[:, KVR:], cosine, sine_table).astype(bf16)
    key_value = nn(latent_norm, kv_full).astype(bf16).reshape(row_count, local_heads, NOPE + VDIM)
    keys = jnp.concatenate(
        [
            key_value[..., :NOPE],
            jnp.broadcast_to(key_rope[:, None, :], (row_count, local_heads, ROPE)),
        ],
        axis=-1,
    )
    values = key_value[..., NOPE:]
    out_along, out_far = gather_weight(w_out.T)
    causal = jnp.arange(LEN)[:, None] >= jnp.arange(LEN)[None, :]

    def score_block():
        scores = jnp.einsum(SCORE, queries, keys, preferred_element_type=f32) * score_scale
        return jnp.where(causal[None], scores, -1e30)

    scores = score_block()
    highest_score = jnp.max(scores, axis=-1, keepdims=True)
    log_total = highest_score + jnp.log(
        jnp.sum(jnp.exp(scores - highest_score), axis=-1, keepdims=True)
    )
    probabilities = jnp.exp(scores - log_total).astype(bf16)
    context = jnp.einsum(MIX, probabilities, values, preferred_element_type=f32)
    context = rows_relative(context.astype(bf16).reshape(row_count, local_heads * VDIM))
    kept, sent, out_full = out_step(context, out_along + out_far)
    attention_own = reduce_heads(kept, sent)
    after_attention = quarter(block_input).astype(f32) + chunks_to(attention_own, absolute, 1)
    second_normed, second_inverse = rms_parts(after_attention)
    second_input = (second_normed * norm2_gain).astype(bf16)

    rows = gather_rows(second_input)
    grads = gather_rows(grad_unit)
    first_expert = ((f * lax.axis_size(HEADS) + h) * EXP_LOC).astype(jnp.int32).reshape(1)
    grad_groups, hidden_parts, gate_parts, up_parts, shared_parts = [], [], [], [], []
    for rows_g, grads_g in zip(rows, grads):
        near, far, hidden_g, gate_g, up_g, shared_g = hidden_step(
            first_expert, rows_g, grads_g, gate_all, up_all, shared_all, down_all
        )
        grad_groups.append((near, far))
        hidden_parts.append(hidden_g)
        gate_parts.append(gate_g)
        up_parts.append(up_g)
        shared_parts.append(shared_g)
    grad_second = scatter_rows(grad_groups)

    second_gain_part = jnp.sum(grad_second * second_normed, axis=0)
    grad_after = cotangent_own.astype(f32) + rms_back(
        grad_second, second_normed, second_inverse, norm2_gain
    )
    grad_after = chunks_to(grad_after, relative, 1)
    grad_attention = gather_heads(grad_after.astype(bf16))
    out_part = tn(grad_attention, context)
    grad_context = nn(grad_attention, out_full).astype(bf16)
    grad_context = rows_absolute(grad_context).reshape(row_count, local_heads, VDIM)
    probabilities = jnp.exp(score_block() - log_total)
    grad_probs = jnp.einsum(SCORE, grad_context, values, preferred_element_type=f32)
    centred = jnp.sum(probabilities * grad_probs, axis=-1, keepdims=True)
    grad_scores = (probabilities * (grad_probs - centred)).astype(bf16)
    grad_queries = (
        jnp.einsum(MIX, grad_scores, keys, preferred_element_type=f32) * score_scale
    )
    grad_keys = (
        jnp.einsum(BACK, grad_scores, queries, preferred_element_type=f32) * score_scale
    )
    grad_values = jnp.einsum(
        BACK, probabilities.astype(bf16), grad_context, preferred_element_type=f32
    )
    grad_query_raw = (
        jnp.concatenate(
            [
                grad_queries[..., :NOPE],
                unrotate(grad_queries[..., NOPE:], cosine[:, None, :], sine_table[:, None, :]),
            ],
            axis=-1,
        )
        .astype(bf16)
        .reshape(row_count, query_width)
    )
    first_from_query = nt(rows_relative(grad_query_raw), w_queries)
    grad_key_value = (
        jnp.concatenate([grad_keys[..., :NOPE], grad_values], axis=-1)
        .astype(bf16)
        .reshape(row_count, local_heads * (NOPE + VDIM))
    )
    grad_latent_norm = nt(grad_key_value, kv_full)
    latent_gain_part = jnp.sum(grad_latent_norm * latent_normed, axis=0)
    grad_compressed = rms_back(grad_latent_norm, latent_normed, latent_inverse, latent_gain)
    grad_key_rope = unrotate(jnp.sum(grad_keys[..., NOPE:], axis=1), cosine, sine_table)
    latent_term = jnp.concatenate([grad_compressed, grad_key_rope], axis=-1)
    latent_term = rows_relative(latent_term.T)
    half = latent_term.shape[0] // 2
    grad_latent = reduce_heads(latent_term[:half], latent_term[half:]).astype(bf16)
    grad_latent_rows = jnp.concatenate([pick(grad_latent, h ^ j, 4, 1) for j in turns], axis=1)
    first_from_latent = lax.dot_general(
        grad_latent_rows, w_latents, (((0,), (1,)), ((), ())), preferred_element_type=f32
    )
    first_pieces = pack_step(
        places, first_input, grad_query_raw, grad_latent.T, latent_norm, grad_key_value
    )
    grad_first = reduce_heads(
        first_from_query[: row_count // 2] + first_from_latent[: row_count // 2],
        first_from_query[row_count // 2 :] + first_from_latent[row_count // 2 :],
    )
    first_normed_own = quarter(first_normed)
    first_gain_part = jnp.sum(grad_first * first_normed_own, axis=0)
    input_own = grad_after + rms_back(grad_first, first_normed_own, quarter(first_inverse), gain1)
    input_grad = rows_absolute(gather_heads(chunks_to(input_own.astype(bf16), absolute, 1))).astype(f32)

    w_out_grad = scatter_weight(out_part.reshape(8, -1, out_part.shape[1])).T
    first_grad = scatter_weight(first_pieces)
    w_query_grad = first_grad[:query_rows, :query_width]
    w_kv_grad = first_grad[query_rows:]
    gain_parts = jnp.concatenate(
        [
            first_gain_part.reshape(8, -1),
            chunks_to(second_gain_part, relative, 0).reshape(8, -1),
            chunks_to(latent_gain_part, relative, 0).reshape(8, -1),
        ],
        axis=1,
    ).reshape(8, -1, latent_width)
    gain_parts = scatter_weight(gain_parts)
    last = jnp.concatenate([first_grad[:query_rows, query_width:latent_stop], gain_parts], axis=0)
    last = rows_absolute(gather_heads(last.astype(bf16))).reshape(4, -1, latent_width).astype(f32)
    latent_rows = w_latent.shape[0]
    w_latent_grad = jnp.concatenate([last[i, :latent_rows] for i in range(4)], axis=1)
    gains = jnp.sum(last[:, latent_rows:], axis=0).reshape(-1)
    side = D // 8

    out_groups = []
    for hidden_g in hidden_parts:
        half = hidden_g.shape[0] // 2
        pair = tuple(nn(p, down_all).astype(bf16) for p in (hidden_g[:half], hidden_g[half:]))
        out_groups.append(tuple(after(p, grad_attention) for p in pair))
    ffn_own = scatter_rows(out_groups)
    output = rows_absolute(gather_heads((after_attention + ffn_own).astype(bf16)))
    rows_list = [p for g in rows for p in g]
    grads_list = [p for g in grads for p in g]
    routed = EXP_LOC * part
    shared_grads = shared_grad(shared_parts, hidden_parts, rows_list, grads_list, routed, shared_hidden)
    shared_grads = lax.all_to_all(
        after(shared_grads, grad_query_raw), PLANE, split_axis=0, concat_axis=0, tiled=True
    ).reshape(8, 3, shared_hidden, -1)
    shared_grads = [shared_grads[:, i].astype(f32).reshape(8 * shared_hidden, -1) for i in range(3)]
    expert_grads = []
    for lefts, rights in ((gate_parts, rows_list), (up_parts, rows_list), (hidden_parts, grads_list)):
        expert_grads.append(weight_grad(lefts, rights, 0, routed, (EXP_LOC, hidden, D)))
    return (
        output,
        input_grad,
        gains[:side],
        gains[2 * side :],
        gains[side : 2 * side],
        w_query_grad,
        w_latent_grad,
        w_kv_grad,
        w_out_grad,
        jnp.swapaxes(expert_grads[0], 1, 2),
        jnp.swapaxes(expert_grads[1], 1, 2),
        expert_grads[2],
        shared_grads[0].T,
        shared_grads[1].T,
        shared_grads[2],
    )


def solution(mesh):
    in_specs = (
        P((FSDP, TENSOR), None),
        P((FSDP, TENSOR), None),
        P(),
        P(),
        P(),
        P((FSDP, TENSOR), HEADS),
        P((FSDP, TENSOR), None),
        P((FSDP, TENSOR), HEADS),
        P(HEADS, (FSDP, TENSOR)),
        P((FSDP, HEADS), None, TENSOR),
        P((FSDP, HEADS), None, TENSOR),
        P((FSDP, HEADS), TENSOR, None),
        P((FSDP, HEADS), TENSOR),
        P((FSDP, HEADS), TENSOR),
        P(TENSOR, (FSDP, HEADS)),
        P((FSDP, TENSOR), None),
        P((FSDP, TENSOR), None),
        P((FSDP, TENSOR), None),
    )
    out_specs = (
        P((FSDP, TENSOR), None),
        P((FSDP, TENSOR), None),
        P((FSDP, TENSOR)),
        P((FSDP, TENSOR)),
        P((FSDP, TENSOR)),
        P((FSDP, TENSOR), HEADS),
        P((FSDP, TENSOR), None),
        P((FSDP, TENSOR), HEADS),
        P(HEADS, (FSDP, TENSOR)),
        P((FSDP, HEADS), None, TENSOR),
        P((FSDP, HEADS), None, TENSOR),
        P((FSDP, HEADS), TENSOR, None),
        P((FSDP, HEADS), TENSOR),
        P((FSDP, HEADS), TENSOR),
        P(TENSOR, (FSDP, HEADS)),
    )
    dense = tuple(mesh.shape[a] for a in (FSDP, HEADS, TENSOR)) == (2, 4, 4)
    program = dense_shards if dense else shards
    program = jax.shard_map(
        program, mesh=mesh, in_specs=in_specs, out_specs=out_specs, check_vma=False
    )
    return program
```

profile of v0, /device:TPU:0, one launch (start us, length us, event | category | flops | bytes accessed | tf_op | source)
XLA Modules:
  0.0 951.9 jit_solution(2162741731124260361)
XLA Ops:
  4.6 5.1 collective-permute-start
  14.3 4.3 all-to-all-start
  27.7 4.2 pad.28
  35.8 5.0 convert_multiply_fusion
  42.7 23.3 %collective-permute-done.2.refs_2_ = bf16[320,1024]{1,0:T(8,128)(2,1)} collective-permute-done((bf16[320,1024]{1,0:T(8,128)(2,1)}, bf16[320,1024]{1,0:T(8,128)(2,1)}, u32[]{:S(2)}, u32[]{:S(2)}) %collective-permute-start.2) | collective-permute-done | bytes 655392 | tf_op jit(solution)/shard_map/ppermute | solution.py:473
  68.0 3.1 copy.244
  71.2 2.7 all_to_all.19
  78.4 5.5 collective-permute-done.5.refs_6_
  83.9 12.1 %collective-permute-done.6.refs_7_ = bf16[320,1024]{1,0:T(8,128)(2,1)} collective-permute-done((bf16[320,1024]{1,0:T(8,128)(2,1)}, bf16[320,1024]{1,0:T(8,128)(2,1)}, u32[]{:S(2)}, u32[]{:S(2)}) %collective-permute-start.6) | collective-permute-done | bytes 655392 | tf_op jit(solution)/shard_map/ppermute | solution.py:481
  96.0 7.8 shard_map.289
  113.4 3.3 collective-permute-done.9.refs_1_
  118.2 11.6 %collective-permute-done.10.refs_2_ = bf16[256,512]{1,0:T(8,128)(2,1)} collective-permute-done((bf16[256,512]{1,0:T(8,128)(2,1)}, bf16[256,512]{1,0:T(8,128)(2,1)}, u32[]{:S(2)}, u32[]{:S(2)}) %collective-permute-start.10) | collective-permute-done | bytes 262176 | tf_op jit(solution)/shard_map/ppermute | solution.py:473
  153.1 5.8 shard_map.290
  169.9 33.7 %collective-permute-done.44 = bf16[128,2176]{1,0:T(8,128)(2,1)} collective-permute-done((bf16[128,2176]{1,0:T(8,128)(2,1)S(1)}, bf16[128,2176]{1,0:T(8,128)(2,1)}, u32[]{:S(2)}, u32[]{:S(2)}) %collective-permute-start.44) | collective-permute-done | bytes 557088 | tf_op jit(solution)/shard_map/ppermute | solution.py:473
  207.1 11.3 %collective-permute-done.17 = bf16[128,2048]{1,0:T(8,128)(2,1)S(1)} collective-permute-done((bf16[128,2048]{1,0:T(8,128)(2,1)S(1)}, bf16[128,2048]{1,0:T(8,128)(2,1)S(1)}, u32[]{:S(2)}, u32[]{:S(2)}) %collective-permute-start.17) | collective-permute-done | bytes 524320 | tf_op jit(solution)/shard_map/ppermute | solution.py:485
  223.2 7.5 collective-permute-done.68.refs_10_.refs_21_.refs_48_
  231.9 10.7 %collective-permute-done.27.refs_11_.refs_6_.refs_33_ = bf16[128,2176]{1,0:T(8,128)(2,1)S(1)} collective-permute-done((bf16[128,2176]{1,0:T(8,128)(2,1)}, bf16[128,2176]{1,0:T(8,128)(2,1)S(1)}, u32[]{:S(2)}, u32[]{:S(2)}) %collective-permute-start.27) | collective-permute-done | bytes 557088 | tf_op jit(solution)/shard_map/ppermute | solution.py:494
  245.1 7.4 collective-permute-done.69.refs_11_.refs_22_.refs_49_
  252.8 5.3 collective-permute-done.46.refs_9_.refs_12_.refs_39_
  258.7 5.8 collective-permute-done.47.refs_10_.refs_13_.refs_40_
  264.5 13.3 %collective-permute-start.36 = (bf16[128,2048]{1,0:T(8,128)(2,1)S(1)}, bf16[128,2048]{1,0:T(8,128)(2,1)S(1)}, u32[]{:S(2)}, u32[]{:S(2)}) collective-permute-start(bf16[128,2048]{1,0:T(8,128)(2,1)S(1)} %multiply_convert_fusion.2.refs_0_.refs_3_), channel_id=1, source_target_pairs={{3,0},{0,1},{1,2},{2,3},{7,4},{4,5},{5,6},{6,7},{11,8},{8,9},{9,10... | collective-permute-start | bytes 1572872 | tf_op jit(solution)/shard_map/ppermute | solution.py:473
  278.4 11.3 %collective-permute-start.58 = (bf16[128,2048]{1,0:T(8,128)(2,1)S(1)}, bf16[128,2048]{1,0:T(8,128)(2,1)}, u32[]{:S(2)}, u32[]{:S(2)}) collective-permute-start(bf16[128,2048]{1,0:T(8,128)(2,1)S(1)} %multiply_convert_fusion.2.refs_0_.refs_3_), channel_id=1, source_target_pairs={{2,0},{3,1},{0,2},{1,3},{6,4},{7,5},{4,6},{5,7},{10,8},{11,9},{8,1... | collective-permute-start | bytes 1572872 | tf_op jit(solution)/shard_map/ppermute | solution.py:473
  292.3 21.2 %collective-permute-done.58.refs_0_.refs_19_ = bf16[128,2048]{1,0:T(8,128)(2,1)} collective-permute-done((bf16[128,2048]{1,0:T(8,128)(2,1)S(1)}, bf16[128,2048]{1,0:T(8,128)(2,1)}, u32[]{:S(2)}, u32[]{:S(2)}) %collective-permute-start.58) | collective-permute-done | bytes 524320 | tf_op jit(solution)/shard_map/ppermute | solution.py:473
  318.9 30.5 %shard_map.291 = (bf16[512,2048]{1,0:T(8,128)(2,1)}, bf16[512,2048]{1,0:T(8,128)(2,1)}, bf16[1024,896]{1,0:T(8,128)(2,1)}, bf16[1024,768]{1,0:T(8,128)(2,1)}, bf...) custom-call(s32[1]{0:T(128)} %bitcast.30.first_ref, bf16[128,2048]{1,0:T(8,128)(2,1)} %copy-done.31, ...), custom_call_target="tpu_custom_call" | custom-call | flops 18790481920 | bytes 29097984 | tf_op jit(solution)/shard_map/pallas_call | solution.py:691
  351.8 5.0 convolution_convert_fusion.4
  360.1 3.6 convolution_convert_fusion.5
  363.7 4.9 collective-permute-done.61.refs_3_.refs_22_
  370.8 51.1 %shard_map.292 = (bf16[1024,2048]{1,0:T(8,128)(2,1)}, bf16[1024,2048]{1,0:T(8,128)(2,1)}, bf16[2048,896]{1,0:T(8,128)(2,1)}, bf16[2048,768]{1,0:T(8,128)(2,1)}, ...) custom-call(s32[1]{0:T(128)} %bitcast.30.first_ref, bf16[256,2048]{1,0:T(8,128)(2,1)} %copy-done.28, ...), custom_call_target="tpu_custom_call" | custom-call | flops 37580963840 | bytes 47185920 | tf_op jit(solution)/shard_map/pallas_call | solution.py:691
  423.1 30.7 %shard_map.293 = (bf16[512,2048]{1,0:T(8,128)(2,1)}, bf16[512,2048]{1,0:T(8,128)(2,1)}, bf16[1024,896]{1,0:T(8,128)(2,1)}, bf16[1024,768]{1,0:T(8,128)(2,1)}, bf...) custom-call(s32[1]{0:T(128)} %bitcast.30.first_ref, bf16[128,2048]{1,0:T(8,128)(2,1)} %collective-permute-done.58.refs_0_.refs_19_, ...), custom_call_target="tpu_custom_call" | custom-call | flops 18790481920 | bytes 29097984 | tf_op jit(solution)/shard_map/pallas_call | solution.py:691
  454.0 5.0 convolution_convert_fusion.2
  458.9 3.7 convolution_convert_fusion.3
  465.3 20.4 %shard_map.297 = f32[2,352,2048]{2,1,0:T(8,128)} custom-call(bf16[1024,896]{1,0:T(8,128)(2,1)} %get-tuple-element.62.refs_0_.refs_27_, bf16[2048,896]{1,0:T(8,128)(2,1)} %get-tuple-element.71.refs_1_.refs_28_, bf16[1024,896]{1,0:T(8,128)(2,1)} %get-tuple-element.74.refs_2_.refs_29_, bf16[128,2176]{1,0:T(8,128)(2,1)} %copy-done.30, ...), custom_call_target="tpu_custom_call" | custom-call | flops 12884901888 | bytes 29360128 | tf_op jit(solution)/shard_map/pallas_call | solution.py:767
  485.6 4.0 add_convert_fusion.1
  493.3 20.4 %shard_map.295 = f32[2,352,2048]{2,1,0:T(8,128)} custom-call(bf16[1024,768]{1,0:T(8,128)(2,1)} %get-tuple-element.87.refs_0_, bf16[2048,768]{1,0:T(8,128)(2,1)} %get-tuple-element.88.refs_1_, bf16[1024,768]{1,0:T(8,128)(2,1)} %get-tuple-element.89.refs_2_, bf16[128,2048]{1,0:T(8,128)(2,1)} %copy-done.31, bf16[128,2048]{1,0:T(8,128)(2,1)} %copy-done.79, ...), custom_call_target="tpu_custom_call" | custom-call | flops 12884901888 | bytes 29360128 | tf_op jit(solution)/shard_map/pallas_call | solution.py:767
  513.7 13.4 %collective-permute-done.75 = bf16[256,2048]{1,0:T(8,128)(2,1)} collective-permute-done((bf16[256,2048]{1,0:T(8,128)(2,1)S(1)}, bf16[256,2048]{1,0:T(8,128)(2,1)}, u32[]{:S(2)}, u32[]{:S(2)}) %collective-permute-start.75) | collective-permute-done | bytes 1048608 | tf_op jit(solution)/shard_map/ppermute | solution.py:494
  531.1 3.1 add_convert_fusion.8
  534.7 20.2 %shard_map.296 = f32[2,352,2048]{2,1,0:T(8,128)} custom-call(bf16[1024,768]{1,0:T(8,128)(2,1)} %get-tuple-element.90.refs_0_, bf16[2048,768]{1,0:T(8,128)(2,1)} %get-tuple-element.91.refs_1_, bf16[1024,768]{1,0:T(8,128)(2,1)} %get-tuple-element.92.refs_2_, bf16[128,2048]{1,0:T(8,128)(2,1)} %copy-done.31, bf16[128,2048]{1,0:T(8,128)(2,1)} %copy-done.79, ...), custom_call_target="tpu_custom_call" | custom-call | flops 12884901888 | bytes 29360128 | tf_op jit(solution)/shard_map/pallas_call | solution.py:767
  562.7 3.4 collective-permute-start.57
  566.7 6.1 convolution_convert_fusion
  572.8 14.8 %collective-permute-done.77 = bf16[128,2048]{1,0:T(8,128)(2,1)S(1)} collective-permute-done((bf16[128,2048]{1,0:T(8,128)(2,1)S(1)}, bf16[128,2048]{1,0:T(8,128)(2,1)S(1)}, u32[]{:S(2)}, u32[]{:S(2)}) %collective-permute-start.77) | collective-permute-done | bytes 524320 | tf_op jit(solution)/shard_map/ppermute | solution.py:477
  587.6 10.9 %collective-permute-done.57 = bf16[128,2048]{1,0:T(8,128)(2,1)S(1)} collective-permute-done((bf16[128,2048]{1,0:T(8,128)(2,1)S(1)}, bf16[128,2048]{1,0:T(8,128)(2,1)S(1)}, u32[]{:S(2)}, u32[]{:S(2)}) %collective-permute-start.57) | collective-permute-done | bytes 524320 | tf_op jit(solution)/shard_map/ppermute | solution.py:477
  604.6 6.2 convolution_convert_fusion.1
  614.1 14.7 %shard_map.298 = bf16[8,264,256]{2,1,0:T(8,128)(2,1)} custom-call(bf16[1024,256]{1,0:T(8,128)(2,1)} %get-tuple-element.93.refs_0_, bf16[2048,256]{1,0:T(8,128)(2,1)} %get-tuple-element.94.refs_1_, bf16[1024,256]{1,0:T(8,128)(2,1)} %get-tuple-element.95.refs_2_, bf16[128,2048]{1,0:T(8,128)(2,1)} %copy-done.31, bf16[128,2048]{1,0:T(8,128)(2,1)} %copy-done.79, ...), custom_call_target="tpu_custom_call" | custom-call | flops 6442450944 | bytes 36700160 | tf_op jit(solution)/shard_map/pallas_call | solution.py:841
  629.5 3.2 convolution_convert_fusion.8
  633.9 3.9 multiply_reduce_fusion
  662.6 4.2 all-to-all-start.1
  666.9 6.1 fusion.4
  682.4 12.9 %collective-permute-start.122 = (bf16[256,512]{1,0:T(8,128)(2,1)S(1)}, bf16[256,512]{1,0:T(8,128)(2,1)S(1)}, u32[]{:S(2)}, u32[]{:S(2)}) collective-permute-start(bf16[256,512]{1,0:T(8,128)(2,1)S(1)} %get-tuple-element.211), channel_id=1, source_target_pairs={{0,2},{1,3},{2,0},{3,1},{4,6},{5,7},{6,4},{7,5},{8,10},{9,11},{10,... | collective-permute-start | bytes 786440 | tf_op jit(solution)/shard_map/ppermute | solution.py:477
  697.2 8.4 collective-permute-start.118
  711.0 6.1 shard_map.294
  724.5 10.6 %collective-permute-done.105 = bf16[320,1024]{1,0:T(8,128)(2,1)} collective-permute-done((bf16[320,1024]{1,0:T(8,128)(2,1)}, bf16[320,1024]{1,0:T(8,128)(2,1)}, u32[]{:S(2)}, u32[]{:S(2)}) %collective-permute-start.105) | collective-permute-done | bytes 655392 | tf_op jit(solution)/shard_map/ppermute | solution.py:481
  737.2 11.9 %collective-permute-done.103 = bf16[320,1024]{1,0:T(8,128)(2,1)} collective-permute-done((bf16[320,1024]{1,0:T(8,128)(2,1)}, bf16[320,1024]{1,0:T(8,128)(2,1)}, u32[]{:S(2)}, u32[]{:S(2)}) %collective-permute-start.103) | collective-permute-done | bytes 655392 | tf_op jit(solution)/shard_map/ppermute | solution.py:481
  751.0 12.2 %collective-permute-done.101 = bf16[320,1024]{1,0:T(8,128)(2,1)} collective-permute-done((bf16[320,1024]{1,0:T(8,128)(2,1)}, bf16[320,1024]{1,0:T(8,128)(2,1)}, u32[]{:S(2)}, u32[]{:S(2)}) %collective-permute-start.101) | collective-permute-done | bytes 655392 | tf_op jit(solution)/shard_map/ppermute | solution.py:481
  768.4 8.2 collective-permute-done.100
  778.7 3.2 collective-permute-done.106
  781.9 24.5 %collective-permute-done.104 = bf16[320,1024]{1,0:T(8,128)(2,1)S(1)} collective-permute-done((bf16[320,1024]{1,0:T(8,128)(2,1)S(1)}, bf16[320,1024]{1,0:T(8,128)(2,1)S(1)}, u32[]{:S(2)}, u32[]{:S(2)}) %collective-permute-start.104) | collective-permute-done | bytes 655392 | tf_op jit(solution)/shard_map/ppermute | solution.py:477
  823.3 3.0 add_convert_fusion
  831.0 3.1 collective-permute-start.111
  835.8 3.8 collective-permute-done.109
  843.0 20.7 %collective-permute-done.89 = bf16[256,2048]{1,0:T(8,128)(2,1)} collective-permute-done((bf16[256,2048]{1,0:T(8,128)(2,1)}, bf16[256,2048]{1,0:T(8,128)(2,1)}, u32[]{:S(2)}, u32[]{:S(2)}) %collective-permute-start.89) | collective-permute-done | bytes 1048608 | tf_op jit(solution)/shard_map/ppermute | solution.py:494
  870.9 13.5 %collective-permute-done.81 = bf16[256,2048]{1,0:T(8,128)(2,1)S(1)} collective-permute-done((bf16[256,2048]{1,0:T(8,128)(2,1)S(1)}, bf16[256,2048]{1,0:T(8,128)(2,1)S(1)}, u32[]{:S(2)}, u32[]{:S(2)}) %collective-permute-start.81) | collective-permute-done | bytes 1048608 | tf_op jit(solution)/shard_map/ppermute | solution.py:494
  908.0 3.6 collective-permute-done.91
  911.6 14.6 %collective-permute-done.87 = bf16[128,2048]{1,0:T(8,128)(2,1)} collective-permute-done((bf16[128,2048]{1,0:T(8,128)(2,1)}, bf16[128,2048]{1,0:T(8,128)(2,1)}, u32[]{:S(2)}, u32[]{:S(2)}) %collective-permute-start.87) | collective-permute-done | bytes 524320 | tf_op jit(solution)/shard_map/ppermute | solution.py:477
  933.1 10.5 %collective-permute-done.92 = bf16[128,2048]{1,0:T(8,128)(2,1)S(1)} collective-permute-done((bf16[128,2048]{1,0:T(8,128)(2,1)S(1)}, bf16[128,2048]{1,0:T(8,128)(2,1)S(1)}, u32[]{:S(2)}, u32[]{:S(2)}) %collective-permute-start.92) | collective-permute-done | bytes 524320 | tf_op jit(solution)/shard_map/ppermute | solution.py:485
  (694 shorter events, 266.6 us)
Async XLA Ops:
  4.6 36.3 %collective-permute-start = (bf16[320,1024]{1,0:T(8,128)(2,1)}, bf16[320,1024]{1,0:T(8,128)(2,1)}, u32[]{:S(2)}, u32[]{:S(2)}) collective-permute-start(bf16[320,1024]{1,0:T(8,128)(2,1)} %pad_maximum_fusion.13.refs_0_), channel_id=1, source_target_pairs={{1,0},{2,1},{3,2},{0,3},{5,4},{6,5},{7,6},{4,7},{9,8},{10,9},{11,1... | collective-permute-start | bytes 1966088 | tf_op jit(solution)/shard_map/ppermute | solution.py:473
  9.7 57.8 %collective-permute-start.1 = (bf16[320,1024]{1,0:T(8,128)(2,1)}, bf16[320,1024]{1,0:T(8,128)(2,1)}, u32[]{:S(2)}, u32[]{:S(2)}) collective-permute-start(bf16[320,1024]{1,0:T(8,128)(2,1)} %pad_maximum_fusion.13.refs_0_), channel_id=1, source_target_pairs={{3,0},{0,1},{1,2},{2,3},{7,4},{4,5},{5,6},{6,7},{11,8},{8,9},{9,10... | collective-permute-start | bytes 1966088 | tf_op jit(solution)/shard_map/ppermute | solution.py:473
  9.7 56.3 %collective-permute-start.2 = (bf16[320,1024]{1,0:T(8,128)(2,1)}, bf16[320,1024]{1,0:T(8,128)(2,1)}, u32[]{:S(2)}, u32[]{:S(2)}) collective-permute-start(bf16[320,1024]{1,0:T(8,128)(2,1)} %pad_maximum_fusion.13.refs_0_), channel_id=1, source_target_pairs={{2,0},{3,1},{0,2},{1,3},{6,4},{7,5},{4,6},{5,7},{10,8},{11,9},{8,1... | collective-permute-start | bytes 1966088 | tf_op jit(solution)/shard_map/ppermute | solution.py:473
  10.7 67.7 %collective-permute-start.3 = (bf16[320,1024]{1,0:T(8,128)(2,1)}, bf16[320,1024]{1,0:T(8,128)(2,1)}, u32[]{:S(2)}, u32[]{:S(2)}) collective-permute-start(bf16[320,1024]{1,0:T(8,128)(2,1)} %pad_maximum_fusion.13.refs_0_), channel_id=1, source_target_pairs={{0,16},{16,0},{1,17},{17,1},{2,18},{18,2},{3,19},{19,3},{4,20},{20... | collective-permute-start | bytes 1966088 | tf_op jit(solution)/shard_map/ppermute | solution.py:481
  14.3 53.7 %all-to-all-start = ((bf16[3,704,256]{2,0,1:T(4,128)(2,1)}), bf16[3,704,256]{2,0,1:T(4,128)(2,1)}, u32[]{:S(2)}, u32[]{:S(2)}) async-start(bf16[3,704,256]{2,0,1:T(4,128)(2,1)} %copy.187), calls=%async_computation | async-start | bytes 2883584 | tf_op jit(solution)/shard_map/all_to_all | solution.py:1049
  40.9 37.6 %collective-permute-start.4 = (bf16[320,1024]{1,0:T(8,128)(2,1)}, bf16[320,1024]{1,0:T(8,128)(2,1)}, u32[]{:S(2)}, u32[]{:S(2)}) collective-permute-start(bf16[320,1024]{1,0:T(8,128)(2,1)} %collective-permute-done.refs_1_), channel_id=1, source_target_pairs={{0,16},{16,0},{1,17},{17,1},{2,18},{18,2},{3,19},{19,3},{4,20},{20... | collective-permute-start | bytes 1966088 | tf_op jit(solution)/shard_map/ppermute | solution.py:481
  67.5 28.5 %collective-permute-start.6 = (bf16[320,1024]{1,0:T(8,128)(2,1)}, bf16[320,1024]{1,0:T(8,128)(2,1)}, u32[]{:S(2)}, u32[]{:S(2)}) collective-permute-start(bf16[320,1024]{1,0:T(8,128)(2,1)} %collective-permute-done.1.refs_3_), channel_id=1, source_target_pairs={{0,16},{16,0},{1,17},{17,1},{2,18},{18,2},{3,19},{19,3},{4,20},{20... | collective-permute-start | bytes 1966088 | tf_op jit(solution)/shard_map/ppermute | solution.py:481
  110.7 42.4 %collective-permute-start.12 = (bf16[256,512]{1,0:T(8,128)(2,1)}, bf16[256,512]{1,0:T(8,128)(2,1)}, u32[]{:S(2)}, u32[]{:S(2)}) collective-permute-start(bf16[256,512]{1,0:T(8,128)(2,1)} %bitcast.29.refs_0_), channel_id=1, source_target_pairs={{0,16},{16,0},{1,17},{17,1},{2,18},{18,2},{3,19},{19,3},{4,20},{20... | collective-permute-start | bytes 786440 | tf_op jit(solution)/shard_map/ppermute | solution.py:481
  116.7 36.3 %collective-permute-start.13 = (bf16[256,512]{1,0:T(8,128)(2,1)}, bf16[256,512]{1,0:T(8,128)(2,1)}, u32[]{:S(2)}, u32[]{:S(2)}) collective-permute-start(bf16[256,512]{1,0:T(8,128)(2,1)} %collective-permute-done.9.refs_1_), channel_id=1, source_target_pairs={{0,16},{16,0},{1,17},{17,1},{2,18},{18,2},{3,19},{19,3},{4,20},{20... | collective-permute-start | bytes 786440 | tf_op jit(solution)/shard_map/ppermute | solution.py:481
  162.7 42.5 %collective-permute-start.66 = (bf16[128,2176]{1,0:T(8,128)(2,1)S(1)}, bf16[128,2176]{1,0:T(8,128)(2,1)}, u32[]{:S(2)}, u32[]{:S(2)}) collective-permute-start(bf16[128,2176]{1,0:T(8,128)(2,1)S(1)} %pad_maximum_fusion.18.refs_8_.refs_3_.refs_30_), channel_id=1, source_target_pairs={{2,0},{3,1},{0,2},{1,3},{6,4},{7,5},{4,6},{5,7},{10,8},{11,9},{8,1... | collective-permute-start | bytes 1671176 | tf_op jit(solution)/shard_map/ppermute | solution.py:473
  165.1 38.5 %collective-permute-start.44 = (bf16[128,2176]{1,0:T(8,128)(2,1)S(1)}, bf16[128,2176]{1,0:T(8,128)(2,1)}, u32[]{:S(2)}, u32[]{:S(2)}) collective-permute-start(bf16[128,2176]{1,0:T(8,128)(2,1)S(1)} %pad_maximum_fusion.18.refs_8_.refs_3_.refs_30_), channel_id=1, source_target_pairs={{1,0},{2,1},{3,2},{0,3},{5,4},{6,5},{7,6},{4,7},{9,8},{10,9},{11,1... | collective-permute-start | bytes 1671176 | tf_op jit(solution)/shard_map/ppermute | solution.py:473
  165.6 39.7 %collective-permute-start.45 = (bf16[128,2176]{1,0:T(8,128)(2,1)S(1)}, bf16[128,2176]{1,0:T(8,128)(2,1)}, u32[]{:S(2)}, u32[]{:S(2)}) collective-permute-start(bf16[128,2176]{1,0:T(8,128)(2,1)S(1)} %pad_maximum_fusion.18.refs_8_.refs_3_.refs_30_), channel_id=1, source_target_pairs={{3,0},{0,1},{1,2},{2,3},{7,4},{4,5},{5,6},{6,7},{11,8},{8,9},{9,10... | collective-permute-start | bytes 1671176 | tf_op jit(solution)/shard_map/ppermute | solution.py:473
  167.3 51.8 %collective-permute-start.25 = (bf16[128,2176]{1,0:T(8,128)(2,1)S(1)}, bf16[128,2176]{1,0:T(8,128)(2,1)}, u32[]{:S(2)}, u32[]{:S(2)}) collective-permute-start(bf16[128,2176]{1,0:T(8,128)(2,1)S(1)} %pad_maximum_fusion.18.refs_8_.refs_3_.refs_30_), channel_id=1, source_target_pairs={{0,16},{4,12},{8,24},{12,4},{16,0},{20,28},{24,8},{28,20},{1,17},{... | collective-permute-start | bytes 1671176 | tf_op jit(solution)/shard_map/ppermute | solution.py:494
  167.8 51.4 %collective-permute-start.26 = (bf16[128,2176]{1,0:T(8,128)(2,1)S(1)}, bf16[128,2176]{1,0:T(8,128)(2,1)S(1)}, u32[]{:S(2)}, u32[]{:S(2)}) collective-permute-start(bf16[128,2176]{1,0:T(8,128)(2,1)S(1)} %pad_maximum_fusion.18.refs_8_.refs_3_.refs_30_), channel_id=1, source_target_pairs={{0,8},{4,20},{8,0},{12,28},{16,24},{20,4},{24,16},{28,12},{1,9},{5... | collective-permute-start | bytes 1671176 | tf_op jit(solution)/shard_map/ppermute | solution.py:494
  230.7 27.4 %collective-permute-start.46 = (bf16[256,2176]{1,0:T(8,128)(2,1)S(1)}, bf16[256,2176]{1,0:T(8,128)(2,1)S(1)}, u32[]{:S(2)}, u32[]{:S(2)}) collective-permute-start(bf16[256,2176]{1,0:T(8,128)(2,1)S(1)} %constant_dynamic-update-slice_fusion.3.refs_8_.refs_11_.refs_38_), channel_id=1, source_target_pairs={{0,16},{4,12},{8,24},{12,4},{16,0},{20,28},{24,8},{28,20},{1,17},{... | collective-permute-start | bytes 3342344 | tf_op jit(solution)/shard_map/ppermute | solution.py:494
  243.1 34.6 %collective-permute-start.49 = (bf16[256,2176]{1,0:T(8,128)(2,1)S(1)}, bf16[256,2176]{1,0:T(8,128)(2,1)S(1)}, u32[]{:S(2)}, u32[]{:S(2)}) collective-permute-start(bf16[256,2176]{1,0:T(8,128)(2,1)S(1)} %constant_dynamic-update-slice_fusion.3.refs_8_.refs_11_.refs_38_), channel_id=1, source_target_pairs={{0,4},{4,0},{8,12},{12,8},{1,5},{5,1},{9,13},{13,9},{2,6},{6,2},{1... | collective-permute-start | bytes 3342344 | tf_op jit(solution)/shard_map/ppermute | solution.py:485
  252.7 25.6 %collective-permute-start.35 = (bf16[128,2048]{1,0:T(8,128)(2,1)S(1)}, bf16[128,2048]{1,0:T(8,128)(2,1)S(1)}, u32[]{:S(2)}, u32[]{:S(2)}) collective-permute-start(bf16[128,2048]{1,0:T(8,128)(2,1)S(1)} %multiply_convert_fusion.2.refs_0_.refs_3_), channel_id=1, source_target_pairs={{1,0},{2,1},{3,2},{0,3},{5,4},{6,5},{7,6},{4,7},{9,8},{10,9},{11,1... | collective-permute-start | bytes 1572872 | tf_op jit(solution)/shard_map/ppermute | solution.py:473
  258.1 33.6 %collective-permute-start.48 = (bf16[256,2176]{1,0:T(8,128)(2,1)S(1)}, bf16[256,2176]{1,0:T(8,128)(2,1)}, u32[]{:S(2)}, u32[]{:S(2)}) collective-permute-start(bf16[256,2176]{1,0:T(8,128)(2,1)S(1)} %collective-permute-done.46.refs_9_.refs_12_.refs_39_), channel_id=1, source_target_pairs={{0,8},{4,20},{8,0},{12,28},{16,24},{20,4},{24,16},{28,12},{1,9},{5... | collective-permute-start | bytes 3342344 | tf_op jit(solution)/shard_map/ppermute | solution.py:494
  264.5 25.1 %collective-permute-start.36 = (bf16[128,2048]{1,0:T(8,128)(2,1)S(1)}, bf16[128,2048]{1,0:T(8,128)(2,1)S(1)}, u32[]{:S(2)}, u32[]{:S(2)}) collective-permute-start(bf16[128,2048]{1,0:T(8,128)(2,1)S(1)} %multiply_convert_fusion.2.refs_0_.refs_3_), channel_id=1, source_target_pairs={{3,0},{0,1},{1,2},{2,3},{7,4},{4,5},{5,6},{6,7},{11,8},{8,9},{9,10... | collective-permute-start | bytes 1572872 | tf_op jit(solution)/shard_map/ppermute | solution.py:473
  278.4 35.2 %collective-permute-start.58 = (bf16[128,2048]{1,0:T(8,128)(2,1)S(1)}, bf16[128,2048]{1,0:T(8,128)(2,1)}, u32[]{:S(2)}, u32[]{:S(2)}) collective-permute-start(bf16[128,2048]{1,0:T(8,128)(2,1)S(1)} %multiply_convert_fusion.2.refs_0_.refs_3_), channel_id=1, source_target_pairs={{2,0},{3,1},{0,2},{1,3},{6,4},{7,5},{4,6},{5,7},{10,8},{11,9},{8,1... | collective-permute-start | bytes 1572872 | tf_op jit(solution)/shard_map/ppermute | solution.py:473
  290.1 24.8 %collective-permute-start.20 = (bf16[128,2048]{1,0:T(8,128)(2,1)S(1)}, bf16[128,2048]{1,0:T(8,128)(2,1)}, u32[]{:S(2)}, u32[]{:S(2)}) collective-permute-start(bf16[128,2048]{1,0:T(8,128)(2,1)S(1)} %collective-permute-done.18.refs_1_.refs_4_), channel_id=1, source_target_pairs={{0,8},{4,20},{8,0},{12,28},{16,24},{20,4},{24,16},{28,12},{1,9},{5... | collective-permute-start | bytes 1572872 | tf_op jit(solution)/shard_map/ppermute | solution.py:494
  291.7 26.1 %collective-permute-start.37 = (bf16[256,2048]{1,0:T(8,128)(2,1)S(1)}, bf16[256,2048]{1,0:T(8,128)(2,1)}, u32[]{:S(2)}, u32[]{:S(2)}) collective-permute-start(bf16[256,2048]{1,0:T(8,128)(2,1)S(1)} %constant_dynamic-update-slice_fusion.1.refs_0_.refs_11_), channel_id=1, source_target_pairs={{0,16},{4,12},{8,24},{12,4},{16,0},{20,28},{24,8},{28,20},{1,17},{... | collective-permute-start | bytes 3145736 | tf_op jit(solution)/shard_map/ppermute | solution.py:494
  315.7 33.8 %collective-permute-start.51 = (bf16[256,2176]{1,0:T(8,128)(2,1)}, bf16[256,2176]{1,0:T(8,128)(2,1)}, u32[]{:S(2)}, u32[]{:S(2)}) collective-permute-start(bf16[256,2176]{1,0:T(8,128)(2,1)} %collective-permute-done.47.refs_10_.refs_13_.refs_40_), channel_id=1, source_target_pairs={{0,4},{4,0},{8,12},{12,8},{1,5},{5,1},{9,13},{13,9},{2,6},{6,2},{1... | collective-permute-start | bytes 3342344 | tf_op jit(solution)/shard_map/ppermute | solution.py:485
  316.1 33.5 %collective-permute-start.52 = (bf16[256,2176]{1,0:T(8,128)(2,1)}, bf16[256,2176]{1,0:T(8,128)(2,1)}, u32[]{:S(2)}, u32[]{:S(2)}) collective-permute-start(bf16[256,2176]{1,0:T(8,128)(2,1)} %collective-permute-done.48.refs_11_.refs_14_.refs_41_), channel_id=1, source_target_pairs={{0,4},{4,0},{8,12},{12,8},{1,5},{5,1},{9,13},{13,9},{2,6},{6,2},{1... | collective-permute-start | bytes 3342344 | tf_op jit(solution)/shard_map/ppermute | solution.py:485
  316.4 35.0 %collective-permute-start.38 = (bf16[256,2048]{1,0:T(8,128)(2,1)S(1)}, bf16[256,2048]{1,0:T(8,128)(2,1)}, u32[]{:S(2)}, u32[]{:S(2)}) collective-permute-start(bf16[256,2048]{1,0:T(8,128)(2,1)S(1)} %constant_dynamic-update-slice_fusion.1.refs_0_.refs_11_), channel_id=1, source_target_pairs={{0,8},{4,20},{8,0},{12,28},{16,24},{20,4},{24,16},{28,12},{1,9},{5... | collective-permute-start | bytes 3145736 | tf_op jit(solution)/shard_map/ppermute | solution.py:494
  317.3 33.3 %collective-permute-start.59 = (bf16[128,2048]{1,0:T(8,128)(2,1)}, bf16[128,2048]{1,0:T(8,128)(2,1)}, u32[]{:S(2)}, u32[]{:S(2)}) collective-permute-start(bf16[128,2048]{1,0:T(8,128)(2,1)} %collective-permute-done.58.refs_0_.refs_19_), channel_id=1, source_target_pairs={{0,16},{4,12},{8,24},{12,4},{16,0},{20,28},{24,8},{28,20},{1,17},{... | collective-permute-start | bytes 1572872 | tf_op jit(solution)/shard_map/ppermute | solution.py:494
  317.8 33.6 %collective-permute-start.39 = (bf16[256,2048]{1,0:T(8,128)(2,1)}, bf16[256,2048]{1,0:T(8,128)(2,1)}, u32[]{:S(2)}, u32[]{:S(2)}) collective-permute-start(bf16[256,2048]{1,0:T(8,128)(2,1)} %collective-permute-done.37.refs_1_.refs_12_), channel_id=1, source_target_pairs={{0,8},{4,20},{8,0},{12,28},{16,24},{20,4},{24,16},{28,12},{1,9},{5... | collective-permute-start | bytes 3145736 | tf_op jit(solution)/shard_map/ppermute | solution.py:494
  368.7 53.2 %collective-permute-start.73 = (bf16[128,2176]{1,0:T(8,128)(2,1)S(1)}, bf16[128,2176]{1,0:T(8,128)(2,1)S(1)}, u32[]{:S(2)}, u32[]{:S(2)}) collective-permute-start(bf16[128,2176]{1,0:T(8,128)(2,1)S(1)} %copy-done.74), channel_id=1, source_target_pairs={{0,4},{4,0},{8,12},{12,8},{1,5},{5,1},{9,13},{13,9},{2,6},{6,2},{1... | collective-permute-start | bytes 1671176 | tf_op jit(solution)/shard_map/ppermute | solution.py:485
  369.7 52.7 %collective-permute-start.62 = (bf16[128,2048]{1,0:T(8,128)(2,1)}, bf16[128,2048]{1,0:T(8,128)(2,1)}, u32[]{:S(2)}, u32[]{:S(2)}) collective-permute-start(bf16[128,2048]{1,0:T(8,128)(2,1)} %collective-permute-done.58.refs_0_.refs_19_), channel_id=1, source_target_pairs={{0,4},{4,0},{8,12},{12,8},{1,5},{5,1},{9,13},{13,9},{2,6},{6,2},{1... | collective-permute-start | bytes 1572872 | tf_op jit(solution)/shard_map/ppermute | solution.py:485
  370.2 52.9 %collective-permute-start.63 = (bf16[128,2048]{1,0:T(8,128)(2,1)}, bf16[128,2048]{1,0:T(8,128)(2,1)}, u32[]{:S(2)}, u32[]{:S(2)}) collective-permute-start(bf16[128,2048]{1,0:T(8,128)(2,1)} %collective-permute-done.59.refs_1_.refs_20_), channel_id=1, source_target_pairs={{0,4},{4,0},{8,12},{12,8},{1,5},{5,1},{9,13},{13,9},{2,6},{6,2},{1... | collective-permute-start | bytes 1572872 | tf_op jit(solution)/shard_map/ppermute | solution.py:485
  370.2 52.9 %collective-permute-start.64 = (bf16[128,2048]{1,0:T(8,128)(2,1)}, bf16[128,2048]{1,0:T(8,128)(2,1)}, u32[]{:S(2)}, u32[]{:S(2)}) collective-permute-start(bf16[128,2048]{1,0:T(8,128)(2,1)} %collective-permute-done.60.refs_2_.refs_21_), channel_id=1, source_target_pairs={{0,4},{4,0},{8,12},{12,8},{1,5},{5,1},{9,13},{13,9},{2,6},{6,2},{1... | collective-permute-start | bytes 1572872 | tf_op jit(solution)/shard_map/ppermute | solution.py:485
  370.7 52.4 %collective-permute-start.65 = (bf16[128,2048]{1,0:T(8,128)(2,1)}, bf16[128,2048]{1,0:T(8,128)(2,1)}, u32[]{:S(2)}, u32[]{:S(2)}) collective-permute-start(bf16[128,2048]{1,0:T(8,128)(2,1)} %collective-permute-done.61.refs_3_.refs_22_), channel_id=1, source_target_pairs={{0,4},{4,0},{8,12},{12,8},{1,5},{5,1},{9,13},{13,9},{2,6},{6,2},{1... | collective-permute-start | bytes 1572872 | tf_op jit(solution)/shard_map/ppermute | solution.py:485
  421.8 40.8 %collective-permute-start.32 = (bf16[512,2048]{1,0:T(8,128)(2,1)}, bf16[512,2048]{1,0:T(8,128)(2,1)S(1)}, u32[]{:S(2)}, u32[]{:S(2)}) collective-permute-start(bf16[512,2048]{1,0:T(8,128)(2,1)} %get-tuple-element.64), channel_id=1, source_target_pairs={{0,4},{4,0},{8,12},{12,8},{1,5},{5,1},{9,13},{13,9},{2,6},{6,2},{1... | collective-permute-start | bytes 6291464 | tf_op jit(solution)/shard_map/ppermute | solution.py:485
  422.6 63.0 %collective-permute-start.53 = (bf16[1024,2048]{1,0:T(8,128)(2,1)}, bf16[1024,2048]{1,0:T(8,128)(2,1)}, u32[]{:S(2)}, u32[]{:S(2)}) collective-permute-start(bf16[1024,2048]{1,0:T(8,128)(2,1)} %get-tuple-element.66), channel_id=1, source_target_pairs={{0,4},{4,0},{8,12},{12,8},{1,5},{5,1},{9,13},{13,9},{2,6},{6,2},{1... | collective-permute-start | bytes 12582920 | tf_op jit(solution)/shard_map/ppermute | solution.py:485
  453.8 36.9 %collective-permute-start.74 = (bf16[512,2048]{1,0:T(8,128)(2,1)}, bf16[512,2048]{1,0:T(8,128)(2,1)}, u32[]{:S(2)}, u32[]{:S(2)}) collective-permute-start(bf16[512,2048]{1,0:T(8,128)(2,1)} %get-tuple-element.68), channel_id=1, source_target_pairs={{0,4},{4,0},{8,12},{12,8},{1,5},{5,1},{9,13},{13,9},{2,6},{6,2},{1... | collective-permute-start | bytes 6291464 | tf_op jit(solution)/shard_map/ppermute | solution.py:485
  464.3 90.6 %collective-permute-start.33 = (bf16[256,2048]{1,0:T(8,128)(2,1)}, bf16[256,2048]{1,0:T(8,128)(2,1)}, u32[]{:S(2)}, u32[]{:S(2)}) collective-permute-start(bf16[256,2048]{1,0:T(8,128)(2,1)} %add_convert_fusion.9), channel_id=1, source_target_pairs={{0,8},{4,20},{8,0},{12,28},{16,24},{20,4},{24,16},{28,12},{1,9},{5... | collective-permute-start | bytes 3145736 | tf_op jit(solution)/shard_map/ppermute | solution.py:494
  489.6 41.5 %collective-permute-start.54 = (bf16[512,2048]{1,0:T(8,128)(2,1)}, bf16[512,2048]{1,0:T(8,128)(2,1)}, u32[]{:S(2)}, u32[]{:S(2)}) collective-permute-start(bf16[512,2048]{1,0:T(8,128)(2,1)} %add_convert_fusion.1), channel_id=1, source_target_pairs={{0,8},{4,20},{8,0},{12,28},{16,24},{20,4},{24,16},{28,12},{1,9},{5... | collective-permute-start | bytes 6291464 | tf_op jit(solution)/shard_map/ppermute | solution.py:494
  492.3 34.9 %collective-permute-start.75 = (bf16[256,2048]{1,0:T(8,128)(2,1)S(1)}, bf16[256,2048]{1,0:T(8,128)(2,1)}, u32[]{:S(2)}, u32[]{:S(2)}) collective-permute-start(bf16[256,2048]{1,0:T(8,128)(2,1)S(1)} %add_convert_fusion.6), channel_id=1, source_target_pairs={{0,8},{4,20},{8,0},{12,28},{16,24},{20,4},{24,16},{28,12},{1,9},{5... | collective-permute-start | bytes 3145736 | tf_op jit(solution)/shard_map/ppermute | solution.py:494
  529.6 28.5 %collective-permute-start.76 = (bf16[128,2048]{1,0:T(8,128)(2,1)}, bf16[128,2048]{1,0:T(8,128)(2,1)}, u32[]{:S(2)}, u32[]{:S(2)}) collective-permute-start(bf16[128,2048]{1,0:T(8,128)(2,1)} %add_convert_fusion.19), channel_id=1, source_target_pairs={{0,16},{4,12},{8,24},{12,4},{16,0},{20,28},{24,8},{28,20},{1,17},{... | collective-permute-start | bytes 1572872 | tf_op jit(solution)/shard_map/ppermute | solution.py:494
  534.2 26.0 %collective-permute-start.55 = (bf16[256,2048]{1,0:T(8,128)(2,1)}, bf16[256,2048]{1,0:T(8,128)(2,1)S(1)}, u32[]{:S(2)}, u32[]{:S(2)}) collective-permute-start(bf16[256,2048]{1,0:T(8,128)(2,1)} %add_convert_fusion.8), channel_id=1, source_target_pairs={{0,16},{4,12},{8,24},{12,4},{16,0},{20,28},{24,8},{28,20},{1,17},{... | collective-permute-start | bytes 3145736 | tf_op jit(solution)/shard_map/ppermute | solution.py:494
  560.0 27.5 %collective-permute-start.77 = (bf16[128,2048]{1,0:T(8,128)(2,1)S(1)}, bf16[128,2048]{1,0:T(8,128)(2,1)S(1)}, u32[]{:S(2)}, u32[]{:S(2)}) collective-permute-start(bf16[128,2048]{1,0:T(8,128)(2,1)S(1)} %add_convert_fusion.18), channel_id=1, source_target_pairs={{0,2},{1,3},{2,0},{3,1},{4,6},{5,7},{6,4},{7,5},{8,10},{9,11},{10,... | collective-permute-start | bytes 1572872 | tf_op jit(solution)/shard_map/ppermute | solution.py:477
  562.7 35.8 %collective-permute-start.57 = (bf16[128,2048]{1,0:T(8,128)(2,1)S(1)}, bf16[128,2048]{1,0:T(8,128)(2,1)S(1)}, u32[]{:S(2)}, u32[]{:S(2)}) collective-permute-start(bf16[128,2048]{1,0:T(8,128)(2,1)S(1)} %get-tuple-element.240), channel_id=1, source_target_pairs={{0,3},{1,0},{2,1},{3,2},{4,7},{5,4},{6,5},{7,6},{8,11},{9,8},{10,9... | collective-permute-start | bytes 1572872 | tf_op jit(solution)/shard_map/ppermute | solution.py:477
  566.1 32.4 %collective-permute-start.56 = (bf16[128,2048]{1,0:T(8,128)(2,1)S(1)}, bf16[128,2048]{1,0:T(8,128)(2,1)S(1)}, u32[]{:S(2)}, u32[]{:S(2)}) collective-permute-start(bf16[128,2048]{1,0:T(8,128)(2,1)S(1)} %get-tuple-element.239), channel_id=1, source_target_pairs={{0,1},{1,2},{2,3},{3,0},{4,5},{5,6},{6,7},{7,4},{8,9},{9,10},{10,1... | collective-permute-start | bytes 1572872 | tf_op jit(solution)/shard_map/ppermute | solution.py:477
  662.6 59.2 %all-to-all-start.1 = ((bf16[8,264,256]{2,1,0:T(8,128)(2,1)}), bf16[8,264,256]{2,1,0:T(8,128)(2,1)}, u32[]{:S(2)}, u32[]{:S(2)}) async-start(bf16[8,264,256]{2,1,0:T(8,128)(2,1)} %shard_map.298), calls=%async_computation.1 | async-start | bytes 2162688 | tf_op jit(solution)/shard_map/all_to_all | solution.py:1228
  675.5 146.4 %collective-permute-start.83 = (bf16[1024,2048]{1,0:T(8,128)(2,1)}, bf16[1024,2048]{1,0:T(8,128)(2,1)}, u32[]{:S(2)}, u32[]{:S(2)}) collective-permute-start(bf16[1024,2048]{1,0:T(8,128)(2,1)} %convolution_convert_fusion), channel_id=1, source_target_pairs={{0,4},{4,0},{8,12},{12,8},{1,5},{5,1},{9,13},{13,9},{2,6},{6,2},{1... | collective-permute-start | bytes 12582920 | tf_op jit(solution)/shard_map/ppermute | solution.py:485
  676.0 41.1 %collective-permute-start.116 = (bf16[256,512]{1,0:T(8,128)(2,1)}, bf16[256,512]{1,0:T(8,128)(2,1)S(1)}, u32[]{:S(2)}, u32[]{:S(2)}) collective-permute-start(bf16[256,512]{1,0:T(8,128)(2,1)} %get-tuple-element.206), channel_id=1, source_target_pairs={{0,16},{16,0},{1,17},{17,1},{2,18},{18,2},{3,19},{19,3},{4,20},{20... | collective-permute-start | bytes 786440 | tf_op jit(solution)/shard_map/ppermute | solution.py:481
  682.4 34.7 %collective-permute-start.122 = (bf16[256,512]{1,0:T(8,128)(2,1)S(1)}, bf16[256,512]{1,0:T(8,128)(2,1)S(1)}, u32[]{:S(2)}, u32[]{:S(2)}) collective-permute-start(bf16[256,512]{1,0:T(8,128)(2,1)S(1)} %get-tuple-element.211), channel_id=1, source_target_pairs={{0,2},{1,3},{2,0},{3,1},{4,6},{5,7},{6,4},{7,5},{8,10},{9,11},{10,... | collective-permute-start | bytes 786440 | tf_op jit(solution)/shard_map/ppermute | solution.py:477
  717.1 47.4 %collective-permute-start.96 = (bf16[256,2048]{1,0:T(8,128)(2,1)S(1)}, bf16[256,2048]{1,0:T(8,128)(2,1)}, u32[]{:S(2)}, u32[]{:S(2)}) collective-permute-start(bf16[256,2048]{1,0:T(8,128)(2,1)S(1)} %fusion.7), channel_id=1, source_target_pairs={{0,4},{4,0},{8,12},{12,8},{1,5},{5,1},{9,13},{13,9},{2,6},{6,2},{1... | collective-permute-start | bytes 3145736 | tf_op jit(solution)/shard_map/ppermute | solution.py:485
  717.6 31.5 %collective-permute-start.103 = (bf16[320,1024]{1,0:T(8,128)(2,1)}, bf16[320,1024]{1,0:T(8,128)(2,1)}, u32[]{:S(2)}, u32[]{:S(2)}) collective-permute-start(bf16[320,1024]{1,0:T(8,128)(2,1)} %get-tuple-element.84), channel_id=1, source_target_pairs={{0,16},{16,0},{1,17},{17,1},{2,18},{18,2},{3,19},{19,3},{4,20},{20... | collective-permute-start | bytes 1966088 | tf_op jit(solution)/shard_map/ppermute | solution.py:481
  719.2 44.0 %collective-permute-start.101 = (bf16[320,1024]{1,0:T(8,128)(2,1)}, bf16[320,1024]{1,0:T(8,128)(2,1)}, u32[]{:S(2)}, u32[]{:S(2)}) collective-permute-start(bf16[320,1024]{1,0:T(8,128)(2,1)} %get-tuple-element.82), channel_id=1, source_target_pairs={{0,16},{16,0},{1,17},{17,1},{2,18},{18,2},{3,19},{19,3},{4,20},{20... | collective-permute-start | bytes 1966088 | tf_op jit(solution)/shard_map/ppermute | solution.py:481
  735.1 41.5 %collective-permute-start.100 = (bf16[320,1024]{1,0:T(8,128)(2,1)}, bf16[320,1024]{1,0:T(8,128)(2,1)S(1)}, u32[]{:S(2)}, u32[]{:S(2)}) collective-permute-start(bf16[320,1024]{1,0:T(8,128)(2,1)} %get-tuple-element.80), channel_id=1, source_target_pairs={{0,16},{16,0},{1,17},{17,1},{2,18},{18,2},{3,19},{19,3},{4,20},{20... | collective-permute-start | bytes 1966088 | tf_op jit(solution)/shard_map/ppermute | solution.py:481
  749.2 32.7 %collective-permute-start.106 = (bf16[320,1024]{1,0:T(8,128)(2,1)S(1)}, bf16[320,1024]{1,0:T(8,128)(2,1)S(1)}, u32[]{:S(2)}, u32[]{:S(2)}) collective-permute-start(bf16[320,1024]{1,0:T(8,128)(2,1)S(1)} %add_convert_fusion.10), channel_id=1, source_target_pairs={{0,2},{1,3},{2,0},{3,1},{4,6},{5,7},{6,4},{7,5},{8,10},{9,11},{10,... | collective-permute-start | bytes 1966088 | tf_op jit(solution)/shard_map/ppermute | solution.py:477
  763.2 43.2 %collective-permute-start.104 = (bf16[320,1024]{1,0:T(8,128)(2,1)S(1)}, bf16[320,1024]{1,0:T(8,128)(2,1)S(1)}, u32[]{:S(2)}, u32[]{:S(2)}) collective-permute-start(bf16[320,1024]{1,0:T(8,128)(2,1)S(1)} %add_convert_fusion.11), channel_id=1, source_target_pairs={{0,3},{1,0},{2,1},{3,2},{4,7},{5,4},{6,5},{7,6},{8,11},{9,8},{10,9... | collective-permute-start | bytes 1966088 | tf_op jit(solution)/shard_map/ppermute | solution.py:477
  764.5 41.8 %collective-permute-start.102 = (bf16[320,1024]{1,0:T(8,128)(2,1)S(1)}, bf16[320,1024]{1,0:T(8,128)(2,1)S(1)}, u32[]{:S(2)}, u32[]{:S(2)}) collective-permute-start(bf16[320,1024]{1,0:T(8,128)(2,1)S(1)} %add_convert_fusion.12), channel_id=1, source_target_pairs={{0,1},{1,2},{2,3},{3,0},{4,5},{5,6},{6,7},{7,4},{8,9},{9,10},{10,1... | collective-permute-start | bytes 1966088 | tf_op jit(solution)/shard_map/ppermute | solution.py:477
  776.6 32.1 %collective-permute-start.97 = (bf16[128,2048]{1,0:T(8,128)(2,1)S(1)}, bf16[128,2048]{1,0:T(8,128)(2,1)S(1)}, u32[]{:S(2)}, u32[]{:S(2)}) collective-permute-start(bf16[128,2048]{1,0:T(8,128)(2,1)S(1)} %slice.644), channel_id=1, source_target_pairs={{0,8},{4,12},{8,0},{12,4},{1,9},{5,13},{9,1},{13,5},{2,10},{6,14},... | collective-permute-start | bytes 1572872 | tf_op jit(solution)/shard_map/ppermute | solution.py:485
  781.9 44.4 %collective-permute-start.88 = (bf16[512,2048]{1,0:T(8,128)(2,1)}, bf16[512,2048]{1,0:T(8,128)(2,1)}, u32[]{:S(2)}, u32[]{:S(2)}) collective-permute-start(bf16[512,2048]{1,0:T(8,128)(2,1)} %convolution_convert_fusion.2), channel_id=1, source_target_pairs={{0,4},{4,0},{8,12},{12,8},{1,5},{5,1},{9,13},{13,9},{2,6},{6,2},{1... | collective-permute-start | bytes 6291464 | tf_op jit(solution)/shard_map/ppermute | solution.py:485
  806.4 33.3 %collective-permute-start.80 = (bf16[512,2048]{1,0:T(8,128)(2,1)}, bf16[512,2048]{1,0:T(8,128)(2,1)}, u32[]{:S(2)}, u32[]{:S(2)}) collective-permute-start(bf16[512,2048]{1,0:T(8,128)(2,1)} %convolution_convert_fusion.4), channel_id=1, source_target_pairs={{0,4},{4,0},{8,12},{12,8},{1,5},{5,1},{9,13},{13,9},{2,6},{6,2},{1... | collective-permute-start | bytes 6291464 | tf_op jit(solution)/shard_map/ppermute | solution.py:485
  826.3 39.5 %collective-permute-start.84 = (bf16[512,2048]{1,0:T(8,128)(2,1)S(1)}, bf16[512,2048]{1,0:T(8,128)(2,1)}, u32[]{:S(2)}, u32[]{:S(2)}) collective-permute-start(bf16[512,2048]{1,0:T(8,128)(2,1)S(1)} %add_convert_fusion), channel_id=1, source_target_pairs={{0,8},{4,20},{8,0},{12,28},{16,24},{20,4},{24,16},{28,12},{1,9},{5... | collective-permute-start | bytes 6291464 | tf_op jit(solution)/shard_map/ppermute | solution.py:494
  830.1 33.6 %collective-permute-start.89 = (bf16[256,2048]{1,0:T(8,128)(2,1)}, bf16[256,2048]{1,0:T(8,128)(2,1)}, u32[]{:S(2)}, u32[]{:S(2)}) collective-permute-start(bf16[256,2048]{1,0:T(8,128)(2,1)} %add_convert_fusion.2), channel_id=1, source_target_pairs={{0,8},{4,20},{8,0},{12,28},{16,24},{20,4},{24,16},{28,12},{1,9},{5... | collective-permute-start | bytes 3145736 | tf_op jit(solution)/shard_map/ppermute | solution.py:494
  841.8 42.6 %collective-permute-start.81 = (bf16[256,2048]{1,0:T(8,128)(2,1)S(1)}, bf16[256,2048]{1,0:T(8,128)(2,1)S(1)}, u32[]{:S(2)}, u32[]{:S(2)}) collective-permute-start(bf16[256,2048]{1,0:T(8,128)(2,1)S(1)} %add_convert_fusion.5), channel_id=1, source_target_pairs={{0,8},{4,20},{8,0},{12,28},{16,24},{20,4},{24,16},{28,12},{1,9},{5... | collective-permute-start | bytes 3145736 | tf_op jit(solution)/shard_map/ppermute | solution.py:494
  869.6 28.9 %collective-permute-start.114 = (bf16[260,144]{1,0:T(8,128)(2,1)S(1)}, bf16[260,144]{1,0:T(8,128)(2,1)S(1)}, u32[]{:S(2)}, u32[]{:S(2)}) collective-permute-start(bf16[260,144]{1,0:T(8,128)(2,1)S(1)} %pad_maximum_fusion.26), channel_id=1, source_target_pairs={{0,8},{4,12},{8,0},{12,4},{1,9},{5,13},{9,1},{13,5},{2,10},{6,14},... | collective-permute-start | bytes 224648 | tf_op jit(solution)/shard_map/ppermute | solution.py:485
  894.5 31.6 %collective-permute-start.87 = (bf16[128,2048]{1,0:T(8,128)(2,1)}, bf16[128,2048]{1,0:T(8,128)(2,1)}, u32[]{:S(2)}, u32[]{:S(2)}) collective-permute-start(bf16[128,2048]{1,0:T(8,128)(2,1)} %get-tuple-element.238), channel_id=1, source_target_pairs={{0,3},{1,0},{2,1},{3,2},{4,7},{5,4},{6,5},{7,6},{8,11},{9,8},{10,9... | collective-permute-start | bytes 1572872 | tf_op jit(solution)/shard_map/ppermute | solution.py:477
  897.0 29.1 %collective-permute-start.86 = (bf16[128,2048]{1,0:T(8,128)(2,1)}, bf16[128,2048]{1,0:T(8,128)(2,1)}, u32[]{:S(2)}, u32[]{:S(2)}) collective-permute-start(bf16[128,2048]{1,0:T(8,128)(2,1)} %get-tuple-element.237), channel_id=1, source_target_pairs={{0,1},{1,2},{2,3},{3,0},{4,5},{5,6},{6,7},{7,4},{8,9},{9,10},{10,1... | collective-permute-start | bytes 1572872 | tf_op jit(solution)/shard_map/ppermute | solution.py:477
  904.1 27.0 %collective-permute-start.98 = (bf16[128,2048]{1,0:T(8,128)(2,1)}, bf16[128,2048]{1,0:T(8,128)(2,1)}, u32[]{:S(2)}, u32[]{:S(2)}) collective-permute-start(bf16[128,2048]{1,0:T(8,128)(2,1)} %constant_dynamic-update-slice_fusion.5), channel_id=1, source_target_pairs={{0,8},{4,12},{8,0},{12,4},{1,9},{5,13},{9,1},{13,5},{2,10},{6,14},... | collective-permute-start | bytes 1572872 | tf_op jit(solution)/shard_map/ppermute | solution.py:485
  (185 other events, 2772.4 us)
where the time goes:
time: 961 us; the launch traced here: 952 us
  waiting for transfers between devices  348 us (36%)
  Pallas kernels  208 us (22%)
  starting transfers between devices  154 us (16%)
  other arithmetic  98.5 us (10%)
  local copies, waits for them, and re-layouts  84.2 us (9%)
  matrix products  56.1 us (6%)
    pallas_call x3, Pallas kernels, hidden_step(): pl.pallas_call(hidden_kernel, out_shape=(row_shape, row_shape) + tuple((j...  112 us
    ppermute x12, waiting for transfers between devices, from_tensor(): return lax.ppermute(array, TENSOR, [((i + k) % 4, i) for i in range(4)])  93.2 us
    ppermute x30, waiting for transfers between devices, swap_plane(): return lax.ppermute(array, PLANE, pairs)  92.6 us
    ppermute x15, waiting for transfers between devices, to_tensor(): return lax.ppermute(array, TENSOR, [(i, (i + k) % 4) for i in range(4)])  75.4 us
    ppermute x20, waiting for transfers between devices, swap_fsdp(): return lax.ppermute(array, FSDP, [(0, 1), (1, 0)])  61.8 us
    pallas_call x3, Pallas kernels, weight_grad(): pl.pallas_call(kernel, out_shape=jax.ShapeDtypeStruct(shape, dtype), in_s...  61 us
    ppermute x12, starting transfers between devices, from_tensor(): return lax.ppermute(array, TENSOR, [((i + k) % 4, i) for i in range(4)])  38.6 us
    ppermute x15, starting transfers between devices, to_tensor(): return lax.ppermute(array, TENSOR, [(i, (i + k) % 4) for i in range(4)])  38.4 us
  transfers between devices with their start and end apart: 125, of which 35 were waited for; matrix products, arithmetic and copies ran while one was open for 20% of the time, Pallas kernels for 20%

commit v1 on v0

--- a/solution.py
+++ b/solution.py
@@ -457,7 +457,7 @@
 
 
 PLANE = (FSDP, HEADS)
-GROUPS = ((0,), (1, 3), (2,))
+GROUPS = (0, 1, 2, 3)
 LANES = 128
 TILE = 512
 UNIT = 128
@@ -496,11 +496,11 @@
 
 def gather_rows(unit):
     along = {0: unit}
-    for k in (1, 3, 2):
+    for k in GROUPS[1:]:
         along[k] = from_tensor(unit, k)
     groups = []
     for group in GROUPS:
-        here = jnp.concatenate([along[k] for k in group], axis=0) if len(group) > 1 else along[group[0]]
+        here = along[group]
         first = swap_plane(here, 0)
         second = swap_plane(here, 1)
         mine = [here, first, second, swap_plane(first, 1)]
@@ -508,9 +508,9 @@
     return groups
 
 
-def scatter_rows(groups):
+def scatter_rows(groups, holds=()):
     total = None
-    for group, (mine, other) in zip(GROUPS, groups):
+    for g, (group, (mine, other)) in enumerate(zip(GROUPS, groups)):
         other = swap_heads(other, 1)
         half = mine.shape[0] // 2
         sent = (mine[half:].astype(f32) + other[half:].astype(f32)).astype(bf16)
@@ -519,11 +519,12 @@
         near = [a[:part].astype(f32) for a in (mine, other, sent)]
         far = [a[part:half].astype(f32) for a in (mine, other)] + [sent[part:].astype(f32)]
         far = swap_plane((far[0] + far[1] + far[2]).astype(bf16), 0)
+        if g < len(holds):
+            far = after(far, holds[g])
         summed = near[0] + near[1] + near[2] + far.astype(f32)
-        for k, piece in zip(group, jnp.split(summed, len(group), axis=0)):
-            if k:
-                piece = to_tensor(piece.astype(bf16), k).astype(f32)
-            total = piece if total is None else total + piece
+        if group:
+            summed = to_tensor(summed.astype(bf16), group).astype(f32)
+        total = summed if total is None else total + summed
     return total
 
 
@@ -535,15 +536,17 @@
     return along, [swap_fsdp(p) for p in along]
 
 
-def scatter_weight(parts):
+def scatter_weight(parts, hold=None, end=None):
     parts = [p.astype(bf16) for p in parts]
     summed = {}
     for k in (1, 3, 2, 0):
         far = swap_fsdp(parts[4 + k])
+        far = far if hold is None else after(far, hold)
         summed[k] = parts[k].astype(f32) + far.astype(f32)
     total = summed[0]
     for k in (1, 3, 2):
-        total = total + to_tensor(summed[k].astype(bf16), k).astype(f32)
+        far = to_tensor(summed[k].astype(bf16), k)
+        total = total + (far if end is None else after(far, end)).astype(f32)
     return total
 
 
@@ -583,8 +586,10 @@
     pieces = 8
     x_refs, g_refs = refs[:pieces], refs[pieces : 2 * pieces]
     gate_ref, up_ref, shared_ref, down_ref = refs[2 * pieces : 2 * pieces + 4]
-    d1_ref, d2_ref, h_ref, bg_ref, bu_ref, bs_ref = refs[2 * pieces + 4 : 2 * pieces + 10]
-    x_scr, g_scr, sems = refs[2 * pieces + 10 :]
+    d1_ref, d2_ref, y1_ref, y2_ref, h_ref, bg_ref, bu_ref, bs_ref = refs[
+        2 * pieces + 4 : 2 * pieces + 12
+    ]
+    x_scr, g_scr, sems = refs[2 * pieces + 12 :]
     step = pl.program_id(0)
     half = pl.num_programs(0) // 2
     plan = spans([r.shape[0] for r in x_refs], TILE)
@@ -657,13 +662,17 @@
     result = nn(back_gate, gate_ref[...]) + nn(back_up, up_ref[...])
     result = (result + nn(bs_ref[...], shared_ref[...])).astype(bf16)
 
+    out = nn(h_ref[...], down_ref[...]).astype(bf16)
+
     @pl.when(step < half)
     def _():
         d1_ref[...] = result
+        y1_ref[...] = out
 
     @pl.when(step >= half)
     def _():
         d2_ref[...] = result
+        y2_ref[...] = out
 
 
 def hidden_step(first, rows, grads, gate_all, up_all, shared_all, down_all):
@@ -690,14 +699,14 @@
     weights = (gate_all, up_all, shared_all, down_all)
     return pl.pallas_call(
         hidden_kernel,
-        out_shape=(row_shape, row_shape)
+        out_shape=(row_shape,) * 4
         + tuple(jax.ShapeDtypeStruct((2 * count, w), bf16) for w in widths),
         grid_spec=pltpu.PrefetchScalarGridSpec(
             num_scalar_prefetch=1,
             grid=(2 * half,),
             in_specs=[pl.BlockSpec(memory_space=pl.ANY)] * (len(rows) + len(grads))
             + [pl.BlockSpec(w.shape, whole, pipeline_mode=once) for w in weights],
-            out_specs=[pl.BlockSpec((TILE, D), near), pl.BlockSpec((TILE, D), far)]
+            out_specs=[pl.BlockSpec((TILE, D), near), pl.BlockSpec((TILE, D), far)] * 2
             + [pl.BlockSpec((TILE, w), step) for w in widths],
             scratch_shapes=[
                 pltpu.VMEM((2, TILE, D), bf16),
@@ -707,7 +716,7 @@
         ),
         compiler_params=pltpu.CompilerParams(vmem_limit_bytes=58 * 1024 * 1024),
         cost_estimate=pl.CostEstimate(
-            flops=2 * count * D * (3 * routed + width + 4 * LANES + routed) * 2,
+            flops=2 * count * D * (3 * routed + 2 * width + 4 * LANES + routed) * 2,
             bytes_accessed=2 * count * (3 * D + 3 * width) * 2 + 3 * D * width * 2,
             transcendentals=2 * count * width,
         ),
@@ -929,6 +938,151 @@
         scratch_shapes=[pltpu.SemaphoreType.DMA((8,))],
         compiler_params=pltpu.CompilerParams(vmem_limit_bytes=58 * 1024 * 1024),
     )(rows, *pieces)
+
+
+def turn(rows, cosine, sine, back=False):
+    lane = lax.broadcasted_iota(jnp.int32, rows.shape, 1)
+    other = jnp.where(lane % ROPE < ROPE // 2, -pltpu.roll(rows, 96, 1), pltpu.roll(rows, 32, 1))
+    return rows * cosine - other * sine if back else rows * cosine + other * sine
+
+
+def masked_scores(query, key, query_rope, key_rope):
+    scores = (nt(query, key) + nt(query_rope, key_rope)) * (NOPE + ROPE) ** (-0.5)
+    row = lax.broadcasted_iota(jnp.int32, scores.shape, 0)
+    return jnp.where(row >= lax.broadcasted_iota(jnp.int32, scores.shape, 1), scores, -1e30)
+
+
+def attend_kernel(
+    first_ref,
+    latent_ref,
+    gain_ref,
+    weight_ref,
+    cosine_ref,
+    sine_ref,
+    norm_ref,
+    query_ref,
+    kv_ref,
+    rope_ref,
+    total_ref,
+    context_ref,
+):
+    cosine, sine = cosine_ref[...], sine_ref[...]
+    latent = latent_ref[...].astype(f32).T
+    norm_ref[...] = (rms_parts(latent[:, :KVR])[0] * gain_ref[...]).astype(bf16)
+    kv_ref[...] = nn(norm_ref[...], weight_ref[...]).astype(bf16)
+    rope = turn(latent[:, KVR:], cosine, sine)
+    ropes = (rope.astype(bf16), pltpu.roll(rope, ROPE, 1).astype(bf16))
+    rope_ref[...] = ropes[0]
+    heads = context_ref.shape[1] // VDIM
+    query_ref[:, : heads * NOPE] = first_ref[:, : heads * NOPE].astype(bf16)
+    totals = jnp.zeros(total_ref.shape, f32)
+    lane = lax.broadcasted_iota(jnp.int32, totals.shape, 1)
+    for n in range(heads):
+        pair = slice(heads * NOPE + n // 2 * LANES, heads * NOPE + (n // 2 + 1) * LANES)
+        if n % 2 == 0:
+            query_ref[:, pair] = turn(first_ref[:, pair], cosine, sine).astype(bf16)
+        key = slice(2 * n * NOPE, (2 * n + 1) * NOPE)
+        value = slice((2 * n + 1) * NOPE, (2 * n + 2) * NOPE)
+        own = slice(n * NOPE, (n + 1) * NOPE)
+        scores = masked_scores(query_ref[:, own], kv_ref[:, key], query_ref[:, pair], ropes[n % 2])
+        highest_score = jnp.max(scores, axis=1, keepdims=True)
+        shifted = jnp.exp(scores - highest_score)
+        total = jnp.sum(shifted, axis=1, keepdims=True)
+        totals = jnp.where(lane == n, highest_score + jnp.log(total), totals)
+        context_ref[:, own] = nn((shifted / total).astype(bf16), kv_ref[:, value]).astype(bf16)
+    total_ref[...] = totals
+
+
+def attend_step(first_out, latent, gain, weight, cosine, sine):
+    rows = first_out.shape[0]
+    vmem = pl.BlockSpec(memory_space=pltpu.VMEM)
+    kv_width = weight.shape[1]
+    heads = kv_width // (NOPE + VDIM)
+    shapes = (
+        ((rows, KVR), bf16),
+        ((rows, heads * (NOPE + ROPE)), bf16),
+        ((rows, kv_width), bf16),
+        ((rows, LANES), bf16),
+        ((rows, LANES), f32),
+        ((rows, heads * VDIM), bf16),
+    )
+    return pl.pallas_call(
+        attend_kernel,
+        out_shape=tuple(jax.ShapeDtypeStruct(*shape) for shape in shapes),
+        in_specs=[vmem] * 6,
+        out_specs=(vmem,) * len(shapes),
+        compiler_params=pltpu.CompilerParams(vmem_limit_bytes=58 * 1024 * 1024),
+    )(first_out, latent, gain, weight, cosine, sine)
+
+
+def attend_back_kernel(
+    grad_ref,
+    latent_ref,
+    gain_ref,
+    weight_ref,
+    cosine_ref,
+    sine_ref,
+    query_ref,
+    kv_ref,
+    rope_ref,
+    total_ref,
+    grad_query_ref,
+    grad_kv_ref,
+    term_ref,
+    gain_grad_ref,
+):
+    cosine, sine = cosine_ref[...], sine_ref[...]
+    scale = (NOPE + ROPE) ** (-0.5)
+    ropes = (rope_ref[...], pltpu.roll(rope_ref[...].astype(f32), ROPE, 1).astype(bf16))
+    totals = total_ref[...]
+    lane = lax.broadcasted_iota(jnp.int32, totals.shape, 1)
+    heads = grad_ref.shape[1] // VDIM
+    grad_ropes = [jnp.zeros(totals.shape, f32), jnp.zeros(totals.shape, f32)]
+    grad_pair = None
+    for n in range(heads):
+        pair = slice(heads * NOPE + n // 2 * LANES, heads * NOPE + (n // 2 + 1) * LANES)
+        key = slice(2 * n * NOPE, (2 * n + 1) * NOPE)
+        value = slice((2 * n + 1) * NOPE, (2 * n + 2) * NOPE)
+        own = slice(n * NOPE, (n + 1) * NOPE)
+        scores = masked_scores(query_ref[:, own], kv_ref[:, key], query_ref[:, pair], ropes[n % 2])
+        total = jnp.sum(jnp.where(lane == n, totals, 0.0), axis=1, keepdims=True)
+        probabilities = jnp.exp(scores - total)
+        grad_probs = nt(grad_ref[:, own], kv_ref[:, value])
+        centred = jnp.sum(probabilities * grad_probs, axis=1, keepdims=True)
+        grad_scores = (probabilities * (grad_probs - centred)).astype(bf16)
+        grad_query_ref[:, own] = (nn(grad_scores, kv_ref[:, key]) * scale).astype(bf16)
+        grad_kv_ref[:, key] = (tn(grad_scores, query_ref[:, own]) * scale).astype(bf16)
+        grad_kv_ref[:, value] = tn(probabilities.astype(bf16), grad_ref[:, own]).astype(bf16)
+        part = nn(grad_scores, ropes[n % 2]) * scale
+        grad_pair = part if n % 2 == 0 else grad_pair + part
+        if n % 2:
+            grad_query_ref[:, pair] = turn(grad_pair, cosine, sine, True).astype(bf16)
+        grad_ropes[n % 2] += tn(grad_scores, query_ref[:, pair]) * scale
+    grad_rope = grad_ropes[0] + pltpu.roll(grad_ropes[1], ROPE, 1)
+    grad_rope = turn(jnp.where(lane < ROPE, grad_rope, 0.0), cosine, sine, True)
+    grad_norm = nt(grad_kv_ref[...], weight_ref[...])
+    normed, inverse = rms_parts(latent_ref[:KVR, :].astype(f32).T)
+    gain_grad_ref[...] = jnp.sum(grad_norm * normed, axis=0, keepdims=True)
+    term_ref[:KVR, :] = rms_back(grad_norm, normed, inverse, gain_ref[...]).T
+    term_ref[KVR:, :] = grad_rope.T
+
+
+def attend_back_step(grad_context, latent, gain, weight, cosine, sine, query, kv, rope, totals):
+    rows = grad_context.shape[0]
+    vmem = pl.BlockSpec(memory_space=pltpu.VMEM)
+    shapes = (
+        (query.shape, bf16),
+        (kv.shape, bf16),
+        ((KVR + LANES, rows), f32),
+        ((1, KVR), f32),
+    )
+    return pl.pallas_call(
+        attend_back_kernel,
+        out_shape=tuple(jax.ShapeDtypeStruct(*shape) for shape in shapes),
+        in_specs=[vmem] * 10,
+        out_specs=(vmem,) * len(shapes),
+        compiler_params=pltpu.CompilerParams(vmem_limit_bytes=58 * 1024 * 1024),
+    )(grad_context, latent, gain, weight, cosine, sine, query, kv, rope, totals)
 
 
 def pack_kernel(place_ref, x_ref, query_ref, latent_ref, norm_ref, kv_ref, *refs):
@@ -993,7 +1147,6 @@
     head_dim = NOPE + ROPE
     local_heads = w_query.shape[1] // head_dim
     query_width = local_heads * head_dim
-    score_scale = head_dim ** (-0.5)
     hosts = lax.axis_size(FSDP) * lax.axis_size(HEADS)
     experts = EXP_LOC * hosts
     capacity = row_count * TOP * 5 // (4 * experts)
@@ -1032,7 +1185,15 @@
     def fill(piece, axis, size):
         return jnp.pad(piece, [(0, size - piece.shape[axis] if a == axis else 0) for a in range(2)])
 
-    first_pack = jnp.concatenate([w_query, pick(w_latent, h, 4, 1)], axis=1)
+    by_head = w_query.reshape(query_rows, local_heads, head_dim)
+    first_pack = jnp.concatenate(
+        [
+            by_head[..., :NOPE].reshape(query_rows, -1),
+            by_head[..., NOPE:].reshape(query_rows, -1),
+            pick(w_latent, h, 4, 1),
+        ],
+        axis=1,
+    )
     first_pack = jnp.concatenate([fill(first_pack, 1, kv_width), w_kv], axis=0)
     first_along, first_far = gather_weight(first_pack)
     first_parts = first_along + first_far
@@ -1068,48 +1229,19 @@
     gain1 = chunks_to(norm1_gain, relative, 0)
     first_normed, first_inverse = rms_parts(residual)
     first_input = (first_normed * gain1).astype(bf16)
-    cosine, sine_table = rope_tables(row_count)
+    cosine, sine_table = (jnp.tile(a, (1, LANES * 2 // ROPE)) for a in rope_tables(row_count))
     first_input = after(first_input, gate_all, up_all, shared_all, down_all)
     places = jnp.stack(relative).astype(jnp.int32)
     first_out, w_first, kv_full = first_step(places, first_input, first_parts, w_kv.shape[0])
     w_queries, w_latents = w_first[:, :query_width], w_first[:, query_width:latent_stop]
     latent_own = first_out[:, query_width:latent_stop].astype(bf16).T
-    latent_raw = rows_absolute(gather_heads(latent_own)).T.astype(f32)
-    query_raw = first_out[:, :query_width].reshape(row_count, local_heads, head_dim)
-    queries = jnp.concatenate(
-        [
-            query_raw[..., :NOPE],
-            rotate(query_raw[..., NOPE:], cosine[:, None, :], sine_table[:, None, :]),
-        ],
-        axis=-1,
-    ).astype(bf16)
-    latent_normed, latent_inverse = rms_parts(latent_raw[:, :KVR])
-    latent_norm = (latent_normed * latent_gain).astype(bf16)
-    key_rope = rotate(latent_raw[:, KVR:], cosine, sine_table).astype(bf16)
-    key_value = nn(latent_norm, kv_full).astype(bf16).reshape(row_count, local_heads, NOPE + VDIM)
-    keys = jnp.concatenate(
-        [
-            key_value[..., :NOPE],
-            jnp.broadcast_to(key_rope[:, None, :], (row_count, local_heads, ROPE)),
-        ],
-        axis=-1,
-    )
-    values = key_value[..., NOPE:]
+    latent_raw = rows_absolute(gather_heads(latent_own))
+    latent_raw = fill(latent_raw, 0, KVR + LANES)
+    latent_gain = latent_gain[None, :]
+    tables = (latent_raw, latent_gain, kv_full, cosine, sine_table)
+    latent_norm, *saved, context = attend_step(first_out, *tables)
     out_along, out_far = gather_weight(w_out.T)
-    causal = jnp.arange(LEN)[:, None] >= jnp.arange(LEN)[None, :]
-
-    def score_block():
-        scores = jnp.einsum(SCORE, queries, keys, preferred_element_type=f32) * score_scale
-        return jnp.where(causal[None], scores, -1e30)
-
-    scores = score_block()
-    highest_score = jnp.max(scores, axis=-1, keepdims=True)
-    log_total = highest_score + jnp.log(
-        jnp.sum(jnp.exp(scores - highest_score), axis=-1, keepdims=True)
-    )
-    probabilities = jnp.exp(scores - log_total).astype(bf16)
-    context = jnp.einsum(MIX, probabilities, values, preferred_element_type=f32)
-    context = rows_relative(context.astype(bf16).reshape(row_count, local_heads * VDIM))
+    context = rows_relative(context)
     kept, sent, out_full = out_step(context, out_along + out_far)
     attention_own = reduce_heads(kept, sent)
     after_attention = quarter(block_input).astype(f32) + chunks_to(attention_own, absolute, 1)
@@ -1119,17 +1251,19 @@
     rows = gather_rows(second_input)
     grads = gather_rows(grad_unit)
     first_expert = ((f * lax.axis_size(HEADS) + h) * EXP_LOC).astype(jnp.int32).reshape(1)
+    out_groups = []
     grad_groups, hidden_parts, gate_parts, up_parts, shared_parts = [], [], [], [], []
     for rows_g, grads_g in zip(rows, grads):
-        near, far, hidden_g, gate_g, up_g, shared_g = hidden_step(
+        near, far, out_near, out_far, hidden_g, gate_g, up_g, shared_g = hidden_step(
             first_expert, rows_g, grads_g, gate_all, up_all, shared_all, down_all
         )
         grad_groups.append((near, far))
+        out_groups.append((out_near, out_far))
         hidden_parts.append(hidden_g)
         gate_parts.append(gate_g)
         up_parts.append(up_g)
         shared_parts.append(shared_g)
-    grad_second = scatter_rows(grad_groups)
+    grad_second = scatter_rows(grad_groups, [grad_groups[3][0]])
 
     second_gain_part = jnp.sum(grad_second * second_normed, axis=0)
     grad_after = cotangent_own.astype(f32) + rms_back(
@@ -1139,43 +1273,13 @@
     grad_attention = gather_heads(grad_after.astype(bf16))
     out_part = tn(grad_attention, context)
     grad_context = nn(grad_attention, out_full).astype(bf16)
-    grad_context = rows_absolute(grad_context).reshape(row_count, local_heads, VDIM)
-    probabilities = jnp.exp(score_block() - log_total)
-    grad_probs = jnp.einsum(SCORE, grad_context, values, preferred_element_type=f32)
-    centred = jnp.sum(probabilities * grad_probs, axis=-1, keepdims=True)
-    grad_scores = (probabilities * (grad_probs - centred)).astype(bf16)
-    grad_queries = (
-        jnp.einsum(MIX, grad_scores, keys, preferred_element_type=f32) * score_scale
-    )
-    grad_keys = (
-        jnp.einsum(BACK, grad_scores, queries, preferred_element_type=f32) * score_scale
-    )
-    grad_values = jnp.einsum(
-        BACK, probabilities.astype(bf16), grad_context, preferred_element_type=f32
-    )
-    grad_query_raw = (
-        jnp.concatenate(
-            [
-                grad_queries[..., :NOPE],
-                unrotate(grad_queries[..., NOPE:], cosine[:, None, :], sine_table[:, None, :]),
-            ],
-            axis=-1,
-        )
-        .astype(bf16)
-        .reshape(row_count, query_width)
-    )
+    grad_context = rows_absolute(grad_context)
+    grad_query_raw, grad_key_value, latent_term, latent_gain_part = attend_back_step(
+        grad_context, *tables, *saved
+    )
+    latent_gain_part = latent_gain_part[0]
     first_from_query = nt(rows_relative(grad_query_raw), w_queries)
-    grad_key_value = (
-        jnp.concatenate([grad_keys[..., :NOPE], grad_values], axis=-1)
-        .astype(bf16)
-        .reshape(row_count, local_heads * (NOPE + VDIM))
-    )
-    grad_latent_norm = nt(grad_key_value, kv_full)
-    latent_gain_part = jnp.sum(grad_latent_norm * latent_normed, axis=0)
-    grad_compressed = rms_back(grad_latent_norm, latent_normed, latent_inverse, latent_gain)
-    grad_key_rope = unrotate(jnp.sum(grad_keys[..., NOPE:], axis=1), cosine, sine_table)
-    latent_term = jnp.concatenate([grad_compressed, grad_key_rope], axis=-1)
-    latent_term = rows_relative(latent_term.T)
+    latent_term = rows_relative(latent_term[: 4 * latent_width])
     half = latent_term.shape[0] // 2
     grad_latent = reduce_heads(latent_term[:half], latent_term[half:]).astype(bf16)
     grad_latent_rows = jnp.concatenate([pick(grad_latent, h ^ j, 4, 1) for j in turns], axis=1)
@@ -1194,9 +1298,17 @@
     input_own = grad_after + rms_back(grad_first, first_normed_own, quarter(first_inverse), gain1)
     input_grad = rows_absolute(gather_heads(chunks_to(input_own.astype(bf16), absolute, 1))).astype(f32)
 
-    w_out_grad = scatter_weight(out_part.reshape(8, -1, out_part.shape[1])).T
-    first_grad = scatter_weight(first_pieces)
-    w_query_grad = first_grad[:query_rows, :query_width]
+    w_out_grad = scatter_weight(out_part.reshape(8, -1, out_part.shape[1]), end=grad_first).T
+    first_grad = scatter_weight(first_pieces, grad_first)
+    w_query_grad = jnp.concatenate(
+        [
+            first_grad[:query_rows, : local_heads * NOPE].reshape(query_rows, local_heads, NOPE),
+            first_grad[:query_rows, local_heads * NOPE : query_width].reshape(
+                query_rows, local_heads, ROPE
+            ),
+        ],
+        axis=2,
+    ).reshape(query_rows, query_width)
     w_kv_grad = first_grad[query_rows:]
     gain_parts = jnp.concatenate(
         [
@@ -1214,11 +1326,7 @@
     gains = jnp.sum(last[:, latent_rows:], axis=0).reshape(-1)
     side = D // 8
 
-    out_groups = []
-    for hidden_g in hidden_parts:
-        half = hidden_g.shape[0] // 2
-        pair = tuple(nn(p, down_all).astype(bf16) for p in (hidden_g[:half], hidden_g[half:]))
-        out_groups.append(tuple(after(p, grad_attention) for p in pair))
+    out_groups = [tuple(after(p, grad_after) for p in pair) for pair in out_groups]
     ffn_own = scatter_rows(out_groups)
     output = rows_absolute(gather_heads((after_attention + ffn_own).astype(bf16)))
     rows_list = [p for g in rows for p in g]

time: 961 us -> 1020 us (1.061)
  starting transfers between devices: 154 us -> 219 us
  Pallas kernels: 208 us -> 258 us
  matrix products: 56.1 us -> 11.8 us
  local copies, waits for them, and re-layouts: 84.2 us -> 66.2 us
    ppermute x30 -> x40, waiting for transfers between devices: 92.6 us -> 149 us  [swap_plane(): return lax.ppermute(array, PLANE, pairs)]
    pallas_call x3 -> x6, Pallas kernels: 112 us -> 163 us  [the longest x4 146 us: hidden_step(): pl.pallas_call(hidden_kernel, out_shape=(row_shape,) * 4 + tuple((jax.Sha...]
    ppermute x15, starting transfers between devices: 38.4 us -> 73.5 us  [to_tensor(): return lax.ppermute(array, TENSOR, [(i, (i + k) % 4) for i in range(4)])]
    dot_general x8 -> x1, matrix products: 34.5 us -> 3.17 us  [nn(): return jnp.dot(left, right, preferred_element_type=f32)]
    ppermute x30 -> x40, starting transfers between devices: 25.7 us -> 49.3 us  [swap_plane(): return lax.ppermute(array, PLANE, pairs)]
    ppermute x12, waiting for transfers between devices: 93.2 us -> 72 us  [from_tensor(): return lax.ppermute(array, TENSOR, [((i + k) % 4, i) for i in range(4)])]
    ppermute x15, waiting for transfers between devices: 75.4 us -> 55 us  [to_tensor(): return lax.ppermute(array, TENSOR, [(i, (i + k) % 4) for i in range(4)])]
    convert_element_type x12 -> x13, other arithmetic: 12 us -> 20.7 us  [the longest x6 11.6 us: scatter_rows(): summed = to_tensor(summed.astype(bf16), group).astype(f32)]
  transfers between devices with their start and end apart: 125 -> 145, of which waited for: 35 -> 46; matrix products, arithmetic and copies ran while one was open for 20% -> 15% of each run, Pallas kernels for 20% -> 26%
where the time goes in v1:
time: 1020 us; the launch traced here: 1010 us
  waiting for transfers between devices  352 us (35%)
  Pallas kernels  258 us (25%)
  starting transfers between devices  219 us (21%)
  other arithmetic  98.3 us (10%)
  local copies, waits for them, and re-layouts  66.2 us (6%)
  matrix products  11.8 us (1%)
    ppermute x40, waiting for transfers between devices, swap_plane(): return lax.ppermute(array, PLANE, pairs)  149 us
    pallas_call x4, Pallas kernels, hidden_step(): pl.pallas_call(hidden_kernel, out_shape=(row_shape,) * 4 + tuple((jax.Sha...  146 us
    ppermute x15, starting transfers between devices, to_tensor(): return lax.ppermute(array, TENSOR, [(i, (i + k) % 4) for i in range(4)])  73.5 us
    ppermute x12, waiting for transfers between devices, from_tensor(): return lax.ppermute(array, TENSOR, [((i + k) % 4, i) for i in range(4)])  72 us
    pallas_call x3, Pallas kernels, weight_grad(): pl.pallas_call(kernel, out_shape=jax.ShapeDtypeStruct(shape, dtype), in_s...  60.2 us
    ppermute x15, waiting for transfers between devices, to_tensor(): return lax.ppermute(array, TENSOR, [(i, (i + k) % 4) for i in range(4)])  55 us
    ppermute x20, waiting for transfers between devices, swap_fsdp(): return lax.ppermute(array, FSDP, [(0, 1), (1, 0)])  54 us
    ppermute x40, starting transfers between devices, swap_plane(): return lax.ppermute(array, PLANE, pairs)  49.3 us
  transfers between devices with their start and end apart: 145, of which 46 were waited for; matrix products, arithmetic and copies ran while one was open for 15% of the time, Pallas kernels for 26%

profile of v1, /device:TPU:0, one launch (start us, length us, event | category | flops | bytes accessed | tf_op | source)
XLA Modules:
  0.0 1008.4 jit_solution(12078824067608090121)
XLA Ops:
  3.3 5.1 collective-permute-start
  13.1 4.3 all-to-all-start
  32.5 4.1 pad.32
  42.1 4.8 convert_multiply_fusion
  48.9 17.0 %collective-permute-done.2.refs_2_ = bf16[320,1024]{1,0:T(8,128)(2,1)} collective-permute-done((bf16[320,1024]{1,0:T(8,128)(2,1)}, bf16[320,1024]{1,0:T(8,128)(2,1)}, u32[]{:S(2)}, u32[]{:S(2)}) %collective-permute-start.2) | collective-permute-done | bytes 655392 | tf_op jit(solution)/shard_map/ppermute | solution.py:473
  78.2 7.7 collective-permute-start.11
  87.4 10.1 %collective-permute-done.6.refs_7_ = bf16[320,1024]{1,0:T(8,128)(2,1)} collective-permute-done((bf16[320,1024]{1,0:T(8,128)(2,1)}, bf16[320,1024]{1,0:T(8,128)(2,1)}, u32[]{:S(2)}, u32[]{:S(2)}) %collective-permute-start.6) | collective-permute-done | bytes 655392 | tf_op jit(solution)/shard_map/ppermute | solution.py:481
  97.5 7.9 shard_map.289
  112.7 4.8 collective-permute-start.43
  122.1 6.6 shard_map.290
  132.6 4.9 collective-permute-done.15.refs_7_
  138.2 5.8 shard_map.291
  144.0 3.4 collective-permute-start.79
  150.5 22.2 %collective-permute-done.79.refs_8_.refs_20_.refs_56_ = bf16[128,2176]{1,0:T(8,128)(2,1)} collective-permute-done((bf16[128,2176]{1,0:T(8,128)(2,1)S(1)}, bf16[128,2176]{1,0:T(8,128)(2,1)}, u32[]{:S(2)}, u32[]{:S(2)}) %collective-permute-start.79) | collective-permute-done | bytes 557088 | tf_op jit(solution)/shard_map/ppermute | solution.py:473
  181.2 8.3 collective-permute-done.44.refs_9_.refs_29_.refs_65_
  192.7 8.9 collective-permute-done.80.refs_9_.refs_21_.refs_57_
  202.3 5.7 collective-permute-start.63
  209.2 5.1 collective-permute-done.81.refs_10_.refs_22_.refs_58_
  215.9 4.0 collective-permute-start.30
  224.6 4.4 collective-permute-done.27.refs_11_.refs_7_.refs_43_
  230.8 4.1 collective-permute-done.46.refs_11_.refs_31_.refs_67_
  241.5 5.3 collective-permute-done.62.refs_11_.refs_15_.refs_51_
  247.0 11.8 %collective-permute-start.35 = (bf16[128,2048]{1,0:T(8,128)(2,1)S(1)}, bf16[128,2048]{1,0:T(8,128)(2,1)S(1)}, u32[]{:S(2)}, u32[]{:S(2)}) collective-permute-start(bf16[128,2048]{1,0:T(8,128)(2,1)S(1)} %multiply_convert_fusion.1.refs_0_.refs_4_), channel_id=1, source_target_pairs={{3,0},{0,1},{1,2},{2,3},{7,4},{4,5},{5,6},{6,7},{11,8},{8,9},{9,10... | collective-permute-start | bytes 1572872 | tf_op jit(solution)/shard_map/ppermute | solution.py:473
  265.1 9.2 collective-permute-done.35.refs_0_.refs_28_
  274.4 22.3 %collective-permute-done.71.refs_0_.refs_20_ = bf16[128,2048]{1,0:T(8,128)(2,1)} collective-permute-done((bf16[128,2048]{1,0:T(8,128)(2,1)S(1)}, bf16[128,2048]{1,0:T(8,128)(2,1)}, u32[]{:S(2)}, u32[]{:S(2)}) %collective-permute-start.71) | collective-permute-done | bytes 524320 | tf_op jit(solution)/shard_map/ppermute | solution.py:473
  300.9 10.4 %collective-permute-done.36.refs_1_.refs_29_ = bf16[128,2048]{1,0:T(8,128)(2,1)} collective-permute-done((bf16[128,2048]{1,0:T(8,128)(2,1)S(1)}, bf16[128,2048]{1,0:T(8,128)(2,1)}, u32[]{:S(2)}, u32[]{:S(2)}) %collective-permute-start.36) | collective-permute-done | bytes 524320 | tf_op jit(solution)/shard_map/ppermute | solution.py:494
  313.8 8.6 collective-permute-done.72.refs_1_.refs_21_
  324.3 3.2 collective-permute-done.20.refs_3_.refs_7_
  336.3 36.5 %shard_map.292 = (bf16[512,2048]{1,0:T(8,128)(2,1)}, bf16[512,2048]{1,0:T(8,128)(2,1)}, bf16[512,2048]{1,0:T(8,128)(2,1)}, bf16[512,2048]{1,0:T(8,128)(2,1)}, bf...) custom-call(s32[1]{0:T(128)} %bitcast.31.first_ref, ...), custom_call_target="tpu_custom_call" | custom-call | flops 22548578304 | bytes 29097984 | tf_op jit(solution)/shard_map/pallas_call | solution.py:700
  375.5 36.6 %shard_map.293 = (bf16[512,2048]{1,0:T(8,128)(2,1)}, bf16[512,2048]{1,0:T(8,128)(2,1)}, bf16[512,2048]{1,0:T(8,128)(2,1)}, bf16[512,2048]{1,0:T(8,128)(2,1)}, bf...) custom-call(s32[1]{0:T(128)} %bitcast.31.first_ref, ...), custom_call_target="tpu_custom_call" | custom-call | flops 22548578304 | bytes 29097984 | tf_op jit(solution)/shard_map/pallas_call | solution.py:700
  414.2 36.3 %shard_map.295 = (bf16[512,2048]{1,0:T(8,128)(2,1)}, bf16[512,2048]{1,0:T(8,128)(2,1)}, bf16[512,2048]{1,0:T(8,128)(2,1)}, bf16[512,2048]{1,0:T(8,128)(2,1)}, bf...) custom-call(s32[1]{0:T(128)} %bitcast.31.first_ref, ...), custom_call_target="tpu_custom_call" | custom-call | flops 22548578304 | bytes 29097984 | tf_op jit(solution)/shard_map/pallas_call | solution.py:700
  452.4 36.8 %shard_map.294 = (bf16[512,2048]{1,0:T(8,128)(2,1)}, bf16[512,2048]{1,0:T(8,128)(2,1)}, bf16[512,2048]{1,0:T(8,128)(2,1)}, bf16[512,2048]{1,0:T(8,128)(2,1)}, bf...) custom-call(s32[1]{0:T(128)} %bitcast.31.first_ref, ...), custom_call_target="tpu_custom_call" | custom-call | flops 22548578304 | bytes 29097984 | tf_op jit(solution)/shard_map/pallas_call | solution.py:700
  489.4 20.2 %shard_map.298 = f32[2,352,2048]{2,1,0:T(8,128)} custom-call(bf16[1024,768]{1,0:T(8,128)(2,1)} %get-tuple-element.148.refs_0_, bf16[1024,768]{1,0:T(8,128)(2,1)} %get-tuple-element.149.refs_1_, bf16[1024,768]{1,0:T(8,128)(2,1)} %get-tuple-element.150.refs_2_, bf16[1024,768]{1,0:T(8,128)(2,1)} %get-tuple-element.151.refs_3_, bf16[128,2048]{1,0:T(8,128)(2,1)} %copy-done.14, ...), custom_call_target="tpu_custom_call" | custom-call | flops 12884901888 | bytes 29360128 | tf_op jit(solution)/shard_map/pallas_call | solution.py:776
  519.7 5.2 collective-permute-done.33
  527.5 14.3 %collective-permute-done.92 = bf16[256,2048]{1,0:T(8,128)(2,1)S(1)} collective-permute-done((bf16[256,2048]{1,0:T(8,128)(2,1)S(1)}, bf16[256,2048]{1,0:T(8,128)(2,1)S(1)}, u32[]{:S(2)}, u32[]{:S(2)}) %collective-permute-start.92) | collective-permute-done | bytes 1048608 | tf_op jit(solution)/shard_map/ppermute | solution.py:494
  544.5 14.0 %collective-permute-done.88 = bf16[256,2048]{1,0:T(8,128)(2,1)S(1)} collective-permute-done((bf16[256,2048]{1,0:T(8,128)(2,1)S(1)}, bf16[256,2048]{1,0:T(8,128)(2,1)S(1)}, u32[]{:S(2)}, u32[]{:S(2)}) %collective-permute-start.88) | collective-permute-done | bytes 1048608 | tf_op jit(solution)/shard_map/ppermute | solution.py:494
  561.4 14.0 %collective-permute-done.68 = bf16[256,2048]{1,0:T(8,128)(2,1)S(1)} collective-permute-done((bf16[256,2048]{1,0:T(8,128)(2,1)S(1)}, bf16[256,2048]{1,0:T(8,128)(2,1)S(1)}, u32[]{:S(2)}, u32[]{:S(2)}) %collective-permute-start.68) | collective-permute-done | bytes 1048608 | tf_op jit(solution)/shard_map/ppermute | solution.py:494
  580.4 10.8 %collective-permute-start.94 = (bf16[128,2048]{1,0:T(8,128)(2,1)}, bf16[128,2048]{1,0:T(8,128)(2,1)}, u32[]{:S(2)}, u32[]{:S(2)}) collective-permute-start(bf16[128,2048]{1,0:T(8,128)(2,1)} %add_convert_fusion.20), channel_id=1, source_target_pairs={{0,3},{1,0},{2,1},{3,2},{4,7},{5,4},{6,5},{7,6},{8,11},{9,8},{10,9... | collective-permute-start | bytes 1572872 | tf_op jit(solution)/shard_map/ppermute | solution.py:477
  596.2 20.0 %shard_map.299 = f32[2,352,2048]{2,1,0:T(8,128)} custom-call(bf16[1024,768]{1,0:T(8,128)(2,1)} %get-tuple-element.152.refs_0_, bf16[1024,768]{1,0:T(8,128)(2,1)} %get-tuple-element.153.refs_1_, bf16[1024,768]{1,0:T(8,128)(2,1)} %get-tuple-element.154.refs_2_, bf16[1024,768]{1,0:T(8,128)(2,1)} %get-tuple-element.155.refs_3_, bf16[128,2048]{1,0:T(8,128)(2,1)} %copy-done.14, ...), custom_call_target="tpu_custom_call" | custom-call | flops 12884901888 | bytes 29360128 | tf_op jit(solution)/shard_map/pallas_call | solution.py:776
  616.2 18.7 %collective-permute-done.90 = bf16[128,2048]{1,0:T(8,128)(2,1)} collective-permute-done((bf16[128,2048]{1,0:T(8,128)(2,1)}, bf16[128,2048]{1,0:T(8,128)(2,1)}, u32[]{:S(2)}, u32[]{:S(2)}) %collective-permute-start.90) | collective-permute-done | bytes 524320 | tf_op jit(solution)/shard_map/ppermute | solution.py:477
  640.9 20.0 %shard_map.300 = f32[2,352,2048]{2,1,0:T(8,128)} custom-call(bf16[1024,896]{1,0:T(8,128)(2,1)} %get-tuple-element.156.refs_0_.refs_36_, bf16[1024,896]{1,0:T(8,128)(2,1)} %get-tuple-element.157.refs_1_.refs_37_, bf16[1024,896]{1,0:T(8,128)(2,1)} %get-tuple-element.158.refs_2_.refs_38_, bf16[1024,896]{1,0:T(8,128)(2,1)} %get-tuple-element.159.refs_3_.refs_39_, ...), custom_call_target="tpu_custom_call" | custom-call | flops 12884901888 | bytes 29360128 | tf_op jit(solution)/shard_map/pallas_call | solution.py:776
  661.1 14.7 %shard_map.301 = bf16[8,264,256]{2,1,0:T(8,128)(2,1)} custom-call(bf16[1024,256]{1,0:T(8,128)(2,1)} %get-tuple-element.160.refs_0_, bf16[1024,256]{1,0:T(8,128)(2,1)} %get-tuple-element.161.refs_1_, bf16[1024,256]{1,0:T(8,128)(2,1)} %get-tuple-element.162.refs_2_, bf16[1024,256]{1,0:T(8,128)(2,1)} %get-tuple-element.163.refs_3_, ...), custom_call_target="tpu_custom_call" | custom-call | flops 6442450944 | bytes 36700160 | tf_op jit(solution)/shard_map/pallas_call | solution.py:850
  677.0 3.2 convolution_convert_fusion.1
  681.0 10.5 %shard_map.296 = (bf16[512,768]{1,0:T(8,128)(2,1)}, bf16[512,1024]{1,0:T(8,128)(2,1)}, f32[640,512]{1,0:T(8,128)}, f32[1,512]{1,0:T(1,128)}) custom-call(bf16[512,512]{1,0:T(8,128)(2,1)} %pad_maximum_fusion.16.grad_ref, bf16[640,512]{1,0:T(8,128)(2,1)} %fusion.28.latent_ref, f32[1,512]{1,0:T(1,128)} %bitcast.121, ...), custom_call_target="tpu_custom_call" | custom-call | tf_op jit(solution)/shard_map/pallas_call | solution.py:1079
  702.7 3.8 fusion.3
  708.0 3.6 all-to-all-start.1
  714.8 5.7 collective-permute-done.139
  724.3 8.9 collective-permute-done.115
  733.1 4.2 collective-permute-start.142
  738.2 6.1 shard_map.297
  772.9 7.8 collective-permute-done.103
  784.0 7.8 collective-permute-done.99
  795.2 10.2 %collective-permute-done.96 = bf16[256,2048]{1,0:T(8,128)(2,1)S(1)} collective-permute-done((bf16[256,2048]{1,0:T(8,128)(2,1)S(1)}, bf16[256,2048]{1,0:T(8,128)(2,1)S(1)}, u32[]{:S(2)}, u32[]{:S(2)}) %collective-permute-start.96) | collective-permute-done | bytes 1048608 | tf_op jit(solution)/shard_map/ppermute | solution.py:494
  808.5 5.8 collective-permute-done.117
  824.1 13.2 %collective-permute-done.121 = bf16[320,1024]{1,0:T(8,128)(2,1)} collective-permute-done((bf16[320,1024]{1,0:T(8,128)(2,1)}, bf16[320,1024]{1,0:T(8,128)(2,1)}, u32[]{:S(2)}, u32[]{:S(2)}) %collective-permute-start.121) | collective-permute-done | bytes 655392 | tf_op jit(solution)/shard_map/ppermute | solution.py:481
  853.6 14.6 %collective-permute-done.132 = bf16[4,144]{1,0:T(4,128)(2,1)S(1)} collective-permute-done((bf16[4,144]{1,0:T(4,128)(2,1)S(1)}, bf16[4,144]{1,0:T(4,128)(2,1)S(1)}, u32[]{:S(2)}, u32[]{:S(2)}) %collective-permute-start.132) | collective-permute-done | bytes 1184 | tf_op jit(solution)/shard_map/ppermute | solution.py:481
  869.1 3.9 collective-permute-start.131
  886.4 3.7 collective-permute-done.100
  892.8 19.2 %collective-permute-done.126 = bf16[320,1024]{1,0:T(8,128)(2,1)S(1)} collective-permute-done((bf16[320,1024]{1,0:T(8,128)(2,1)}, bf16[320,1024]{1,0:T(8,128)(2,1)S(1)}, u32[]{:S(2)}, u32[]{:S(2)}) %collective-permute-start.126) | collective-permute-done | bytes 655392 | tf_op jit(solution)/shard_map/ppermute | solution.py:477
  912.0 13.6 %collective-permute-start.109 = (bf16[128,2048]{1,0:T(8,128)(2,1)S(1)}, bf16[128,2048]{1,0:T(8,128)(2,1)S(1)}, u32[]{:S(2)}, u32[]{:S(2)}) collective-permute-start(bf16[128,2048]{1,0:T(8,128)(2,1)S(1)} %add_convert_fusion.13), channel_id=1, source_target_pairs={{0,3},{1,0},{2,1},{3,2},{4,7},{5,4},{6,5},{7,6},{8,11},{9,8},{10,9... | collective-permute-start | bytes 1572872 | tf_op jit(solution)/shard_map/ppermute | solution.py:477
  925.6 13.0 %collective-permute-start.105 = (bf16[128,2048]{1,0:T(8,128)(2,1)S(1)}, bf16[128,2048]{1,0:T(8,128)(2,1)S(1)}, u32[]{:S(2)}, u32[]{:S(2)}) collective-permute-start(bf16[128,2048]{1,0:T(8,128)(2,1)S(1)} %add_convert_fusion.15), channel_id=1, source_target_pairs={{0,2},{1,3},{2,0},{3,1},{4,6},{5,7},{6,4},{7,5},{8,10},{9,11},{10,... | collective-permute-start | bytes 1572872 | tf_op jit(solution)/shard_map/ppermute | solution.py:477
  938.6 21.0 %collective-permute-start.101 = (bf16[128,2048]{1,0:T(8,128)(2,1)S(1)}, bf16[128,2048]{1,0:T(8,128)(2,1)S(1)}, u32[]{:S(2)}, u32[]{:S(2)}) collective-permute-start(bf16[128,2048]{1,0:T(8,128)(2,1)S(1)} %add_convert_fusion.17), channel_id=1, source_target_pairs={{0,1},{1,2},{2,3},{3,0},{4,5},{5,6},{6,7},{7,4},{8,9},{9,10},{10,1... | collective-permute-start | bytes 1572872 | tf_op jit(solution)/shard_map/ppermute | solution.py:477
  962.3 3.2 collective-permute-done.134
  966.1 16.9 %collective-permute-done.105 = bf16[128,2048]{1,0:T(8,128)(2,1)S(1)} collective-permute-done((bf16[128,2048]{1,0:T(8,128)(2,1)S(1)}, bf16[128,2048]{1,0:T(8,128)(2,1)S(1)}, u32[]{:S(2)}, u32[]{:S(2)}) %collective-permute-start.105) | collective-permute-done | bytes 524320 | tf_op jit(solution)/shard_map/ppermute | solution.py:477
  (693 shorter events, 287.1 us)
Async XLA Ops:
  3.3 43.6 %collective-permute-start = (bf16[320,1024]{1,0:T(8,128)(2,1)}, bf16[320,1024]{1,0:T(8,128)(2,1)}, u32[]{:S(2)}, u32[]{:S(2)}) collective-permute-start(bf16[320,1024]{1,0:T(8,128)(2,1)} %pad_maximum_fusion.11.refs_0_), channel_id=1, source_target_pairs={{1,0},{2,1},{3,2},{0,3},{5,4},{6,5},{7,6},{4,7},{9,8},{10,9},{11,1... | collective-permute-start | bytes 1966088 | tf_op jit(solution)/shard_map/ppermute | solution.py:473
  8.4 59.0 %collective-permute-start.1 = (bf16[320,1024]{1,0:T(8,128)(2,1)}, bf16[320,1024]{1,0:T(8,128)(2,1)}, u32[]{:S(2)}, u32[]{:S(2)}) collective-permute-start(bf16[320,1024]{1,0:T(8,128)(2,1)} %pad_maximum_fusion.11.refs_0_), channel_id=1, source_target_pairs={{3,0},{0,1},{1,2},{2,3},{7,4},{4,5},{5,6},{6,7},{11,8},{8,9},{9,10... | collective-permute-start | bytes 1966088 | tf_op jit(solution)/shard_map/ppermute | solution.py:473
  8.4 57.5 %collective-permute-start.2 = (bf16[320,1024]{1,0:T(8,128)(2,1)}, bf16[320,1024]{1,0:T(8,128)(2,1)}, u32[]{:S(2)}, u32[]{:S(2)}) collective-permute-start(bf16[320,1024]{1,0:T(8,128)(2,1)} %pad_maximum_fusion.11.refs_0_), channel_id=1, source_target_pairs={{2,0},{3,1},{0,2},{1,3},{6,4},{7,5},{4,6},{5,7},{10,8},{11,9},{8,1... | collective-permute-start | bytes 1966088 | tf_op jit(solution)/shard_map/ppermute | solution.py:473
  9.4 68.8 %collective-permute-start.3 = (bf16[320,1024]{1,0:T(8,128)(2,1)}, bf16[320,1024]{1,0:T(8,128)(2,1)}, u32[]{:S(2)}, u32[]{:S(2)}) collective-permute-start(bf16[320,1024]{1,0:T(8,128)(2,1)} %pad_maximum_fusion.11.refs_0_), channel_id=1, source_target_pairs={{0,16},{16,0},{1,17},{17,1},{2,18},{18,2},{3,19},{19,3},{4,20},{20... | collective-permute-start | bytes 1966088 | tf_op jit(solution)/shard_map/ppermute | solution.py:481
  13.1 54.8 %all-to-all-start = ((bf16[3,704,256]{2,0,1:T(4,128)(2,1)}), bf16[3,704,256]{2,0,1:T(4,128)(2,1)}, u32[]{:S(2)}, u32[]{:S(2)}) async-start(bf16[3,704,256]{2,0,1:T(4,128)(2,1)} %copy.139), calls=%async_computation | async-start | bytes 2883584 | tf_op jit(solution)/shard_map/all_to_all | solution.py:1210
  18.2 94.5 %collective-permute-start.9 = (bf16[256,512]{1,0:T(8,128)(2,1)}, bf16[256,512]{1,0:T(8,128)(2,1)}, u32[]{:S(2)}, u32[]{:S(2)}) collective-permute-start(bf16[256,512]{1,0:T(8,128)(2,1)} %bitcast.30.refs_0_), channel_id=1, source_target_pairs={{1,0},{2,1},{3,2},{0,3},{5,4},{6,5},{7,6},{4,7},{9,8},{10,9},{11,1... | collective-permute-start | bytes 786440 | tf_op jit(solution)/shard_map/ppermute | solution.py:473
  47.0 31.2 %collective-permute-start.4 = (bf16[320,1024]{1,0:T(8,128)(2,1)}, bf16[320,1024]{1,0:T(8,128)(2,1)}, u32[]{:S(2)}, u32[]{:S(2)}) collective-permute-start(bf16[320,1024]{1,0:T(8,128)(2,1)} %collective-permute-done.refs_1_), channel_id=1, source_target_pairs={{0,16},{16,0},{1,17},{17,1},{2,18},{18,2},{3,19},{19,3},{4,20},{20... | collective-permute-start | bytes 1966088 | tf_op jit(solution)/shard_map/ppermute | solution.py:481
  67.4 30.2 %collective-permute-start.6 = (bf16[320,1024]{1,0:T(8,128)(2,1)}, bf16[320,1024]{1,0:T(8,128)(2,1)}, u32[]{:S(2)}, u32[]{:S(2)}) collective-permute-start(bf16[320,1024]{1,0:T(8,128)(2,1)} %collective-permute-done.1.refs_3_), channel_id=1, source_target_pairs={{0,16},{16,0},{1,17},{17,1},{2,18},{18,2},{3,19},{19,3},{4,20},{20... | collective-permute-start | bytes 1966088 | tf_op jit(solution)/shard_map/ppermute | solution.py:481
  78.2 39.4 %collective-permute-start.10 = (bf16[256,512]{1,0:T(8,128)(2,1)}, bf16[256,512]{1,0:T(8,128)(2,1)S(1)}, u32[]{:S(2)}, u32[]{:S(2)}) collective-permute-start(bf16[256,512]{1,0:T(8,128)(2,1)} %bitcast.30.refs_0_), channel_id=1, source_target_pairs={{2,0},{3,1},{0,2},{1,3},{6,4},{7,5},{4,6},{5,7},{10,8},{11,9},{8,1... | collective-permute-start | bytes 786440 | tf_op jit(solution)/shard_map/ppermute | solution.py:473
  78.2 40.8 %collective-permute-start.11 = (bf16[256,512]{1,0:T(8,128)(2,1)}, bf16[256,512]{1,0:T(8,128)(2,1)S(1)}, u32[]{:S(2)}, u32[]{:S(2)}) collective-permute-start(bf16[256,512]{1,0:T(8,128)(2,1)} %bitcast.30.refs_0_), channel_id=1, source_target_pairs={{3,0},{0,1},{1,2},{2,3},{7,4},{4,5},{5,6},{6,7},{11,8},{8,9},{9,10... | collective-permute-start | bytes 786440 | tf_op jit(solution)/shard_map/ppermute | solution.py:473
  85.9 45.4 %collective-permute-start.12 = (bf16[256,512]{1,0:T(8,128)(2,1)}, bf16[256,512]{1,0:T(8,128)(2,1)}, u32[]{:S(2)}, u32[]{:S(2)}) collective-permute-start(bf16[256,512]{1,0:T(8,128)(2,1)} %bitcast.30.refs_0_), channel_id=1, source_target_pairs={{0,16},{16,0},{1,17},{17,1},{2,18},{18,2},{3,19},{19,3},{4,20},{20... | collective-permute-start | bytes 786440 | tf_op jit(solution)/shard_map/ppermute | solution.py:481
  112.7 36.3 %collective-permute-start.43 = (bf16[128,2176]{1,0:T(8,128)(2,1)S(1)}, bf16[128,2176]{1,0:T(8,128)(2,1)S(1)}, u32[]{:S(2)}, u32[]{:S(2)}) collective-permute-start(bf16[128,2176]{1,0:T(8,128)(2,1)S(1)} %pad_maximum_fusion.14.refs_8_.refs_4_.refs_40_), channel_id=1, source_target_pairs={{3,0},{0,1},{1,2},{2,3},{7,4},{4,5},{5,6},{6,7},{11,8},{8,9},{9,10... | collective-permute-start | bytes 1671176 | tf_op jit(solution)/shard_map/ppermute | solution.py:473
  144.0 33.1 %collective-permute-start.16 = (bf16[256,2048]{1,0:T(8,128)(2,1)}, bf16[256,2048]{1,0:T(8,128)(2,1)S(1)}, u32[]{:S(2)}, u32[]{:S(2)}) collective-permute-start(bf16[256,2048]{1,0:T(8,128)(2,1)} %get-tuple-element.96), channel_id=1, source_target_pairs={{0,4},{4,0},{8,12},{12,8},{1,5},{5,1},{9,13},{13,9},{2,6},{6,2},{1... | collective-permute-start | bytes 3145736 | tf_op jit(solution)/shard_map/ppermute | solution.py:485
  258.9 37.8 %collective-permute-start.71 = (bf16[128,2048]{1,0:T(8,128)(2,1)S(1)}, bf16[128,2048]{1,0:T(8,128)(2,1)}, u32[]{:S(2)}, u32[]{:S(2)}) collective-permute-start(bf16[128,2048]{1,0:T(8,128)(2,1)S(1)} %multiply_convert_fusion.1.refs_0_.refs_4_), channel_id=1, source_target_pairs={{2,0},{3,1},{0,2},{1,3},{6,4},{7,5},{4,6},{5,7},{10,8},{11,9},{8,1... | collective-permute-start | bytes 1572872 | tf_op jit(solution)/shard_map/ppermute | solution.py:473
  262.0 36.2 %collective-permute-start.51 = (bf16[128,2048]{1,0:T(8,128)(2,1)S(1)}, bf16[128,2048]{1,0:T(8,128)(2,1)}, u32[]{:S(2)}, u32[]{:S(2)}) collective-permute-start(bf16[128,2048]{1,0:T(8,128)(2,1)S(1)} %multiply_convert_fusion.1.refs_0_.refs_4_), channel_id=1, source_target_pairs={{1,0},{2,1},{3,2},{0,3},{5,4},{6,5},{7,6},{4,7},{9,8},{10,9},{11,1... | collective-permute-start | bytes 1572872 | tf_op jit(solution)/shard_map/ppermute | solution.py:473
  262.1 37.7 %collective-permute-start.18 = (bf16[128,2048]{1,0:T(8,128)(2,1)S(1)}, bf16[128,2048]{1,0:T(8,128)(2,1)S(1)}, u32[]{:S(2)}, u32[]{:S(2)}) collective-permute-start(bf16[128,2048]{1,0:T(8,128)(2,1)S(1)} %multiply_convert_fusion.1.refs_0_.refs_4_), channel_id=1, source_target_pairs={{0,16},{4,12},{8,24},{12,4},{16,0},{20,28},{24,8},{28,20},{1,17},{... | collective-permute-start | bytes 1572872 | tf_op jit(solution)/shard_map/ppermute | solution.py:494
  263.6 36.1 %collective-permute-start.19 = (bf16[128,2048]{1,0:T(8,128)(2,1)S(1)}, bf16[128,2048]{1,0:T(8,128)(2,1)S(1)}, u32[]{:S(2)}, u32[]{:S(2)}) collective-permute-start(bf16[128,2048]{1,0:T(8,128)(2,1)S(1)} %multiply_convert_fusion.1.refs_0_.refs_4_), channel_id=1, source_target_pairs={{0,8},{4,20},{8,0},{12,28},{16,24},{20,4},{24,16},{28,12},{1,9},{5... | collective-permute-start | bytes 1572872 | tf_op jit(solution)/shard_map/ppermute | solution.py:494
  329.2 43.5 %collective-permute-start.52 = (bf16[128,2048]{1,0:T(8,128)(2,1)}, bf16[128,2048]{1,0:T(8,128)(2,1)S(1)}, u32[]{:S(2)}, u32[]{:S(2)}) collective-permute-start(bf16[128,2048]{1,0:T(8,128)(2,1)} %collective-permute-done.51.refs_0_.refs_12_), channel_id=1, source_target_pairs={{0,16},{4,12},{8,24},{12,4},{16,0},{20,28},{24,8},{28,20},{1,17},{... | collective-permute-start | bytes 1572872 | tf_op jit(solution)/shard_map/ppermute | solution.py:494
  330.7 43.0 %collective-permute-start.40 = (bf16[128,2048]{1,0:T(8,128)(2,1)}, bf16[128,2048]{1,0:T(8,128)(2,1)S(1)}, u32[]{:S(2)}, u32[]{:S(2)}) collective-permute-start(bf16[128,2048]{1,0:T(8,128)(2,1)} %collective-permute-done.36.refs_1_.refs_29_), channel_id=1, source_target_pairs={{0,4},{4,0},{8,12},{12,8},{1,5},{5,1},{9,13},{13,9},{2,6},{6,2},{1... | collective-permute-start | bytes 1572872 | tf_op jit(solution)/shard_map/ppermute | solution.py:485
  330.7 43.8 %collective-permute-start.41 = (bf16[128,2048]{1,0:T(8,128)(2,1)}, bf16[128,2048]{1,0:T(8,128)(2,1)S(1)}, u32[]{:S(2)}, u32[]{:S(2)}) collective-permute-start(bf16[128,2048]{1,0:T(8,128)(2,1)} %copy-done.74), channel_id=1, source_target_pairs={{0,4},{4,0},{8,12},{12,8},{1,5},{5,1},{9,13},{13,9},{2,6},{6,2},{1... | collective-permute-start | bytes 1572872 | tf_op jit(solution)/shard_map/ppermute | solution.py:485
  334.1 40.6 %collective-permute-start.74 = (bf16[128,2048]{1,0:T(8,128)(2,1)}, bf16[128,2048]{1,0:T(8,128)(2,1)}, u32[]{:S(2)}, u32[]{:S(2)}) collective-permute-start(bf16[128,2048]{1,0:T(8,128)(2,1)} %copy-done.76), channel_id=1, source_target_pairs={{0,8},{4,20},{8,0},{12,28},{16,24},{20,4},{24,16},{28,12},{1,9},{5... | collective-permute-start | bytes 1572872 | tf_op jit(solution)/shard_map/ppermute | solution.py:494
  336.2 39.3 %collective-permute-start.42 = (bf16[128,2048]{1,0:T(8,128)(2,1)}, bf16[128,2048]{1,0:T(8,128)(2,1)}, u32[]{:S(2)}, u32[]{:S(2)}) collective-permute-start(bf16[128,2048]{1,0:T(8,128)(2,1)} %collective-permute-done.38.refs_3_.refs_31_), channel_id=1, source_target_pairs={{0,4},{4,0},{8,12},{12,8},{1,5},{5,1},{9,13},{13,9},{2,6},{6,2},{1... | collective-permute-start | bytes 1572872 | tf_op jit(solution)/shard_map/ppermute | solution.py:485
  372.8 39.4 %collective-permute-start.53 = (bf16[128,2048]{1,0:T(8,128)(2,1)}, bf16[128,2048]{1,0:T(8,128)(2,1)}, u32[]{:S(2)}, u32[]{:S(2)}) collective-permute-start(bf16[128,2048]{1,0:T(8,128)(2,1)} %collective-permute-done.51.refs_0_.refs_12_), channel_id=1, source_target_pairs={{0,8},{4,20},{8,0},{12,28},{16,24},{20,4},{24,16},{28,12},{1,9},{5... | collective-permute-start | bytes 1572872 | tf_op jit(solution)/shard_map/ppermute | solution.py:494
  373.8 38.9 %collective-permute-start.76 = (bf16[128,2048]{1,0:T(8,128)(2,1)S(1)}, bf16[128,2048]{1,0:T(8,128)(2,1)S(1)}, u32[]{:S(2)}, u32[]{:S(2)}) collective-permute-start(bf16[128,2048]{1,0:T(8,128)(2,1)S(1)} %copy-done.77), channel_id=1, source_target_pairs={{0,4},{4,0},{8,12},{12,8},{1,5},{5,1},{9,13},{13,9},{2,6},{6,2},{1... | collective-permute-start | bytes 1572872 | tf_op jit(solution)/shard_map/ppermute | solution.py:485
  374.6 38.2 %collective-permute-start.77 = (bf16[128,2048]{1,0:T(8,128)(2,1)S(1)}, bf16[128,2048]{1,0:T(8,128)(2,1)S(1)}, u32[]{:S(2)}, u32[]{:S(2)}) collective-permute-start(bf16[128,2048]{1,0:T(8,128)(2,1)S(1)} %copy-done.79), channel_id=1, source_target_pairs={{0,4},{4,0},{8,12},{12,8},{1,5},{5,1},{9,13},{13,9},{2,6},{6,2},{1... | collective-permute-start | bytes 1572872 | tf_op jit(solution)/shard_map/ppermute | solution.py:485
  374.7 38.6 %collective-permute-start.54 = (bf16[128,2048]{1,0:T(8,128)(2,1)S(1)}, bf16[128,2048]{1,0:T(8,128)(2,1)}, u32[]{:S(2)}, u32[]{:S(2)}) collective-permute-start(bf16[128,2048]{1,0:T(8,128)(2,1)S(1)} %collective-permute-done.52.refs_1_.refs_13_), channel_id=1, source_target_pairs={{0,8},{4,20},{8,0},{12,28},{16,24},{20,4},{24,16},{28,12},{1,9},{5... | collective-permute-start | bytes 1572872 | tf_op jit(solution)/shard_map/ppermute | solution.py:494
  375.5 37.9 %collective-permute-start.78 = (bf16[128,2048]{1,0:T(8,128)(2,1)}, bf16[128,2048]{1,0:T(8,128)(2,1)S(1)}, u32[]{:S(2)}, u32[]{:S(2)}) collective-permute-start(bf16[128,2048]{1,0:T(8,128)(2,1)} %collective-permute-done.74.refs_3_.refs_23_), channel_id=1, source_target_pairs={{0,4},{4,0},{8,12},{12,8},{1,5},{5,1},{9,13},{13,9},{2,6},{6,2},{1... | collective-permute-start | bytes 1572872 | tf_op jit(solution)/shard_map/ppermute | solution.py:485
  412.2 38.3 %collective-permute-start.66 = (bf16[128,2176]{1,0:T(8,128)(2,1)S(1)}, bf16[128,2176]{1,0:T(8,128)(2,1)S(1)}, u32[]{:S(2)}, u32[]{:S(2)}) collective-permute-start(bf16[128,2176]{1,0:T(8,128)(2,1)S(1)} %collective-permute-done.62.refs_11_.refs_15_.refs_51_), channel_id=1, source_target_pairs={{0,4},{4,0},{8,12},{12,8},{1,5},{5,1},{9,13},{13,9},{2,6},{6,2},{1... | collective-permute-start | bytes 1671176 | tf_op jit(solution)/shard_map/ppermute | solution.py:485
  412.7 38.3 %collective-permute-start.55 = (bf16[128,2048]{1,0:T(8,128)(2,1)}, bf16[128,2048]{1,0:T(8,128)(2,1)S(1)}, u32[]{:S(2)}, u32[]{:S(2)}) collective-permute-start(bf16[128,2048]{1,0:T(8,128)(2,1)} %collective-permute-done.51.refs_0_.refs_12_), channel_id=1, source_target_pairs={{0,4},{4,0},{8,12},{12,8},{1,5},{5,1},{9,13},{13,9},{2,6},{6,2},{1... | collective-permute-start | bytes 1572872 | tf_op jit(solution)/shard_map/ppermute | solution.py:485
  412.8 38.3 %collective-permute-start.56 = (bf16[128,2048]{1,0:T(8,128)(2,1)S(1)}, bf16[128,2048]{1,0:T(8,128)(2,1)S(1)}, u32[]{:S(2)}, u32[]{:S(2)}) collective-permute-start(bf16[128,2048]{1,0:T(8,128)(2,1)S(1)} %collective-permute-done.52.refs_1_.refs_13_), channel_id=1, source_target_pairs={{0,4},{4,0},{8,12},{12,8},{1,5},{5,1},{9,13},{13,9},{2,6},{6,2},{1... | collective-permute-start | bytes 1572872 | tf_op jit(solution)/shard_map/ppermute | solution.py:485
  413.3 38.3 %collective-permute-start.57 = (bf16[128,2048]{1,0:T(8,128)(2,1)}, bf16[128,2048]{1,0:T(8,128)(2,1)S(1)}, u32[]{:S(2)}, u32[]{:S(2)}) collective-permute-start(bf16[128,2048]{1,0:T(8,128)(2,1)} %collective-permute-done.53.refs_2_.refs_14_), channel_id=1, source_target_pairs={{0,4},{4,0},{8,12},{12,8},{1,5},{5,1},{9,13},{13,9},{2,6},{6,2},{1... | collective-permute-start | bytes 1572872 | tf_op jit(solution)/shard_map/ppermute | solution.py:485
  413.4 38.2 %collective-permute-start.58 = (bf16[128,2048]{1,0:T(8,128)(2,1)}, bf16[128,2048]{1,0:T(8,128)(2,1)}, u32[]{:S(2)}, u32[]{:S(2)}) collective-permute-start(bf16[128,2048]{1,0:T(8,128)(2,1)} %collective-permute-done.54.refs_3_.refs_15_), channel_id=1, source_target_pairs={{0,4},{4,0},{8,12},{12,8},{1,5},{5,1},{9,13},{13,9},{2,6},{6,2},{1... | collective-permute-start | bytes 1572872 | tf_op jit(solution)/shard_map/ppermute | solution.py:485
  450.5 59.0 %collective-permute-start.32 = (bf16[512,2048]{1,0:T(8,128)(2,1)}, bf16[512,2048]{1,0:T(8,128)(2,1)S(1)}, u32[]{:S(2)}, u32[]{:S(2)}) collective-permute-start(bf16[512,2048]{1,0:T(8,128)(2,1)} %get-tuple-element.99), channel_id=1, source_target_pairs={{0,4},{4,0},{8,12},{12,8},{1,5},{5,1},{9,13},{13,9},{2,6},{6,2},{1... | collective-permute-start | bytes 6291464 | tf_op jit(solution)/shard_map/ppermute | solution.py:485
  451.0 60.3 %collective-permute-start.91 = (bf16[512,2048]{1,0:T(8,128)(2,1)}, bf16[512,2048]{1,0:T(8,128)(2,1)}, u32[]{:S(2)}, u32[]{:S(2)}) collective-permute-start(bf16[512,2048]{1,0:T(8,128)(2,1)} %get-tuple-element.106), channel_id=1, source_target_pairs={{0,4},{4,0},{8,12},{12,8},{1,5},{5,1},{9,13},{13,9},{2,6},{6,2},{1... | collective-permute-start | bytes 6291464 | tf_op jit(solution)/shard_map/ppermute | solution.py:485
  451.1 63.0 %collective-permute-start.87 = (bf16[512,2048]{1,0:T(8,128)(2,1)}, bf16[512,2048]{1,0:T(8,128)(2,1)}, u32[]{:S(2)}, u32[]{:S(2)}) collective-permute-start(bf16[512,2048]{1,0:T(8,128)(2,1)} %get-tuple-element.105), channel_id=1, source_target_pairs={{0,4},{4,0},{8,12},{12,8},{1,5},{5,1},{9,13},{13,9},{2,6},{6,2},{1... | collective-permute-start | bytes 6291464 | tf_op jit(solution)/shard_map/ppermute | solution.py:485
  512.9 28.8 %collective-permute-start.92 = (bf16[256,2048]{1,0:T(8,128)(2,1)S(1)}, bf16[256,2048]{1,0:T(8,128)(2,1)S(1)}, u32[]{:S(2)}, u32[]{:S(2)}) collective-permute-start(bf16[256,2048]{1,0:T(8,128)(2,1)S(1)} %add_convert_fusion.4), channel_id=1, source_target_pairs={{0,8},{4,20},{8,0},{12,28},{16,24},{20,4},{24,16},{28,12},{1,9},{5... | collective-permute-start | bytes 3145736 | tf_op jit(solution)/shard_map/ppermute | solution.py:494
  515.9 42.7 %collective-permute-start.88 = (bf16[256,2048]{1,0:T(8,128)(2,1)S(1)}, bf16[256,2048]{1,0:T(8,128)(2,1)S(1)}, u32[]{:S(2)}, u32[]{:S(2)}) collective-permute-start(bf16[256,2048]{1,0:T(8,128)(2,1)S(1)} %add_convert_fusion.5), channel_id=1, source_target_pairs={{0,8},{4,20},{8,0},{12,28},{16,24},{20,4},{24,16},{28,12},{1,9},{5... | collective-permute-start | bytes 3145736 | tf_op jit(solution)/shard_map/ppermute | solution.py:494
  518.5 56.9 %collective-permute-start.68 = (bf16[256,2048]{1,0:T(8,128)(2,1)S(1)}, bf16[256,2048]{1,0:T(8,128)(2,1)S(1)}, u32[]{:S(2)}, u32[]{:S(2)}) collective-permute-start(bf16[256,2048]{1,0:T(8,128)(2,1)S(1)} %add_convert_fusion.6), channel_id=1, source_target_pairs={{0,8},{4,20},{8,0},{12,28},{16,24},{20,4},{24,16},{28,12},{1,9},{5... | collective-permute-start | bytes 3145736 | tf_op jit(solution)/shard_map/ppermute | solution.py:494
  526.0 90.2 %collective-permute-start.34 = (bf16[128,2048]{1,0:T(8,128)(2,1)}, bf16[128,2048]{1,0:T(8,128)(2,1)S(1)}, u32[]{:S(2)}, u32[]{:S(2)}) collective-permute-start(bf16[128,2048]{1,0:T(8,128)(2,1)} %add_convert_fusion.26), channel_id=1, source_target_pairs={{0,16},{4,12},{8,24},{12,4},{16,0},{20,28},{24,8},{28,20},{1,17},{... | collective-permute-start | bytes 1572872 | tf_op jit(solution)/shard_map/ppermute | solution.py:494
  543.0 35.2 %collective-permute-start.93 = (bf16[128,2048]{1,0:T(8,128)(2,1)S(1)}, bf16[128,2048]{1,0:T(8,128)(2,1)S(1)}, u32[]{:S(2)}, u32[]{:S(2)}) collective-permute-start(bf16[128,2048]{1,0:T(8,128)(2,1)S(1)} %add_convert_fusion.21), channel_id=1, source_target_pairs={{0,16},{4,12},{8,24},{12,4},{16,0},{20,28},{24,8},{28,20},{1,17},{... | collective-permute-start | bytes 1572872 | tf_op jit(solution)/shard_map/ppermute | solution.py:494
  559.9 31.4 %collective-permute-start.89 = (bf16[128,2048]{1,0:T(8,128)(2,1)S(1)}, bf16[128,2048]{1,0:T(8,128)(2,1)S(1)}, u32[]{:S(2)}, u32[]{:S(2)}) collective-permute-start(bf16[128,2048]{1,0:T(8,128)(2,1)S(1)} %add_convert_fusion.23), channel_id=1, source_target_pairs={{0,16},{4,12},{8,24},{12,4},{16,0},{20,28},{24,8},{28,20},{1,17},{... | collective-permute-start | bytes 1572872 | tf_op jit(solution)/shard_map/ppermute | solution.py:494
  580.4 35.8 %collective-permute-start.94 = (bf16[128,2048]{1,0:T(8,128)(2,1)}, bf16[128,2048]{1,0:T(8,128)(2,1)}, u32[]{:S(2)}, u32[]{:S(2)}) collective-permute-start(bf16[128,2048]{1,0:T(8,128)(2,1)} %add_convert_fusion.20), channel_id=1, source_target_pairs={{0,3},{1,0},{2,1},{3,2},{4,7},{5,4},{6,5},{7,6},{8,11},{9,8},{10,9... | collective-permute-start | bytes 1572872 | tf_op jit(solution)/shard_map/ppermute | solution.py:477
  593.4 41.6 %collective-permute-start.90 = (bf16[128,2048]{1,0:T(8,128)(2,1)}, bf16[128,2048]{1,0:T(8,128)(2,1)}, u32[]{:S(2)}, u32[]{:S(2)}) collective-permute-start(bf16[128,2048]{1,0:T(8,128)(2,1)} %add_convert_fusion.22), channel_id=1, source_target_pairs={{0,2},{1,3},{2,0},{3,1},{4,6},{5,7},{6,4},{7,5},{8,10},{9,11},{10,... | collective-permute-start | bytes 1572872 | tf_op jit(solution)/shard_map/ppermute | solution.py:477
  595.6 39.4 %collective-permute-start.70 = (bf16[128,2048]{1,0:T(8,128)(2,1)}, bf16[128,2048]{1,0:T(8,128)(2,1)}, u32[]{:S(2)}, u32[]{:S(2)}) collective-permute-start(bf16[128,2048]{1,0:T(8,128)(2,1)} %add_convert_fusion.24), channel_id=1, source_target_pairs={{0,1},{1,2},{2,3},{3,0},{4,5},{5,6},{6,7},{7,4},{8,9},{9,10},{10,1... | collective-permute-start | bytes 1572872 | tf_op jit(solution)/shard_map/ppermute | solution.py:477
  675.9 73.4 %collective-permute-start.106 = (bf16[512,2048]{1,0:T(8,128)(2,1)}, bf16[512,2048]{1,0:T(8,128)(2,1)}, u32[]{:S(2)}, u32[]{:S(2)}) collective-permute-start(bf16[512,2048]{1,0:T(8,128)(2,1)} %get-tuple-element.121), channel_id=1, source_target_pairs={{0,4},{4,0},{8,12},{12,8},{1,5},{5,1},{9,13},{13,9},{2,6},{6,2},{1... | collective-permute-start | bytes 6291464 | tf_op jit(solution)/shard_map/ppermute | solution.py:485
  708.0 52.9 %all-to-all-start.1 = ((bf16[8,264,256]{2,1,0:T(8,128)(2,1)}), bf16[8,264,256]{2,1,0:T(8,128)(2,1)S(1)}, u32[]{:S(2)}, u32[]{:S(2)}) async-start(bf16[8,264,256]{2,1,0:T(8,128)(2,1)} %shard_map.301), calls=%async_computation.1 | async-start | bytes 2162688 | tf_op jit(solution)/shard_map/all_to_all | solution.py:1336
  711.5 40.2 %collective-permute-start.102 = (bf16[512,2048]{1,0:T(8,128)(2,1)}, bf16[512,2048]{1,0:T(8,128)(2,1)}, u32[]{:S(2)}, u32[]{:S(2)}) collective-permute-start(bf16[512,2048]{1,0:T(8,128)(2,1)} %get-tuple-element.117), channel_id=1, source_target_pairs={{0,4},{4,0},{8,12},{12,8},{1,5},{5,1},{9,13},{13,9},{2,6},{6,2},{1... | collective-permute-start | bytes 6291464 | tf_op jit(solution)/shard_map/ppermute | solution.py:485
  713.5 41.1 %collective-permute-start.98 = (bf16[512,2048]{1,0:T(8,128)(2,1)}, bf16[512,2048]{1,0:T(8,128)(2,1)}, u32[]{:S(2)}, u32[]{:S(2)}) collective-permute-start(bf16[512,2048]{1,0:T(8,128)(2,1)} %get-tuple-element.113), channel_id=1, source_target_pairs={{0,4},{4,0},{8,12},{12,8},{1,5},{5,1},{9,13},{13,9},{2,6},{6,2},{1... | collective-permute-start | bytes 6291464 | tf_op jit(solution)/shard_map/ppermute | solution.py:485
  714.8 43.3 %collective-permute-start.95 = (bf16[512,2048]{1,0:T(8,128)(2,1)}, bf16[512,2048]{1,0:T(8,128)(2,1)S(1)}, u32[]{:S(2)}, u32[]{:S(2)}) collective-permute-start(bf16[512,2048]{1,0:T(8,128)(2,1)} %get-tuple-element.109), channel_id=1, source_target_pairs={{0,4},{4,0},{8,12},{12,8},{1,5},{5,1},{9,13},{13,9},{2,6},{6,2},{1... | collective-permute-start | bytes 6291464 | tf_op jit(solution)/shard_map/ppermute | solution.py:485
  733.1 105.3 %collective-permute-start.142 = (bf16[256,512]{1,0:T(8,128)(2,1)}, bf16[256,512]{1,0:T(8,128)(2,1)}, u32[]{:S(2)}, u32[]{:S(2)}) collective-permute-start(bf16[256,512]{1,0:T(8,128)(2,1)} %get-tuple-element.278), channel_id=1, source_target_pairs={{0,2},{1,3},{2,0},{3,1},{4,6},{5,7},{6,4},{7,5},{8,10},{9,11},{10,... | collective-permute-start | bytes 786440 | tf_op jit(solution)/shard_map/ppermute | solution.py:477
  749.3 90.4 %collective-permute-start.140 = (bf16[256,512]{1,0:T(8,128)(2,1)}, bf16[256,512]{1,0:T(8,128)(2,1)}, u32[]{:S(2)}, u32[]{:S(2)}) collective-permute-start(bf16[256,512]{1,0:T(8,128)(2,1)} %get-tuple-element.279), channel_id=1, source_target_pairs={{0,3},{1,0},{2,1},{3,2},{4,7},{5,4},{6,5},{7,6},{8,11},{9,8},{10,9... | collective-permute-start | bytes 786440 | tf_op jit(solution)/shard_map/ppermute | solution.py:477
  769.5 35.9 %collective-permute-start.96 = (bf16[256,2048]{1,0:T(8,128)(2,1)S(1)}, bf16[256,2048]{1,0:T(8,128)(2,1)S(1)}, u32[]{:S(2)}, u32[]{:S(2)}) collective-permute-start(bf16[256,2048]{1,0:T(8,128)(2,1)S(1)} %copy-done.32), channel_id=1, source_target_pairs={{0,8},{4,20},{8,0},{12,28},{16,24},{20,4},{24,16},{28,12},{1,9},{5... | collective-permute-start | bytes 3145736 | tf_op jit(solution)/shard_map/ppermute | solution.py:494
  780.7 37.8 %collective-permute-start.125 = (bf16[320,1024]{1,0:T(8,128)(2,1)}, bf16[320,1024]{1,0:T(8,128)(2,1)}, u32[]{:S(2)}, u32[]{:S(2)}) collective-permute-start(bf16[320,1024]{1,0:T(8,128)(2,1)} %get-tuple-element.142), channel_id=1, source_target_pairs={{0,16},{16,0},{1,17},{17,1},{2,18},{18,2},{3,19},{19,3},{4,20},{20... | collective-permute-start | bytes 1966088 | tf_op jit(solution)/shard_map/ppermute | solution.py:481
  837.3 35.7 %collective-permute-start.120 = (bf16[320,1024]{1,0:T(8,128)(2,1)}, bf16[320,1024]{1,0:T(8,128)(2,1)S(1)}, u32[]{:S(2)}, u32[]{:S(2)}) collective-permute-start(bf16[320,1024]{1,0:T(8,128)(2,1)} %get-tuple-element.133), channel_id=1, source_target_pairs={{0,16},{16,0},{1,17},{17,1},{2,18},{18,2},{3,19},{19,3},{4,20},{20... | collective-permute-start | bytes 1966088 | tf_op jit(solution)/shard_map/ppermute | solution.py:481
  838.5 40.8 %collective-permute-start.108 = (bf16[128,2048]{1,0:T(8,128)(2,1)}, bf16[128,2048]{1,0:T(8,128)(2,1)}, u32[]{:S(2)}, u32[]{:S(2)}) collective-permute-start(bf16[128,2048]{1,0:T(8,128)(2,1)} %add_convert_fusion.14), channel_id=1, source_target_pairs={{0,16},{4,12},{8,24},{12,4},{16,0},{20,28},{24,8},{28,20},{1,17},{... | collective-permute-start | bytes 1572872 | tf_op jit(solution)/shard_map/ppermute | solution.py:494
  877.2 88.4 %collective-permute-start.97 = (bf16[128,2048]{1,0:T(8,128)(2,1)}, bf16[128,2048]{1,0:T(8,128)(2,1)S(1)}, u32[]{:S(2)}, u32[]{:S(2)}) collective-permute-start(bf16[128,2048]{1,0:T(8,128)(2,1)} %add_convert_fusion.19), channel_id=1, source_target_pairs={{0,16},{4,12},{8,24},{12,4},{16,0},{20,28},{24,8},{28,20},{1,17},{... | collective-permute-start | bytes 1572872 | tf_op jit(solution)/shard_map/ppermute | solution.py:494
  878.5 33.5 %collective-permute-start.126 = (bf16[320,1024]{1,0:T(8,128)(2,1)}, bf16[320,1024]{1,0:T(8,128)(2,1)S(1)}, u32[]{:S(2)}, u32[]{:S(2)}) collective-permute-start(bf16[320,1024]{1,0:T(8,128)(2,1)} %add_convert_fusion.8), channel_id=1, source_target_pairs={{0,2},{1,3},{2,0},{3,1},{4,6},{5,7},{6,4},{7,5},{8,10},{9,11},{10,... | collective-permute-start | bytes 1966088 | tf_op jit(solution)/shard_map/ppermute | solution.py:477
  879.3 46.4 %collective-permute-start.124 = (bf16[320,1024]{1,0:T(8,128)(2,1)}, bf16[320,1024]{1,0:T(8,128)(2,1)S(1)}, u32[]{:S(2)}, u32[]{:S(2)}) collective-permute-start(bf16[320,1024]{1,0:T(8,128)(2,1)} %add_convert_fusion.9), channel_id=1, source_target_pairs={{0,3},{1,0},{2,1},{3,2},{4,7},{5,4},{6,5},{7,6},{8,11},{9,8},{10,9... | collective-permute-start | bytes 1966088 | tf_op jit(solution)/shard_map/ppermute | solution.py:477
  884.5 54.1 %collective-permute-start.122 = (bf16[320,1024]{1,0:T(8,128)(2,1)}, bf16[320,1024]{1,0:T(8,128)(2,1)S(1)}, u32[]{:S(2)}, u32[]{:S(2)}) collective-permute-start(bf16[320,1024]{1,0:T(8,128)(2,1)} %add_convert_fusion.10), channel_id=1, source_target_pairs={{0,1},{1,2},{2,3},{3,0},{4,5},{5,6},{6,7},{7,4},{8,9},{9,10},{10,1... | collective-permute-start | bytes 1966088 | tf_op jit(solution)/shard_map/ppermute | solution.py:477
  890.1 70.1 %collective-permute-start.118 = (bf16[128,2048]{1,0:T(8,128)(2,1)S(1)}, bf16[128,2048]{1,0:T(8,128)(2,1)S(1)}, u32[]{:S(2)}, u32[]{:S(2)}) collective-permute-start(bf16[128,2048]{1,0:T(8,128)(2,1)S(1)} %constant_dynamic-update-slice_fusion.1), channel_id=1, source_target_pairs={{0,8},{4,12},{8,0},{12,4},{1,9},{5,13},{9,1},{13,5},{2,10},{6,14},... | collective-permute-start | bytes 1572872 | tf_op jit(solution)/shard_map/ppermute | solution.py:485
  912.0 54.1 %collective-permute-start.109 = (bf16[128,2048]{1,0:T(8,128)(2,1)S(1)}, bf16[128,2048]{1,0:T(8,128)(2,1)S(1)}, u32[]{:S(2)}, u32[]{:S(2)}) collective-permute-start(bf16[128,2048]{1,0:T(8,128)(2,1)S(1)} %add_convert_fusion.13), channel_id=1, source_target_pairs={{0,3},{1,0},{2,1},{3,2},{4,7},{5,4},{6,5},{7,6},{8,11},{9,8},{10,9... | collective-permute-start | bytes 1572872 | tf_op jit(solution)/shard_map/ppermute | solution.py:477
  925.6 57.4 %collective-permute-start.105 = (bf16[128,2048]{1,0:T(8,128)(2,1)S(1)}, bf16[128,2048]{1,0:T(8,128)(2,1)S(1)}, u32[]{:S(2)}, u32[]{:S(2)}) collective-permute-start(bf16[128,2048]{1,0:T(8,128)(2,1)S(1)} %add_convert_fusion.15), channel_id=1, source_target_pairs={{0,2},{1,3},{2,0},{3,1},{4,6},{5,7},{6,4},{7,5},{8,10},{9,11},{10,... | collective-permute-start | bytes 1572872 | tf_op jit(solution)/shard_map/ppermute | solution.py:477
  938.6 44.4 %collective-permute-start.101 = (bf16[128,2048]{1,0:T(8,128)(2,1)S(1)}, bf16[128,2048]{1,0:T(8,128)(2,1)S(1)}, u32[]{:S(2)}, u32[]{:S(2)}) collective-permute-start(bf16[128,2048]{1,0:T(8,128)(2,1)S(1)} %add_convert_fusion.17), channel_id=1, source_target_pairs={{0,1},{1,2},{2,3},{3,0},{4,5},{5,6},{6,7},{7,4},{8,9},{9,10},{10,1... | collective-permute-start | bytes 1572872 | tf_op jit(solution)/shard_map/ppermute | solution.py:477
  965.5 35.3 %collective-permute-start.119 = (bf16[256,2048]{1,0:T(8,128)(2,1)}, bf16[256,2048]{1,0:T(8,128)(2,1)}, u32[]{:S(2)}, u32[]{:S(2)}) collective-permute-start(bf16[256,2048]{1,0:T(8,128)(2,1)} %pad_maximum_fusion.7), channel_id=1, source_target_pairs={{0,4},{4,0},{8,12},{12,8},{1,5},{5,1},{9,13},{13,9},{2,6},{6,2},{1... | collective-permute-start | bytes 3145736 | tf_op jit(solution)/shard_map/ppermute | solution.py:485
  (201 other events, 3490.5 us)
